TPU v7x, 32 devices: a whole 2x2x4 slice. The times are simulated.
32 devices in a mesh: dp: 8 (over y, x, core), fsdp: 4 (over z).
Axes of the slice: x: 2, y: 2, z: 4, core: 2. Of those that a mesh axis runs over, the one named last changes fastest.
Arguments:
- patches: bfloat16 [8192, 1152], P(('dp', 'fsdp')), may hold values from -6 to 6
- conditions: bfloat16 [128, 1152], P(('dp', 'fsdp')), may hold values from -6 to 6
- segment_ids: int32 [8192], P(('dp', 'fsdp')), may hold values from 0 to 3, as said below
- grid_coords: int32 [2, 8192], P(None, ('dp', 'fsdp')), may hold values from 0 to 15, as said below
- mod_weight: bfloat16 [1152, 6912], P('dp', 'fsdp'), may hold values from -0.1875 to 0.1875
- mod_bias: bfloat16 [6912], P('fsdp'), may hold values from -3 to 3
- qkv_weight: bfloat16 [1152, 3456], P('dp', 'fsdp'), may hold values from -0.1875 to 0.1875
- qkv_bias: bfloat16 [3456], P('fsdp'), may hold values from -3 to 3
- qk_gains: bfloat16 [2, 72], P(None, 'fsdp'), may hold values from 0.25 to 1.75
- proj_weight: bfloat16 [1152, 1152], P('dp', 'fsdp'), may hold values from -2 to 2
- proj_bias: bfloat16 [1152], P('fsdp'), may hold values from -3 to 3
- up_weight: bfloat16 [1152, 6144], P('dp', 'fsdp'), may hold values from -0.1875 to 0.1875
- up_bias: bfloat16 [6144], P('fsdp'), may hold values from -3 to 3
- down_weight: bfloat16 [3072, 1152], P('dp', 'fsdp'), may hold values from -0.109375 to 0.109375
- down_bias: bfloat16 [1152], P('fsdp'), may hold values from -3 to 3
- out_cotangent: bfloat16 [8192, 1152], P(('dp', 'fsdp')), may hold values from -6 to 6
Outputs:
- block_out: bfloat16 [8192, 1152], P(('dp', 'fsdp'))
- patch_grad: bfloat16 [8192, 1152], P(('dp', 'fsdp'))
- cond_grad: bfloat16 [128, 1152], P(('dp', 'fsdp'))
- mod_weight_grad: float32 [1152, 6912], P('dp', 'fsdp')
- mod_bias_grad: float32 [6912], P('fsdp')
- qkv_weight_grad: float32 [1152, 3456], P('dp', 'fsdp')
- qkv_bias_grad: float32 [3456], P('fsdp')
- qk_gains_grad: float32 [2, 72], P(None, 'fsdp')
- proj_weight_grad: float32 [1152, 1152], P('dp', 'fsdp')
- proj_bias_grad: float32 [1152], P('fsdp')
- up_weight_grad: float32 [1152, 6144], P('dp', 'fsdp')
- up_bias_grad: float32 [6144], P('fsdp')
- down_weight_grad: float32 [3072, 1152], P('dp', 'fsdp')
- down_bias_grad: float32 [1152], P('fsdp')
Inputs may be any that keep to these rules, and one draw needn't show every extreme that they name: `segment_ids`: the 256 rows r with the same r // 256 hold either one image (all ids 0) or four images of 64 rows in order with ids 0, 1, 2, 3; both kinds occur in every draw. `grid_coords`: row and column of each patch on its image's grid in row-major order: 16 x 16 for an image of 256 rows, 8 on each side for one of 64 rows.
All inputs are finite; a program needn't handle non-finite values.
Results may differ from a plain program's by a relative error of at most 0.017.
Values may be sent and summed in bfloat16 or wider, within the bound.
A program may use at most 256 MiB of HBM per device.

v0:
```python
import jax
import jax.numpy as jnp
from jax import lax
from jax.sharding import PartitionSpec as P

HEADS = 16


epsilon = 1e-06
highest = lax.Precision.HIGHEST


def rms_scale(values):
    return lax.rsqrt(jnp.mean(values * values, axis=-1, keepdims=True) + epsilon)


def norm_backward(grad_normed, normed, factor):
    return factor * (grad_normed - normed * jnp.mean(grad_normed * normed, axis=-1, keepdims=True))


def rotary_tables(coord_rows, quarter):
    frequencies = 10000.0 ** (-jnp.arange(quarter, dtype=jnp.float32) / quarter)
    row_angle = coord_rows[0].astype(jnp.float32)[:, None, None] * frequencies
    col_angle = coord_rows[1].astype(jnp.float32)[:, None, None] * frequencies
    return (jnp.cos(row_angle), jnp.sin(row_angle), jnp.cos(col_angle), jnp.sin(col_angle))


def rotate(values, tables, direction):
    half_size = values.shape[-1] // 2
    quarter = half_size // 2
    pieces_out = []
    for which_half in range(2):
        cosine = tables[2 * which_half]
        sine_tab = direction * tables[2 * which_half + 1]
        start_col = which_half * half_size
        first_part = values[..., start_col : start_col + quarter]
        second = values[..., start_col + quarter : start_col + half_size]
        pieces_out.append(first_part * cosine - second * sine_tab)
        pieces_out.append(second * cosine + first_part * sine_tab)
    return jnp.concatenate(pieces_out, axis=-1)


def masked_scores(query_blk, key_low, seg_blk, segment_ids, score_scale):
    scores = (
        jnp.einsum("qhd,khd->hqk", query_blk, key_low, preferred_element_type=jnp.float32)
        * score_scale
    )
    same_item = seg_blk[:, None] == segment_ids[None, :]
    return jnp.where(same_item[None], scores, -1e30)


def attention_forward(query_low, key_low, value_low, segment_ids, block_rows, score_scale):
    row_count = query_low.shape[0]
    block_count = row_count // block_rows
    query_blocks = query_low.reshape(
        block_count, block_rows, query_low.shape[1], query_low.shape[2]
    )
    seg_blocks = segment_ids.reshape(block_count, block_rows)

    def one_block(inputs):
        query_blk, seg_blk = inputs
        scores = masked_scores(query_blk, key_low, seg_blk, segment_ids, score_scale)
        row_max = jnp.max(scores, axis=-1, keepdims=True)
        exponentials = jnp.exp(scores - row_max)
        denominator = jnp.sum(exponentials, axis=-1, keepdims=True)
        probs_low = (exponentials / denominator).astype(jnp.bfloat16)
        attended = jnp.einsum(
            "hqk,khd->qhd", probs_low, value_low, preferred_element_type=jnp.float32
        )
        return (attended, row_max[..., 0] + jnp.log(denominator[..., 0]))

    attended, log_total = lax.map(one_block, (query_blocks, seg_blocks))
    return (attended.reshape(row_count, -1), log_total)


def attention_backward(
    query_low, key_low, value_low, grad_low, segment_ids, log_total, block_rows, score_scale
):
    row_count = query_low.shape[0]
    block_count = row_count // block_rows
    block_shape = (block_count, block_rows, query_low.shape[1], query_low.shape[2])
    query_blocks = query_low.reshape(block_shape)
    grad_blocks = grad_low.reshape(block_shape)
    seg_blocks = segment_ids.reshape(block_count, block_rows)

    def one_block(totals, inputs):
        grad_keys, grad_values = totals
        query_blk, grad_blk, seg_blk, total_blk = inputs
        scores = masked_scores(query_blk, key_low, seg_blk, segment_ids, score_scale)
        probs = jnp.exp(scores - total_blk[..., None])
        grad_probs = jnp.einsum(
            "qhd,khd->hqk", grad_blk, value_low, preferred_element_type=jnp.float32
        )
        row_dot = jnp.sum(probs * grad_probs, axis=-1, keepdims=True)
        grad_scores = (probs * (grad_probs - row_dot)).astype(jnp.bfloat16)
        grad_query = score_scale * jnp.einsum(
            "hqk,khd->qhd", grad_scores, key_low, preferred_element_type=jnp.float32
        )
        grad_keys = grad_keys + score_scale * jnp.einsum(
            "hqk,qhd->khd", grad_scores, query_blk, preferred_element_type=jnp.float32
        )
        grad_values = grad_values + jnp.einsum(
            "hqk,qhd->khd", probs.astype(jnp.bfloat16), grad_blk, preferred_element_type=jnp.float32
        )
        return ((grad_keys, grad_values), grad_query)

    empty_grad = jnp.zeros(key_low.shape, jnp.float32)
    totals, grad_query = lax.scan(
        one_block, (empty_grad, empty_grad), (query_blocks, grad_blocks, seg_blocks, log_total)
    )
    return (grad_query.reshape(key_low.shape), totals[0], totals[1])


def silu_slope(values):
    sigmoid_gate = jax.nn.sigmoid(values)
    return sigmoid_gate * (1.0 + values * (1.0 - sigmoid_gate))


def outer_grad(left, right):
    return jnp.einsum("rd,rf->df", left, right, preferred_element_type=jnp.float32)


def per_device(
    patches,
    conditions,
    segment_ids,
    grid_coords,
    mod_weight,
    mod_bias,
    qkv_weight,
    qkv_bias,
    qk_gains,
    proj_weight,
    proj_bias,
    up_weight,
    up_bias,
    down_weight,
    down_bias,
    out_cotangent,
):
    fsdp_whole = (
        lax.all_gather(mod_weight, "fsdp", axis=1, tiled=True),
        lax.all_gather(qkv_weight, "fsdp", axis=1, tiled=True),
        lax.all_gather(proj_weight, "fsdp", axis=1, tiled=True),
        lax.all_gather(up_weight, "fsdp", axis=1, tiled=True),
        lax.all_gather(down_weight, "fsdp", axis=1, tiled=True),
        lax.all_gather(mod_bias, "fsdp", axis=0, tiled=True),
        lax.all_gather(qkv_bias, "fsdp", axis=0, tiled=True),
        lax.all_gather(proj_bias, "fsdp", axis=0, tiled=True),
        lax.all_gather(up_bias, "fsdp", axis=0, tiled=True),
        lax.all_gather(down_bias, "fsdp", axis=0, tiled=True),
        lax.all_gather(qk_gains, "fsdp", axis=1, tiled=True),
    )
    gathered = (
        lax.all_gather(fsdp_whole[0], "dp", axis=0, tiled=True),
        lax.all_gather(fsdp_whole[1], "dp", axis=0, tiled=True),
        lax.all_gather(fsdp_whole[2], "dp", axis=0, tiled=True),
        lax.all_gather(fsdp_whole[3], "dp", axis=0, tiled=True),
        lax.all_gather(fsdp_whole[4], "dp", axis=0, tiled=True),
    )
    mod_full, qkv_full, proj_full, up_full, down_full = gathered
    mod_vector = fsdp_whole[5].astype(jnp.float32)
    qkv_vector = fsdp_whole[6].astype(jnp.float32)
    proj_vector = fsdp_whole[7].astype(jnp.float32)
    up_vector = fsdp_whole[8].astype(jnp.float32)
    down_vector = fsdp_whole[9].astype(jnp.float32)
    gains_full = fsdp_whole[10].astype(jnp.float32)
    row_count = patches.shape[0]
    model_width = patches.shape[1]
    head_size = model_width // HEADS
    hidden_units = up_full.shape[1] // 2
    score_scale = head_size ** (-0.5)
    head_shape = (row_count, HEADS, head_size)
    tables = rotary_tables(grid_coords, head_size // 4)
    onehot = (
        segment_ids[:, None] == jnp.arange(conditions.shape[0], dtype=jnp.int32)[None, :]
    ).astype(jnp.float32)
    cond_full = conditions.astype(jnp.float32)
    silu_low = jax.nn.silu(cond_full).astype(jnp.bfloat16)
    modulation = jnp.dot(silu_low, mod_full, preferred_element_type=jnp.float32) + mod_vector
    per_token = jnp.dot(onehot, modulation, precision=highest)
    shift_attn = per_token[:, 0:model_width]
    scale_attn = per_token[:, model_width : 2 * model_width]
    gate_attn = per_token[:, 2 * model_width : 3 * model_width]
    shift_ffn = per_token[:, 3 * model_width : 4 * model_width]
    scale_ffn = per_token[:, 4 * model_width : 5 * model_width]
    gate_ffn = per_token[:, 5 * model_width : 6 * model_width]
    patch_full = patches.astype(jnp.float32)
    scale_one = rms_scale(patch_full)
    normed_one = patch_full * scale_one
    hidden_one = (normed_one * (1.0 + scale_attn) + shift_attn).astype(jnp.bfloat16)
    qkv_rows = jnp.dot(hidden_one, qkv_full, preferred_element_type=jnp.float32) + qkv_vector
    query_raw = qkv_rows[:, 0:model_width].reshape(head_shape)
    key_raw = qkv_rows[:, model_width : 2 * model_width].reshape(head_shape)
    value_low = qkv_rows[:, 2 * model_width :].reshape(head_shape).astype(jnp.bfloat16)
    query_scale = rms_scale(query_raw)
    query_unit = query_raw * query_scale
    key_scale = rms_scale(key_raw)
    key_unit = key_raw * key_scale
    query_low = rotate(query_unit * gains_full[0], tables, 1.0).astype(jnp.bfloat16)
    key_low = rotate(key_unit * gains_full[1], tables, 1.0).astype(jnp.bfloat16)
    attended, log_total = attention_forward(
        query_low, key_low, value_low, segment_ids, row_count, score_scale
    )
    attended_low = attended.astype(jnp.bfloat16)
    branch_attn = jnp.dot(attended_low, proj_full, preferred_element_type=jnp.float32) + proj_vector
    middle = patch_full + gate_attn * branch_attn
    scale_two = rms_scale(middle)
    normed_two = middle * scale_two
    hidden_two = (normed_two * (1.0 + scale_ffn) + shift_ffn).astype(jnp.bfloat16)
    gate_up = jnp.dot(hidden_two, up_full, preferred_element_type=jnp.float32) + up_vector
    gate_part = gate_up[:, :hidden_units]
    up_part = gate_up[:, hidden_units:]
    gated_low = (jax.nn.silu(gate_part) * up_part).astype(jnp.bfloat16)
    branch_ffn = jnp.dot(gated_low, down_full, preferred_element_type=jnp.float32) + down_vector
    block_out = (middle + gate_ffn * branch_ffn).astype(jnp.bfloat16)
    regathered = (
        lax.all_gather(mod_weight, "fsdp", axis=1, tiled=True),
        lax.all_gather(qkv_weight, "fsdp", axis=1, tiled=True),
        lax.all_gather(proj_weight, "fsdp", axis=1, tiled=True),
        lax.all_gather(up_weight, "fsdp", axis=1, tiled=True),
        lax.all_gather(down_weight, "fsdp", axis=1, tiled=True),
        lax.all_gather(qk_gains, "fsdp", axis=1, tiled=True),
    )
    mod_back, qkv_back, proj_back, up_back, down_back = (
        lax.all_gather(regathered[0], "dp", axis=0, tiled=True),
        lax.all_gather(regathered[1], "dp", axis=0, tiled=True),
        lax.all_gather(regathered[2], "dp", axis=0, tiled=True),
        lax.all_gather(regathered[3], "dp", axis=0, tiled=True),
        lax.all_gather(regathered[4], "dp", axis=0, tiled=True),
    )
    gains_back = regathered[5].astype(jnp.float32)
    grad_out = out_cotangent.astype(jnp.float32)
    grad_gate_ffn = grad_out * branch_ffn
    grad_branch_ffn = (grad_out * gate_ffn).astype(jnp.bfloat16)
    down_bias_grad = jnp.sum(grad_branch_ffn.astype(jnp.float32), axis=0)
    grad_gated = jnp.einsum(
        "rd,fd->rf", grad_branch_ffn, down_back, preferred_element_type=jnp.float32
    )
    grad_gate_up = jnp.concatenate(
        [grad_gated * up_part * silu_slope(gate_part), grad_gated * jax.nn.silu(gate_part)], axis=1
    ).astype(jnp.bfloat16)
    up_bias_grad = jnp.sum(grad_gate_up.astype(jnp.float32), axis=0)
    grad_hidden_two = jnp.einsum(
        "rf,df->rd", grad_gate_up, up_back, preferred_element_type=jnp.float32
    )
    grad_middle = grad_out + norm_backward(
        grad_hidden_two * (1.0 + scale_ffn), normed_two, scale_two
    )
    grad_gate_attn = grad_middle * branch_attn
    grad_branch_attn = (grad_middle * gate_attn).astype(jnp.bfloat16)
    proj_bias_grad = jnp.sum(grad_branch_attn.astype(jnp.float32), axis=0)
    grad_attended = jnp.einsum(
        "rd,ed->re", grad_branch_attn, proj_back, preferred_element_type=jnp.float32
    ).astype(jnp.bfloat16)
    grad_query_rot, grad_key_rot, grad_values = attention_backward(
        query_low,
        key_low,
        value_low,
        grad_attended.reshape(head_shape),
        segment_ids,
        log_total,
        row_count,
        score_scale,
    )
    back_query = rotate(grad_query_rot, tables, -1.0)
    back_key = rotate(grad_key_rot, tables, -1.0)
    gains_grad = jnp.stack(
        [jnp.sum(back_query * query_unit, axis=(0, 1)), jnp.sum(back_key * key_unit, axis=(0, 1))]
    )
    grad_query_raw = norm_backward(back_query * gains_back[0], query_unit, query_scale)
    grad_key_raw = norm_backward(back_key * gains_back[1], key_unit, key_scale)
    grad_qkv = jnp.concatenate(
        [
            grad_query_raw.reshape(row_count, model_width),
            grad_key_raw.reshape(row_count, model_width),
            grad_values.reshape(row_count, model_width),
        ],
        axis=1,
    ).astype(jnp.bfloat16)
    qkv_bias_grad = jnp.sum(grad_qkv.astype(jnp.float32), axis=0)
    grad_hidden_one = jnp.einsum(
        "rf,df->rd", grad_qkv, qkv_back, preferred_element_type=jnp.float32
    )
    patch_grad = (
        grad_middle + norm_backward(grad_hidden_one * (1.0 + scale_attn), normed_one, scale_one)
    ).astype(jnp.bfloat16)
    grad_per_token = jnp.concatenate(
        [
            grad_hidden_one,
            grad_hidden_one * normed_one,
            grad_gate_attn,
            grad_hidden_two,
            grad_hidden_two * normed_two,
            grad_gate_ffn,
        ],
        axis=1,
    )
    grad_modulation = jnp.einsum("rs,rm->sm", onehot, grad_per_token, precision=highest).astype(
        jnp.bfloat16
    )
    mod_bias_grad = jnp.sum(grad_modulation.astype(jnp.float32), axis=0)
    cond_grad = (
        jnp.einsum("sm,dm->sd", grad_modulation, mod_back, preferred_element_type=jnp.float32)
        * silu_slope(cond_full)
    ).astype(jnp.bfloat16)
    mod_grad = outer_grad(silu_low, grad_modulation)
    qkv_grad = outer_grad(hidden_one, grad_qkv)
    proj_grad = outer_grad(attended_low, grad_branch_attn)
    up_grad = outer_grad(hidden_two, grad_gate_up)
    down_grad = outer_grad(gated_low, grad_branch_ffn)
    part_grads = (
        lax.psum_scatter(
            mod_grad.astype(jnp.bfloat16), "fsdp", scatter_dimension=1, tiled=True
        ).astype(jnp.float32),
        lax.psum_scatter(
            qkv_grad.astype(jnp.bfloat16), "fsdp", scatter_dimension=1, tiled=True
        ).astype(jnp.float32),
        lax.psum_scatter(
            proj_grad.astype(jnp.bfloat16), "fsdp", scatter_dimension=1, tiled=True
        ).astype(jnp.float32),
        lax.psum_scatter(
            up_grad.astype(jnp.bfloat16), "fsdp", scatter_dimension=1, tiled=True
        ).astype(jnp.float32),
        lax.psum_scatter(
            down_grad.astype(jnp.bfloat16), "fsdp", scatter_dimension=1, tiled=True
        ).astype(jnp.float32),
        lax.psum_scatter(
            mod_bias_grad.astype(jnp.bfloat16), "fsdp", scatter_dimension=0, tiled=True
        ).astype(jnp.float32),
        lax.psum_scatter(
            qkv_bias_grad.astype(jnp.bfloat16), "fsdp", scatter_dimension=0, tiled=True
        ).astype(jnp.float32),
        lax.psum_scatter(
            proj_bias_grad.astype(jnp.bfloat16), "fsdp", scatter_dimension=0, tiled=True
        ).astype(jnp.float32),
        lax.psum_scatter(
            up_bias_grad.astype(jnp.bfloat16), "fsdp", scatter_dimension=0, tiled=True
        ).astype(jnp.float32),
        lax.psum_scatter(
            down_bias_grad.astype(jnp.bfloat16), "fsdp", scatter_dimension=0, tiled=True
        ).astype(jnp.float32),
        lax.psum_scatter(
            gains_grad.astype(jnp.bfloat16), "fsdp", scatter_dimension=1, tiled=True
        ).astype(jnp.float32),
    )
    matrix_grads = (
        lax.psum_scatter(part_grads[0], "dp", scatter_dimension=0, tiled=True),
        lax.psum_scatter(part_grads[1], "dp", scatter_dimension=0, tiled=True),
        lax.psum_scatter(part_grads[2], "dp", scatter_dimension=0, tiled=True),
        lax.psum_scatter(part_grads[3], "dp", scatter_dimension=0, tiled=True),
        lax.psum_scatter(part_grads[4], "dp", scatter_dimension=0, tiled=True),
    )
    vector_grads = lax.psum(
        (part_grads[5], part_grads[6], part_grads[7], part_grads[8], part_grads[9], part_grads[10]),
        "dp",
    )
    return (
        block_out,
        patch_grad,
        cond_grad,
        matrix_grads[0],
        vector_grads[0],
        matrix_grads[1],
        vector_grads[1],
        vector_grads[5],
        matrix_grads[2],
        vector_grads[2],
        matrix_grads[3],
        vector_grads[3],
        matrix_grads[4],
        vector_grads[4],
    )


def solution(mesh):
    return jax.shard_map(
        per_device,
        mesh=mesh,
        in_specs=(
            P(("dp", "fsdp"), None),
            P(("dp", "fsdp"), None),
            P(("dp", "fsdp")),
            P(None, ("dp", "fsdp")),
            P("dp", "fsdp"),
            P("fsdp"),
            P("dp", "fsdp"),
            P("fsdp"),
            P(None, "fsdp"),
            P("dp", "fsdp"),
            P("fsdp"),
            P("dp", "fsdp"),
            P("fsdp"),
            P("dp", "fsdp"),
            P("fsdp"),
            P(("dp", "fsdp"), None),
        ),
        out_specs=(
            P(("dp", "fsdp"), None),
            P(("dp", "fsdp"), None),
            P(("dp", "fsdp"), None),
            P("dp", "fsdp"),
            P("fsdp"),
            P("dp", "fsdp"),
            P("fsdp"),
            P(None, "fsdp"),
            P("dp", "fsdp"),
            P("fsdp"),
            P("dp", "fsdp"),
            P("fsdp"),
            P("dp", "fsdp"),
            P("fsdp"),
        ),
        check_vma=False,
    )
```

profile of v0, /device:TPU:0, one launch (start us, length us, event | category | flops | bytes accessed | tf_op | source)
XLA Modules:
  0.0 1591.7 jit_solution(6411309651146937582)
XLA Ops:
  8.7 48.7 %all-gather.25.cloned.1.call-done = bf16[4,1728,144]{1,2,0:T(8,128)(2,1)} async-done(((bf16[1,1728,144]{1,2,0:T(8,128)(2,1)}), bf16[4,1728,144]{1,2,0:T(8,128)(2,1)}) %all-gather.25.cloned.1.call-update) | async-done | bytes 1990672 | tf_op jit(solution)/shard_map/all_gather | solution.py:142
  57.4 2.6 copy.128
  60.1 2.8 reshape.363
  63.8 36.6 %all-gather.1 = bf16[4,864,144]{1,2,0:T(8,128)(2,1)S(1)} all-gather(bf16[1,864,144]{1,2,0:T(8,128)(2,1)S(1)} %bitcast.121), channel_id=1, replica_groups=mesh['dp'=8,'fsdp'=4] {'fsdp'}, dimensions={0}, use_global_device_ids=true | all-gather | bytes 1244160 | tf_op jit(solution)/shard_map/all_gather | solution.py:143
  100.9 1.7 reshape.365
  102.7 19.7 %all-gather.3 = bf16[4,288,144]{1,2,0:T(8,128)(2,1)S(1)} all-gather(bf16[1,288,144]{1,2,0:T(8,128)(2,1)S(1)} %bitcast.122), channel_id=1, replica_groups=mesh['dp'=8,'fsdp'=4] {'fsdp'}, dimensions={0}, use_global_device_ids=true | all-gather | bytes 414720 | tf_op jit(solution)/shard_map/all_gather | solution.py:144
  124.3 19.9 %all_gather.72 = bf16[384,1152]{0,1:T(8,128)(2,1)} all-gather(bf16[384,288]{0,1:T(8,128)(2,1)S(1)} %copy-done.59), channel_id=1, replica_groups=mesh['dp'=8,'fsdp'=4] {'fsdp'}, dimensions={1}, use_global_device_ids=true | all-gather | bytes 1105920 | tf_op jit(solution)/shard_map/all_gather | solution.py:146
  147.9 17.4 %all-reduce.12 = (bf16[6912]{0:T(1024)(128)(2,1)S(1)}, bf16[3456]{0:T(1024)(128)(2,1)S(1)}, bf16[1152]{0:T(1024)(128)(2,1)S(1)}, bf16[1152]{0:T(1024)(128)(2,1)S(1)}) all-reduce(bf16[6912]{0:T(1024)(128)(2,1)S(1)} %dynamic-update-slice, bf16[3456]{0:T(1024)(128)(2,1)S(1)} %dynamic-update-slice.1, ...), channel_id=1, replica_groups=mesh['dp'=8,'fsdp'=4] {'fsdp'}, use_global_device_ids=true, to_apply=%add | all-reduce | flops 12672 | bytes 50688
  165.3 7.8 all-gather.2
  173.2 13.4 all-gather.4
  189.6 16.8 %all-gather.13.cloned.1.call-done = bf16[1152,6912]{1,0:T(8,128)(2,1)} async-done(((bf16[144,6912]{1,0:T(8,128)(2,1)}), bf16[1152,6912]{1,0:T(8,128)(2,1)}) %all-gather.13.cloned.1.call-update) | async-done | bytes 15925264 | tf_op jit(solution)/shard_map/all_gather | solution.py:155
  206.4 7.7 convolution_add_fusion.1
  214.1 3.0 fusion.34
  217.1 2.8 copy-done.2
  220.2 41.0 %all-gather.15.cloned.1.call-done = bf16[1152,3456]{1,0:T(8,128)(2,1)} async-done(((bf16[144,3456]{1,0:T(8,128)(2,1)}), bf16[1152,3456]{1,0:T(8,128)(2,1)}) %all-gather.15.cloned.1.call-update) | async-done | bytes 7962640 | tf_op jit(solution)/shard_map/all_gather | solution.py:156
  261.3 5.8 convolution_add_fusion.2
  269.8 2.1 copy.130
  277.7 1.7 fusion.14
  279.4 14.3 all-gather.17.cloned.1.call-done
  293.7 4.6 multiply_reduce_fusion.6
  298.3 2.9 fusion.52
  301.2 3.0 fusion.29
  304.2 69.9 %all-gather.21.cloned.1.call-done = bf16[1152,6144]{1,0:T(8,128)(2,1)} async-done(((bf16[144,6144]{1,0:T(8,128)(2,1)}), bf16[1152,6144]{1,0:T(8,128)(2,1)}) %all-gather.21.cloned.1.call-update) | async-done | bytes 14155792 | tf_op jit(solution)/shard_map/all_gather | solution.py:158
  374.1 12.0 convolution_add_fusion
  386.1 40.0 %all-gather.23.cloned.1.call-done = bf16[3072,1152]{0,1:T(8,128)(2,1)} async-done(((bf16[384,1152]{0,1:T(8,128)(2,1)}), bf16[3072,1152]{0,1:T(8,128)(2,1)}) %all-gather.23.cloned.1.call-update) | async-done | bytes 7077904 | tf_op jit(solution)/shard_map/all_gather | solution.py:159
  426.1 9.9 multiply_convert_fusion.2
  436.0 3.3 convolution_add_fusion.4
  439.2 12.7 multiply_reduce_fusion.5
  452.0 4.3 fusion.54
  457.1 2.5 convolution_convert_fusion.5
  459.6 6.5 convolution_convert_fusion.3
  468.2 3.8 convolution_convert_fusion.6
  472.0 2.1 copy.136
  474.9 3.8 multiply_reduce_fusion
  483.5 3.1 multiply_reduce_fusion.3
  489.5 1.4 copy.138
  491.0 1.4 copy.143
  492.5 1.5 copy.141
  494.1 1.4 copy.146
  495.5 3.0 fusion.15
  499.7 4.1 multiply_reduce_fusion.2
  504.9 5.6 convolution_convert_fusion.2
  511.9 11.5 convolution_convert_fusion.1
  524.4 6.6 constant_dynamic-update-slice_fusion.1
  531.1 2.7 fusion.25
  537.9 2.6 fusion.58
  540.5 7.8 convolution_convert_fusion
  548.4 2.6 copy.164
  551.1 86.9 %reduce-scatter.28.cloned.1.call-done = bf16[3072,288]{0,1:T(8,128)(2,1)} async-done(((bf16[3072,1152]{0,1:T(8,128)(2,1)}), bf16[3072,288]{0,1:T(8,128)(2,1)}) %reduce-scatter.28.cloned.1.call-update) | async-done | bytes 1769488 | tf_op jit(solution)/shard_map/reduce_scatter | solution.py:325
  638.0 3.7 convert_element_type.215
  642.1 136.9 %reduce-scatter.20.cloned.1.call-done = bf16[1152,864]{0,1:T(8,128)(2,1)} async-done(((bf16[1152,3456]{0,1:T(8,128)(2,1)}), bf16[1152,864]{0,1:T(8,128)(2,1)}) %reduce-scatter.20.cloned.1.call-update) | async-done | bytes 1990672 | tf_op jit(solution)/shard_map/reduce_scatter | solution.py:316
  779.0 4.3 copy.160
  783.3 235.8 %reduce-scatter.24.cloned.1.call-done = bf16[1152,1536]{1,0:T(8,128)(2,1)} async-done(((bf16[1152,6144]{1,0:T(8,128)(2,1)}), bf16[1152,1536]{1,0:T(8,128)(2,1)}) %reduce-scatter.24.cloned.1.call-update) | async-done | bytes 3538960 | tf_op jit(solution)/shard_map/reduce_scatter | solution.py:322
  1019.1 5.8 convert_element_type.212
  1025.0 264.9 %reduce-scatter.18.cloned.1.call-done = bf16[1152,1728]{0,1:T(8,128)(2,1)} async-done(((bf16[1152,6912]{0,1:T(8,128)(2,1)}), bf16[1152,1728]{0,1:T(8,128)(2,1)}) %reduce-scatter.18.cloned.1.call-update) | async-done | bytes 3981328 | tf_op jit(solution)/shard_map/reduce_scatter | solution.py:313
  1289.9 6.9 copy.158
  1300.9 2.0 fusion.32
  1302.9 18.6 %all-reduce.11 = (bf16[6912]{0:T(1024)(128)(2,1)S(1)}, bf16[3456]{0:T(1024)(128)(2,1)S(1)}, bf16[2,72]{1,0:T(2,128)(2,1)S(1)}, bf16[1152]{0:T(1024)(128)(2,1)S(1...) all-reduce(bf16[6912]{0:T(1024)(128)(2,1)S(1)} %get-tuple-element.2, ...), channel_id=4, replica_groups=mesh['dp'=8,'fsdp'=4] {'fsdp'}, use_global_device_ids=true, to_apply=%region_14.15.clone | all-reduce | flops 18960 | bytes 75840
  1322.0 23.3 %all-reduce.10 = (f32[1728]{0:T(1024)}, f32[864]{0:T(1024)}, f32[2,18]{1,0:T(2,128)}, f32[288]{0:T(512)}, f32[1536]{0:T(1024)}, /*index=5*/f32[288]{0:T(512)}) all-reduce(f32[1728]{0:T(1024)S(1)} %dynamic-slice_convert_fusion.1, f32[864]{0:T(1024)S(1)} %dynamic-slice_convert_fusion.2, ...), channel_id=1, replica_groups=mesh['dp'=8,'fsdp'=4] {'dp'}, use_global_device_ids=true, to_apply=%region_15.16 | all-reduce | flops 4740 | bytes 37920 | tf_op jit(solution)/shard_map/psum | solution.py:354
  1345.4 11.4 fusion.3
  1356.8 28.8 %reduce-scatter.30.cloned.1.call-done = f32[384,288]{0,1:T(8,128)} async-done(((f32[3072,288]{0,1:T(8,128)}), f32[384,288]{0,1:T(8,128)}) %reduce-scatter.30.cloned.1.call-update) | async-done | bytes 442384 | tf_op jit(solution)/shard_map/reduce_scatter | solution.py:352
  1385.6 54.7 %reduce-scatter.34.cloned.1.call-done = f32[144,864]{1,0:T(8,128)} async-done(((f32[1152,864]{1,0:T(8,128)}), f32[144,864]{1,0:T(8,128)}) %reduce-scatter.34.cloned.1.call-update) | async-done | bytes 497680
  1440.4 69.5 %reduce-scatter.26.cloned.1.call-done = f32[144,1536]{1,0:T(8,128)} async-done(((f32[1152,1536]{1,0:T(8,128)}), f32[144,1536]{1,0:T(8,128)}) %reduce-scatter.26.cloned.1.call-update) | async-done | bytes 884752 | tf_op jit(solution)/shard_map/reduce_scatter | solution.py:351
  1509.9 74.9 %reduce-scatter.32.cloned.1.call-done = f32[144,1728]{1,0:T(8,128)} async-done(((f32[1152,1728]{1,0:T(8,128)}), f32[144,1728]{1,0:T(8,128)}) %reduce-scatter.32.cloned.1.call-update) | async-done | bytes 995344
  (296 shorter events, 39.9 us)
Async XLA Ops:
  7.2 50.3 %all-gather.25.cloned.1.call-start = ((), (), s32[]{:S(2)}) async-start(), calls=%async_computation.23 | async-start | bytes 2580480 | tf_op jit(solution)/shard_map/all_gather | solution.py:142
  7.9 115.7 %all-gather.19.cloned.1.call-start = ((), (), s32[]{:S(2)}) async-start(), calls=%async_computation.13 | async-start | bytes 2211840 | tf_op jit(solution)/shard_map/all_gather | solution.py:145
  8.7 197.7 %all-gather.13.cloned.1.call-start = ((), (), s32[]{:S(2)}) async-start(), calls=%async_computation.10 | async-start | bytes 17915904 | tf_op jit(solution)/shard_map/all_gather | solution.py:155
  62.9 198.4 %all-gather.15.cloned.1.call-start = ((), (), s32[]{:S(2)}) async-start(), calls=%async_computation.11 | async-start | bytes 8957952 | tf_op jit(solution)/shard_map/all_gather | solution.py:156
  100.8 1.8 copy-start.60
  102.6 191.1 %all-gather.17.cloned.1.call-start = ((), (), s32[]{:S(2)}) async-start(), calls=%async_computation.12 | async-start | bytes 2985984 | tf_op jit(solution)/shard_map/all_gather | solution.py:157
  122.5 1.7 copy-start.59
  123.6 250.6 %all-gather.21.cloned.1.call-start = ((), (), s32[]{:S(2)}) async-start(), calls=%async_computation.14 | async-start | bytes 15925248 | tf_op jit(solution)/shard_map/all_gather | solution.py:158
  123.7 20.6 %copy-start.83 = (u32[32]{0:T(128)S(1)}, u32[32]{0:T(128)}, u32[]{:S(2)}) copy-start(u32[32]{0:T(128)} %constant.87) | copy-start | bytes 388
  123.7 23.1 %copy-start.86 = (bf16[288]{0:T(512)(128)(2,1)S(1)}, bf16[288]{0:T(512)(128)(2,1)}, u32[]{:S(2)}) copy-start(bf16[288]{0:T(512)(128)(2,1)} %param.26) | copy-start | bytes 1732
  123.7 23.4 %copy-start.87 = (bf16[288]{0:T(512)(128)(2,1)S(1)}, bf16[288]{0:T(512)(128)(2,1)}, u32[]{:S(2)}) copy-start(bf16[288]{0:T(512)(128)(2,1)} %param.30) | copy-start | bytes 1732
  123.7 23.6 %copy-start.81 = (bf16[1728]{0:T(1024)(128)(2,1)S(1)}, bf16[1728]{0:T(1024)(128)(2,1)}, u32[]{:S(2)}) copy-start(bf16[1728]{0:T(1024)(128)(2,1)} %param.21) | copy-start | bytes 10372
  123.7 23.9 %copy-start.84 = (bf16[864]{0:T(1024)(128)(2,1)S(1)}, bf16[864]{0:T(1024)(128)(2,1)}, u32[]{:S(2)}) copy-start(bf16[864]{0:T(1024)(128)(2,1)} %param.23) | copy-start | bytes 5188
  123.7 41.5 %copy-start.88 = (bf16[2,18]{1,0:T(2,128)(2,1)S(1)}, bf16[2,18]{1,0:T(2,128)(2,1)}, u32[]{:S(2)}) copy-start(bf16[2,18]{1,0:T(2,128)(2,1)} %param.24) | copy-start | bytes 220
  123.7 49.4 %copy-start.82 = (bf16[1536]{0:T(1024)(128)(2,1)S(1)}, bf16[1536]{0:T(1024)(128)(2,1)}, u32[]{:S(2)}) copy-start(bf16[1536]{0:T(1024)(128)(2,1)} %param.28) | copy-start | bytes 9220
  124.2 63.0 %copy-start.5 = (bf16[256,1152]{1,0:T(8,128)(2,1)S(1)}, bf16[256,1152]{1,0:T(8,128)(2,1)}, u32[]{:S(2)}) copy-start(bf16[256,1152]{1,0:T(8,128)(2,1)} %param.16) | copy-start | bytes 1769476
  124.2 63.8 %copy-start.85 = (s32[2,256]{1,0:T(2,128)S(1)}, s32[2,256]{1,0:T(2,128)}, u32[]{:S(2)}) copy-start(s32[2,256]{1,0:T(2,128)} %param.19) | copy-start | bytes 6148
  124.2 63.8 %copy-start.67 = (s32[256]{0:T(256)S(1)}, s32[256]{0:T(256)}, u32[]{:S(2)}) copy-start(s32[256]{0:T(256)} %param.18) | copy-start | bytes 3076
  124.2 82.2 %copy-start.61 = (bf16[4,1152]{1,0:T(4,128)(2,1)S(1)}, bf16[4,1152]{1,0:T(4,128)(2,1)}, u32[]{:S(2)}) copy-start(bf16[4,1152]{1,0:T(4,128)(2,1)} %param.17) | copy-start | bytes 27652
  124.2 301.9 %all-gather.23.cloned.1.call-start = ((), (), s32[]{:S(2)}) async-start(), calls=%async_computation.15 | async-start | bytes 7962624 | tf_op jit(solution)/shard_map/all_gather | solution.py:159
  144.2 404.2 %reduce-scatter.22.cloned.1.call-start = ((), (), s32[]{:S(2)}) async-start(), calls=%async_computation.18 | async-start | bytes 3317760 | tf_op jit(solution)/shard_map/reduce_scatter | solution.py:319
  187.4 29.7 %copy-start.73 = (f32[256]{0:T(256)}, f32[256]{0:T(256)S(1)}, u32[]{:S(2)}) copy-start(f32[256]{0:T(256)S(1)} %add_rsqrt_fusion.3) | copy-start | bytes 3076
  217.1 2.8 copy-start.2
  220.2 46.8 %copy-start.24 = (bf16[256,1152]{1,0:T(8,128)(2,1)}, bf16[256,1152]{1,0:T(8,128)(2,1)S(1)}, u32[]{:S(2)}) copy-start(bf16[256,1152]{1,0:T(8,128)(2,1)S(1)} %fusion.19) | copy-start | bytes 1769476
  267.1 2.0 copy-start.7
  274.0 1.7 copy-start.36
  274.0 1.7 copy-start.38
  274.1 1.7 copy-start.40
  274.1 1.7 copy-start.42
  275.8 1.9 copy-start
  275.8 1.9 copy-start.63
  275.8 1.9 copy-start.23
  276.8 2.6 copy-start.64
  293.7 4.6 copy-start.10
  298.3 153.6 %copy-start.71 = (f32[256]{0:T(256)}, f32[256]{0:T(256)S(1)}, u32[]{:S(2)}) copy-start(f32[256]{0:T(256)S(1)} %add_rsqrt_fusion.2) | copy-start | bytes 3076
  426.1 9.9 copy-start.89
  436.0 3.3 copy-start.21
  451.9 5.1 copy-start.26
  459.6 178.4 %reduce-scatter.28.cloned.1.call-start = ((), (), s32[]{:S(2)}) async-start(), calls=%async_computation.21 | async-start | bytes 8847360 | tf_op jit(solution)/shard_map/reduce_scatter | solution.py:325
  466.2 312.8 %reduce-scatter.20.cloned.1.call-start = ((), (), s32[]{:S(2)}) async-start(), calls=%async_computation.17 | async-start | bytes 9953280 | tf_op jit(solution)/shard_map/reduce_scatter | solution.py:316
  474.9 3.8 copy-start.1
  486.6 1.5 copy-start.65
  488.1 1.5 copy-start.19
  489.5 1.5 copy-start.18
  492.4 1.6 copy-start.50
  494.0 1.5 copy-start.12
  499.7 5.2 copy-start.25
  510.5 508.6 %reduce-scatter.24.cloned.1.call-start = ((), (), s32[]{:S(2)}) async-start(), calls=%async_computation.19 | async-start | bytes 17694720 | tf_op jit(solution)/shard_map/reduce_scatter | solution.py:322
  523.4 7.7 copy-start.3
  523.4 766.5 %reduce-scatter.18.cloned.1.call-start = ((), (), s32[]{:S(2)}) async-start(), calls=%async_computation.16 | async-start | bytes 19906560 | tf_op jit(solution)/shard_map/reduce_scatter | solution.py:313
  524.4 6.6 copy-start.74
  531.1 2.7 copy-start.20
  535.7 1.5 copy-start.27
  537.9 2.6 copy-start.62
  548.3 808.5 %reduce-scatter.36.cloned.1.call-start = ((), (), s32[]{:S(2)}) async-start(), calls=%async_computation.26 | async-start | bytes 1990656
  551.0 834.6 %reduce-scatter.30.cloned.1.call-start = ((), (), s32[]{:S(2)}) async-start(), calls=%async_computation.22 | async-start | bytes 3981312 | tf_op jit(solution)/shard_map/reduce_scatter | solution.py:352
  641.8 798.6 %reduce-scatter.34.cloned.1.call-start = ((), (), s32[]{:S(2)}) async-start(), calls=%async_computation.25 | async-start | bytes 4644864
  783.3 726.6 %reduce-scatter.26.cloned.1.call-start = ((), (), s32[]{:S(2)}) async-start(), calls=%async_computation.20 | async-start | bytes 7962624 | tf_op jit(solution)/shard_map/reduce_scatter | solution.py:351
  1024.9 559.8 %reduce-scatter.32.cloned.1.call-start = ((), (), s32[]{:S(2)}) async-start(), calls=%async_computation.24 | async-start | bytes 9289728
  1296.9 3.7 copy-start.14
  1296.9 3.7 copy-start.16
  1296.9 4.0 copy-start.9
  1300.9 2.1 copy-start.69
  1300.9 2.1 copy-start.70
  (43 other events, 39.8 us)
Sparse Core Ops, SparseCore 0:
  9.6 47.8 all-gather.24
  59.0 57.6 all-gather.18
  118.6 87.7 all-gather.12
  208.7 52.5 all-gather.14
  263.6 30.1 all-gather.16
  295.5 78.6 all-gather.20
  376.0 50.0 all-gather.22
  459.7 52.7 reduce-scatter.21
  514.8 123.1 reduce-scatter.27
  640.2 138.7 reduce-scatter.19
  781.3 237.7 reduce-scatter.23
  1021.3 268.5 reduce-scatter.17
  1293.9 39.8 reduce-scatter.35
  1337.7 47.9 reduce-scatter.29
  1389.5 50.8 reduce-scatter.33
  1444.3 65.4 reduce-scatter.25
  1513.9 70.7 reduce-scatter.31
where the time goes:
time: 1600 us; the launch traced here: 1590 us
  waiting for transfers between devices  1190 us (74%)
  blocking collectives  157 us (10%)
  matrix products  128 us (8%)
  local copies, waits for them, and re-layouts  59.5 us (4%)
  other arithmetic  40.3 us (3%)
  between operations  20.8 us (1%)
    reduce_scatter x1, waiting for transfers between devices, per_device(): lax.psum_scatter(mod_grad.astype(jnp.bfloat16), 'fsdp', scatter_dimension...  265 us
    reduce_scatter x1, waiting for transfers between devices, per_device(): lax.psum_scatter(up_grad.astype(jnp.bfloat16), 'fsdp', scatter_dimension=...  236 us
    reduce_scatter x1, waiting for transfers between devices, per_device(): lax.psum_scatter(qkv_grad.astype(jnp.bfloat16), 'fsdp', scatter_dimension...  137 us
    unnamed x20, waiting for transfers between devices  132 us
    reduce_scatter x1, waiting for transfers between devices, per_device(): lax.psum_scatter(down_grad.astype(jnp.bfloat16), 'fsdp', scatter_dimensio...  86.9 us
    all_gather x1, waiting for transfers between devices, per_device(): lax.all_gather(fsdp_whole[3], 'dp', axis=0, tiled=True)  69.9 us
    reduce_scatter x1, waiting for transfers between devices, per_device(): lax.psum_scatter(part_grads[3], 'dp', scatter_dimension=0, tiled=True)  69.5 us
    all_gather x1, waiting for transfers between devices, per_device(): lax.all_gather(mod_weight, 'fsdp', axis=1, tiled=True)  48.7 us
  transfers between devices with their start and end apart: 17, of which 14 were waited for; matrix products, arithmetic and copies ran while one was open for 11% of the time, Pallas kernels for 0%

commit v1 on v0

v1 whole, which is shorter than its diff:
```python
import jax
import jax.numpy as jnp
from jax import lax
from jax.sharding import PartitionSpec as P

HEADS = 16
SPAN = 64

epsilon = 1e-06
low = jnp.bfloat16
full = jnp.float32


def rms_scale(values):
    return lax.rsqrt(jnp.mean(values * values, axis=-1, keepdims=True) + epsilon)


def norm_backward(grad_normed, normed, factor):
    return factor * (grad_normed - normed * jnp.mean(grad_normed * normed, axis=-1, keepdims=True))


def rotary_tables(coord_rows, quarter):
    frequencies = 10000.0 ** (-jnp.arange(quarter, dtype=full) / quarter)
    row_angle = coord_rows[0].astype(full)[:, None, None] * frequencies
    col_angle = coord_rows[1].astype(full)[:, None, None] * frequencies
    return (jnp.cos(row_angle), jnp.sin(row_angle), jnp.cos(col_angle), jnp.sin(col_angle))


def rotate(values, tables, direction):
    half_size = values.shape[-1] // 2
    quarter = half_size // 2
    pieces_out = []
    for which_half in range(2):
        cosine = tables[2 * which_half]
        sine_tab = direction * tables[2 * which_half + 1]
        start_col = which_half * half_size
        first_part = values[..., start_col : start_col + quarter]
        second = values[..., start_col + quarter : start_col + half_size]
        pieces_out.append(first_part * cosine - second * sine_tab)
        pieces_out.append(second * cosine + first_part * sine_tab)
    return jnp.concatenate(pieces_out, axis=-1)


def dot(left, right):
    return jnp.dot(left, right, preferred_element_type=full)


def dot_t(left, right):
    return lax.dot_general(left, right, (((1,), (1,)), ((), ())), preferred_element_type=full)


def outer_grad(left, right):
    return lax.dot_general(left, right, (((0,), (0,)), ((), ())), preferred_element_type=full)


def silu_slope(values):
    sigmoid_gate = jax.nn.sigmoid(values)
    return sigmoid_gate * (1.0 + values * (1.0 - sigmoid_gate))


def swap(values, axis, size, bit):
    return lax.ppermute(values, axis, [(k, k ^ bit) for k in range(size)])


def bits_of(size):
    return [1 << b for b in range(size.bit_length() - 1)]


def gather_small(values, axis, size):
    index = lax.axis_index(axis)
    for bit in bits_of(size):
        other = swap(values, axis, size, bit)
        upper = (index & bit) != 0
        values = jnp.concatenate(
            [jnp.where(upper, other, values), jnp.where(upper, values, other)], axis=0
        )
    return values


def scatter_sum_small(values, axis, size):
    index = lax.axis_index(axis)
    for bit in reversed(bits_of(size)):
        half = values.shape[0] // 2
        upper = (index & bit) != 0
        first, second = values[:half], values[half:]
        values = jnp.where(upper, second, first) + swap(
            jnp.where(upper, first, second), axis, size, bit
        )
    return values


def sum_small(values, axis, size):
    for bit in bits_of(size):
        values = values + swap(values, axis, size, bit)
    return values


def xor_order(values, index, size):
    tail = values.shape[1:]
    for bit in bits_of(size):
        paired = values.reshape((size // (2 * bit), 2, bit) + tail)
        values = jnp.where((index & bit) != 0, jnp.flip(paired, axis=1), paired)
        values = values.reshape((size,) + tail)
    return values


def exchange_small(values, axis, size):
    index = lax.axis_index(axis)
    tail = values.shape[1:]
    values = xor_order(values, index, size)
    for bit in bits_of(size):
        paired = values.reshape((size // (2 * bit), 2, bit) + tail)
        moved = swap(paired[:, 1], axis, size, bit)
        values = jnp.stack([paired[:, 0], moved], axis=1).reshape((size,) + tail)
    return xor_order(values, index, size)


def gather_weight(weight, dp_size, fsdp_size):
    rows, cols = weight.shape
    whole = lax.all_gather(weight, ("dp", "fsdp"), axis=0, tiled=False)
    whole = whole.reshape(dp_size, fsdp_size, rows, cols).transpose(1, 0, 2, 3)
    return whole.reshape(fsdp_size, dp_size * rows, cols)


def scatter_grad(blocks, dp_size):
    rows, cols = blocks[0].shape
    parts = jnp.stack([b.reshape(dp_size, rows // dp_size, cols) for b in blocks], axis=1)
    parts = lax.psum_scatter(parts, "dp", scatter_dimension=0, tiled=False)
    return lax.psum_scatter(parts, "fsdp", scatter_dimension=0, tiled=False).astype(full)


def masked_scores(query_low, key_low, same_item, score_scale):
    scores = jnp.einsum("qhd,khd->hqk", query_low, key_low, preferred_element_type=full)
    return jnp.where(same_item, scores * score_scale, -1e30)


def make_per_device(dp_size, fsdp_size):
    def per_device(
        patches,
        conditions,
        segment_ids,
        grid_coords,
        mod_weight,
        mod_bias,
        qkv_weight,
        qkv_bias,
        qk_gains,
        proj_weight,
        proj_bias,
        up_weight,
        up_bias,
        down_weight,
        down_bias,
        out_cotangent,
    ):
        row_count, model_width = patches.shape
        slots = conditions.shape[0]
        spans = row_count // SPAN
        head_size = model_width // HEADS
        score_scale = head_size ** (-0.5)
        head_shape = (row_count, HEADS, head_size)
        dp_index = lax.axis_index("dp")
        mod_rows, mod_cols = mod_weight.shape

        qkv_full = gather_weight(qkv_weight, dp_size, fsdp_size)
        proj_full = gather_weight(proj_weight, dp_size, fsdp_size)
        up_full = gather_weight(up_weight, dp_size, fsdp_size)
        down_full = gather_weight(down_weight, dp_size, fsdp_size)

        gain_cols = qk_gains.shape[1]
        sizes = [qkv_bias.shape[0], proj_bias.shape[0], up_bias.shape[0], down_bias.shape[0]]
        vector = jnp.concatenate(
            [qkv_bias, proj_bias, up_bias, down_bias, qk_gains[0], qk_gains[1]]
        )
        vectors = gather_small(vector[None], "fsdp", fsdp_size).astype(full)
        bounds = [0]
        for size in sizes + [gain_cols, gain_cols]:
            bounds.append(bounds[-1] + size)
        pieces = [vectors[:, bounds[k] : bounds[k + 1]] for k in range(6)]
        qkv_vector, proj_vector, up_vector, down_vector, gain_q, gain_k = [
            p.reshape(-1) for p in pieces
        ]

        cond_full = conditions.astype(full)
        silu_low = jax.nn.silu(cond_full).astype(low)
        silu_all = gather_small(
            gather_small(silu_low[None], "fsdp", fsdp_size)[None], "dp", dp_size
        ).reshape(dp_size * fsdp_size * slots, model_width)
        silu_cols = lax.dynamic_slice_in_dim(silu_all, dp_index * mod_rows, mod_rows, axis=1)
        mod_part = dot(silu_cols, mod_weight).reshape(dp_size, fsdp_size, slots, mod_cols)
        mod_sum = scatter_sum_small(mod_part, "dp", dp_size)[0] + mod_bias.astype(full)
        modulation = exchange_small(mod_sum, "fsdp", fsdp_size)
        modulation = modulation.transpose(1, 0, 2).reshape(slots, fsdp_size * mod_cols)
        span_ids = segment_ids.reshape(spans, SPAN)[:, 0]
        span_hot = (span_ids[:, None] == jnp.arange(slots, dtype=jnp.int32)[None, :]).astype(full)
        span_mod = jnp.sum(span_hot[:, :, None] * modulation[None], axis=1)

        def per_row(k):
            part = span_mod[:, k * model_width : (k + 1) * model_width]
            return jnp.broadcast_to(part[:, None, :], (spans, SPAN, model_width)).reshape(
                row_count, model_width
            )

        shift_attn, scale_attn, gate_attn, shift_ffn, scale_ffn, gate_ffn = map(per_row, range(6))

        def cols_of(blocks):
            return jnp.concatenate(blocks, axis=1)

        def forward_dot(rows_low, weight_full):
            return cols_of([dot(rows_low, weight_full[j]) for j in range(fsdp_size)])

        def split(values):
            width = values.shape[1] // fsdp_size
            return [values[:, j * width : (j + 1) * width] for j in range(fsdp_size)]

        def backward_dot(grad_low, weight_full):
            parts = split(grad_low)
            total = dot_t(parts[0], weight_full[0])
            for j in range(1, fsdp_size):
                total = total + dot_t(parts[j], weight_full[j])
            return total

        def weight_grad(rows_low, grad_low):
            return scatter_grad(
                [outer_grad(rows_low, part).astype(low) for part in split(grad_low)], dp_size
            )

        tables = rotary_tables(grid_coords, head_size // 4)
        patch_full = patches.astype(full)
        scale_one = rms_scale(patch_full)
        normed_one = patch_full * scale_one
        hidden_one = (normed_one * (1.0 + scale_attn) + shift_attn).astype(low)
        qkv_rows = forward_dot(hidden_one, qkv_full) + qkv_vector
        query_raw = qkv_rows[:, 0:model_width].reshape(head_shape)
        key_raw = qkv_rows[:, model_width : 2 * model_width].reshape(head_shape)
        value_low = qkv_rows[:, 2 * model_width :].reshape(head_shape).astype(low)
        query_scale = rms_scale(query_raw)
        query_unit = query_raw * query_scale
        key_scale = rms_scale(key_raw)
        key_unit = key_raw * key_scale
        query_low = rotate(query_unit * gain_q, tables, 1.0).astype(low)
        key_low = rotate(key_unit * gain_k, tables, 1.0).astype(low)
        same_item = (segment_ids[:, None] == segment_ids[None, :])[None]
        scores = masked_scores(query_low, key_low, same_item, score_scale)
        exponentials = jnp.exp(scores - jnp.max(scores, axis=-1, keepdims=True))
        probs = exponentials / jnp.sum(exponentials, axis=-1, keepdims=True)
        probs_low = probs.astype(low)
        attended_low = (
            jnp.einsum("hqk,khd->qhd", probs_low, value_low, preferred_element_type=full)
            .reshape(row_count, model_width)
            .astype(low)
        )
        branch_attn = forward_dot(attended_low, proj_full) + proj_vector
        middle = patch_full + gate_attn * branch_attn
        scale_two = rms_scale(middle)
        normed_two = middle * scale_two
        hidden_two = (normed_two * (1.0 + scale_ffn) + shift_ffn).astype(low)
        gate_up = forward_dot(hidden_two, up_full) + up_vector
        hidden_units = gate_up.shape[1] // 2
        gate_part = gate_up[:, :hidden_units]
        up_part = gate_up[:, hidden_units:]
        gated_low = (jax.nn.silu(gate_part) * up_part).astype(low)
        branch_ffn = forward_dot(gated_low, down_full) + down_vector
        block_out = (middle + gate_ffn * branch_ffn).astype(low)

        grad_out = out_cotangent.astype(full)
        grad_gate_ffn = grad_out * branch_ffn
        grad_branch_ffn = (grad_out * gate_ffn).astype(low)
        down_bias_grad = jnp.sum(grad_branch_ffn.astype(full), axis=0)
        grad_gated = backward_dot(grad_branch_ffn, down_full)
        down_grad = weight_grad(gated_low, grad_branch_ffn)
        grad_gate_up = jnp.concatenate(
            [grad_gated * up_part * silu_slope(gate_part), grad_gated * jax.nn.silu(gate_part)],
            axis=1,
        ).astype(low)
        up_bias_grad = jnp.sum(grad_gate_up.astype(full), axis=0)
        grad_hidden_two = backward_dot(grad_gate_up, up_full)
        up_grad = weight_grad(hidden_two, grad_gate_up)
        grad_middle = grad_out + norm_backward(
            grad_hidden_two * (1.0 + scale_ffn), normed_two, scale_two
        )
        grad_gate_attn = grad_middle * branch_attn
        grad_branch_attn = (grad_middle * gate_attn).astype(low)
        proj_bias_grad = jnp.sum(grad_branch_attn.astype(full), axis=0)
        grad_attended = backward_dot(grad_branch_attn, proj_full).astype(low).reshape(head_shape)
        proj_grad = weight_grad(attended_low, grad_branch_attn)
        grad_probs = jnp.einsum(
            "qhd,khd->hqk", grad_attended, value_low, preferred_element_type=full
        )
        row_dot = jnp.sum(probs * grad_probs, axis=-1, keepdims=True)
        grad_scores = (probs * (grad_probs - row_dot)).astype(low)
        grad_values = jnp.einsum(
            "hqk,qhd->khd", probs_low, grad_attended, preferred_element_type=full
        )
        grad_query_rot = score_scale * jnp.einsum(
            "hqk,khd->qhd", grad_scores, key_low, preferred_element_type=full
        )
        grad_key_rot = score_scale * jnp.einsum(
            "hqk,qhd->khd", grad_scores, query_low, preferred_element_type=full
        )
        back_query = rotate(grad_query_rot, tables, -1.0)
        back_key = rotate(grad_key_rot, tables, -1.0)
        gain_q_grad = jnp.sum(back_query * query_unit, axis=(0, 1))
        gain_k_grad = jnp.sum(back_key * key_unit, axis=(0, 1))
        grad_query_raw = norm_backward(back_query * gain_q, query_unit, query_scale)
        grad_key_raw = norm_backward(back_key * gain_k, key_unit, key_scale)
        grad_qkv = jnp.concatenate(
            [
                grad_query_raw.reshape(row_count, model_width),
                grad_key_raw.reshape(row_count, model_width),
                grad_values.reshape(row_count, model_width),
            ],
            axis=1,
        ).astype(low)
        qkv_grad = weight_grad(hidden_one, grad_qkv)
        qkv_bias_grad = jnp.sum(grad_qkv.astype(full), axis=0)
        grad_hidden_one = backward_dot(grad_qkv, qkv_full)
        patch_grad = (
            grad_middle + norm_backward(grad_hidden_one * (1.0 + scale_attn), normed_one, scale_one)
        ).astype(low)

        def span_sum(values):
            return jnp.sum(values.reshape(spans, SPAN, model_width), axis=1)

        grad_spans = jnp.concatenate(
            [
                span_sum(grad_hidden_one),
                span_sum(grad_hidden_one * normed_one),
                span_sum(grad_gate_attn),
                span_sum(grad_hidden_two),
                span_sum(grad_hidden_two * normed_two),
                span_sum(grad_gate_ffn),
            ],
            axis=1,
        )
        grad_modulation = jnp.sum(span_hot[:, :, None] * grad_spans[:, None, :], axis=0).astype(low)
        grad_mod = grad_modulation.reshape(slots, fsdp_size, mod_cols).transpose(1, 0, 2)
        grad_mod = exchange_small(grad_mod, "fsdp", fsdp_size)
        grad_mod = gather_small(grad_mod[None], "dp", dp_size).reshape(-1, mod_cols)
        mod_bias_grad = jnp.sum(grad_mod.astype(full), axis=0)
        mod_grad = outer_grad(silu_cols, grad_mod)
        cond_part = dot_t(grad_mod, mod_weight).reshape(dp_size, fsdp_size, slots, mod_rows)
        cond_part = scatter_sum_small(cond_part.transpose(1, 0, 2, 3), "fsdp", fsdp_size)[0]
        cond_part = exchange_small(cond_part, "dp", dp_size)
        cond_grad = (
            cond_part.transpose(1, 0, 2).reshape(slots, model_width) * silu_slope(cond_full)
        ).astype(low)

        rows = [qkv_bias_grad, proj_bias_grad, up_bias_grad, down_bias_grad, gain_q_grad, gain_k_grad]
        vector_grad = jnp.concatenate([r.reshape(fsdp_size, -1) for r in rows], axis=1)
        vector_grad = scatter_sum_small(vector_grad, "fsdp", fsdp_size)
        vector_grad = sum_small(vector_grad, "dp", dp_size)[0]
        out = [vector_grad[bounds[k] : bounds[k + 1]] for k in range(6)]
        return (
            block_out,
            patch_grad,
            cond_grad,
            mod_grad,
            mod_bias_grad,
            qkv_grad,
            out[0],
            jnp.stack([out[4], out[5]]),
            proj_grad,
            out[1],
            up_grad,
            out[2],
            down_grad,
            out[3],
        )

    return per_device


def solution(mesh):
    rows = P(("dp", "fsdp"), None)
    matrix = P("dp", "fsdp")
    vector = P("fsdp")
    gains = P(None, "fsdp")
    return jax.shard_map(
        make_per_device(mesh.shape["dp"], mesh.shape["fsdp"]),
        mesh=mesh,
        in_specs=(
            rows,
            rows,
            P(("dp", "fsdp")),
            P(None, ("dp", "fsdp")),
            matrix,
            vector,
            matrix,
            vector,
            gains,
            matrix,
            vector,
            matrix,
            vector,
            matrix,
            vector,
            rows,
        ),
        out_specs=(
            rows,
            rows,
            rows,
            matrix,
            vector,
            matrix,
            vector,
            gains,
            matrix,
            vector,
            matrix,
            vector,
            matrix,
            vector,
        ),
        check_vma=False,
    )
```

time: 1600 us -> 908 us (0.57)
  waiting for transfers between devices: 1190 us -> 555 us
  blocking collectives: 157 us -> 0 us
  local copies, waits for them, and re-layouts: 59.5 us -> 148 us
  matrix products: 128 us -> 74.2 us
  starting transfers between devices: 1.16 us -> 37.4 us
  other arithmetic: 40.3 us -> 66.5 us
    reduce_scatter x7 -> x6, waiting for transfers between devices: 823 us -> 249 us  [the longest x2 147 us: scatter_grad(): parts = lax.psum_scatter(parts, 'dp', scatter_dimension=0, tiled=False)]
    all_gather x5 -> x0, blocking collectives: 97.3 us -> none  [the longest x1 36.6 us: per_device(): lax.all_gather(qkv_weight, 'fsdp', axis=1, tiled=True)]
    all_gather x7 -> x4, waiting for transfers between devices: 231 us -> 170 us  [gather_weight(): whole = lax.all_gather(weight, ('dp', 'fsdp'), axis=0, tiled=False)]
    dot_general x23 -> x56, matrix products: 128 us -> 68.6 us  [the longest x17 22.7 us: dot_t(): lax.dot_general(left, right, (((1,), (1,)), ((), ())), preferred_element_...]
    ppermute x0 -> x27, waiting for transfers between devices: none -> 43.7 us  [swap(): return lax.ppermute(values, axis, [(k, k ^ bit) for k in range(size)])]
    unnamed x20 -> x12, waiting for transfers between devices: 132 us -> 92.7 us
    ppermute x0 -> x27, starting transfers between devices: none -> 36.2 us  [swap(): return lax.ppermute(values, axis, [(k, k ^ bit) for k in range(size)])]
    unnamed x2 -> x0, blocking collectives: 36 us -> none
  transfers between devices with their start and end apart: 17 -> 38, of which waited for: 14 -> 28; matrix products, arithmetic and copies ran while one was open for 11% -> 19% of each run, Pallas kernels for 0% -> 0%
where the time goes in v1:
time: 908 us; the launch traced here: 898 us
  waiting for transfers between devices  555 us (61%)
  local copies, waits for them, and re-layouts  148 us (16%)
  matrix products  74.2 us (8%)
  other arithmetic  66.5 us (7%)
  starting transfers between devices  37.4 us (4%)
  between operations  16.2 us (2%)
    all_gather x4, waiting for transfers between devices, gather_weight(): whole = lax.all_gather(weight, ('dp', 'fsdp'), axis=0, tiled=False)  170 us
    reduce_scatter x2, waiting for transfers between devices, scatter_grad(): parts = lax.psum_scatter(parts, 'dp', scatter_dimension=0, tiled=False)  147 us
    reduce_scatter x4, waiting for transfers between devices, scatter_grad(): lax.psum_scatter(parts, 'fsdp', scatter_dimension=0, tiled=False)  102 us
    unnamed x12, waiting for transfers between devices  92.7 us
    ppermute x27, waiting for transfers between devices, swap(): return lax.ppermute(values, axis, [(k, k ^ bit) for k in range(size)])  43.7 us
    ppermute x27, starting transfers between devices, swap(): return lax.ppermute(values, axis, [(k, k ^ bit) for k in range(size)])  36.2 us
    unnamed x273, local copies, waits for them, and re-layouts  32.9 us
    convert_element_type x8, local copies, waits for them, and re-layouts, weight_grad(): outer_grad(rows_low, part).astype(low)  25.6 us
  transfers between devices with their start and end apart: 38, of which 28 were waited for; matrix products, arithmetic and copies ran while one was open for 19% of the time, Pallas kernels for 0%

profile of v1, /device:TPU:0, one launch (start us, length us, event | category | flops | bytes accessed | tf_op | source)
XLA Modules:
  0.0 897.5 jit_solution(16913700931957712099)
XLA Ops:
  10.8 3.1 collective-permute-start
  14.6 2.8 concatenate.90
  22.2 3.1 collective-permute-start.1
  35.2 3.4 collective-permute-done.4
  46.4 2.7 collective-permute-start.11
  49.5 5.7 collective-permute-done.5
  58.6 9.7 %collective-permute-done.6 = f32[2,4,4,1728]{3,0,2,1:T(2,128)S(1)} collective-permute-done((f32[2,4,4,1728]{3,0,2,1:T(2,128)S(1)}, f32[2,4,4,1728]{3,0,2,1:T(2,128)S(1)}, u32[]{:S(2)}, u32[]{:S(2)}) %collective-permute-start.6) | collective-permute-done | bytes 221216 | tf_op jit(solution)/shard_map/ppermute | solution.py:62
  72.1 3.6 collective-permute-done.8
  87.5 2.7 copy.316
  91.2 2.7 copy.314
  95.0 2.7 copy.313
  98.8 2.7 copy.320
  101.4 2.3 convert_reduce_fusion.2
  104.0 4.0 fusion.97
  108.0 43.9 %all-gather.15.cloned.1.call-done = bf16[12288,288]{0,1:T(8,128)(2,1)} async-done(((bf16[384,288]{0,1:T(8,128)(2,1)}), bf16[12288,288]{0,1:T(8,128)(2,1)}) %all-gather.15.cloned.1.call-update) | async-done | bytes 7077904 | tf_op jit(solution)/shard_map/all_gather | solution.py:120
  151.9 11.9 %reshape.545 = bf16[8,4,384,288]{2,1,0,3:T(4,128)(2,1)} reshape(bf16[12288,288]{0,1:T(8,128)(2,1)} %all-gather.15.cloned.1.call-done) | data formatting | bytes 14155776 | tf_op jit(solution)/shard_map/reshape | solution.py:121
  163.9 3.9 copy.416
  173.7 2.8 convolution_add_fusion.1
  176.4 53.1 %all-gather.9.cloned.1.call-done = bf16[4608,864]{1,0:T(8,128)(2,1)} async-done(((bf16[144,864]{1,0:T(8,128)(2,1)}), bf16[4608,864]{1,0:T(8,128)(2,1)}) %all-gather.9.cloned.1.call-update) | async-done | bytes 7962640 | tf_op jit(solution)/shard_map/all_gather | solution.py:120
  229.5 3.7 fusion.95
  237.6 3.7 maximum_add_fusion.1
  246.7 5.6 fusion.102
  252.3 2.9 convolution_convert_fusion.17
  260.6 72.7 %all-gather.13.cloned.1.call-done = bf16[4608,1536]{1,0:T(8,128)(2,1)} async-done(((bf16[144,1536]{1,0:T(8,128)(2,1)}), bf16[4608,1536]{1,0:T(8,128)(2,1)}) %all-gather.13.cloned.1.call-update) | async-done | bytes 14155792 | tf_op jit(solution)/shard_map/all_gather | solution.py:120
  333.3 5.8 fusion.94
  342.7 2.4 fusion.111
  348.0 3.6 multiply_convert_fusion.1
  361.8 2.6 multiply_reduce_fusion.3
  364.4 2.9 convert_multiply_fusion
  374.5 3.5 multiply_reduce_fusion
  399.5 4.1 copy.364
  403.6 4.1 copy.363
  407.6 4.1 copy.362
  411.7 4.1 copy.361
  415.8 2.3 copy.368
  418.1 2.3 copy.367
  420.4 2.3 copy.366
  422.8 2.4 copy.365
  425.1 7.6 pad_maximum_fusion.1
  440.9 3.5 pad_maximum_fusion.2
  450.6 5.3 pad_maximum_fusion
  457.7 2.3 fusion.23
  466.3 2.6 fusion.15
  468.9 2.7 copy.338
  471.6 2.8 copy.339
  474.4 3.4 fusion.37
  477.8 2.7 copy.340
  480.5 2.7 copy.341
  484.7 2.8 copy.343
  492.1 2.5 convert_reduce_fusion
  507.3 90.0 %all-reduce.5.cloned.1.call-done = (bf16[8,4,144,864]{3,2,0,1:T(8,128)(2,1)}, bf16[8,4,144,288]{3,2,0,1:T(8,128)(2,1)}) async-done(((bf16[8,4,144,864]{3,2,0,1:T(8,128)(2,1)}, bf16[8,4,144,288]{3,2,0,1:T(8,128)(2,1)}), (bf16[8,4,144,864]{3,2,0,1:T(8,128)(2,1)}, bf16[8,4,144,288]{3,2,0,1:T(8,128)(2,1)})) %all-reduce.5.cloned.1.call-update) | async-done | bytes 10616848
  597.2 2.5 dynamic-slice_bitcast_fusion.1
  601.3 2.9 dynamic-slice_bitcast_fusion
  607.8 3.8 collective-permute-done.15
  613.1 53.1 %reduce-scatter.17.cloned.1.call-done = bf16[1,4,384,288]{2,3,1,0:T(8,128)(2,1)} async-done(((bf16[8,4,384,288]{2,3,1,0:T(8,128)(2,1)}), bf16[1,4,384,288]{2,3,1,0:T(8,128)(2,1)}) %reduce-scatter.17.cloned.1.call-update) | async-done | bytes 884752 | tf_op jit(solution)/shard_map/reduce_scatter | solution.py:128
  667.3 2.5 collective-permute-start.17
  670.4 3.1 collective-permute-done.17
  674.7 2.8 collective-permute-done.18
  677.8 93.8 %reduce-scatter.13.cloned.1.call-done = bf16[1,4,144,1536]{3,2,1,0:T(8,128)(2,1)} async-done(((bf16[8,4,144,1536]{3,2,1,0:T(8,128)(2,1)}), bf16[1,4,144,1536]{3,2,1,0:T(8,128)(2,1)}) %reduce-scatter.13.cloned.1.call-update) | async-done | bytes 1769488 | tf_op jit(solution)/shard_map/reduce_scatter | solution.py:128
  774.5 2.3 fusion.68
  781.6 14.1 %reduce-scatter.11.cloned.1.call-done = bf16[1,144,288]{2,1,0:T(8,128)(2,1)} async-done(((bf16[4,144,288]{2,1,0:T(8,128)(2,1)}), bf16[1,144,288]{2,1,0:T(8,128)(2,1)}) %reduce-scatter.11.cloned.1.call-update) | async-done | bytes 82960 | tf_op jit(solution)/shard_map/reduce_scatter | solution.py:129
  797.3 26.2 %reduce-scatter.9.cloned.1.call-done = bf16[1,144,864]{2,1,0:T(8,128)(2,1)} async-done(((bf16[4,144,864]{2,1,0:T(8,128)(2,1)}), bf16[1,144,864]{2,1,0:T(8,128)(2,1)}) %reduce-scatter.9.cloned.1.call-update) | async-done | bytes 248848 | tf_op jit(solution)/shard_map/reduce_scatter | solution.py:129
  825.3 23.6 %reduce-scatter.19.cloned.1.call-done = bf16[1,384,288]{1,2,0:T(8,128)(2,1)} async-done(((bf16[4,384,288]{1,2,0:T(8,128)(2,1)}), bf16[1,384,288]{1,2,0:T(8,128)(2,1)}) %reduce-scatter.19.cloned.1.call-update) | async-done | bytes 221200 | tf_op jit(solution)/shard_map/reduce_scatter | solution.py:129
  850.6 38.2 %reduce-scatter.15.cloned.1.call-done = bf16[1,144,1536]{2,1,0:T(8,128)(2,1)} async-done(((bf16[4,144,1536]{2,1,0:T(8,128)(2,1)}), bf16[1,144,1536]{2,1,0:T(8,128)(2,1)}) %reduce-scatter.15.cloned.1.call-update) | async-done | bytes 442384 | tf_op jit(solution)/shard_map/reduce_scatter | solution.py:129
  (570 shorter events, 179.8 us)
Async XLA Ops:
  7.2 32.6 %copy-start = (bf16[144,1728]{1,0:T(8,128)(2,1)S(1)}, bf16[144,1728]{1,0:T(8,128)(2,1)}, u32[]{:S(2)}) copy-start(bf16[144,1728]{1,0:T(8,128)(2,1)} %param.20) | copy-start | bytes 1492996
  7.2 20.2 %copy-start.96 = (bf16[256,1152]{1,0:T(8,128)(2,1)S(1)}, bf16[256,1152]{1,0:T(8,128)(2,1)}, u32[]{:S(2)}) copy-start(bf16[256,1152]{1,0:T(8,128)(2,1)} %param.16) | copy-start | bytes 1769476
  7.2 96.8 %all-gather.11.cloned.1.call-start = ((), (), s32[]{:S(2)}) async-start(), calls=%async_computation.13 | async-start | bytes 3649536 | tf_op jit(solution)/shard_map/all_gather | solution.py:120
  7.9 144.0 %all-gather.15.cloned.1.call-start = ((), (), s32[]{:S(2)}) async-start(), calls=%async_computation.15 | async-start | bytes 7299072 | tf_op jit(solution)/shard_map/all_gather | solution.py:120
  8.7 220.8 %all-gather.9.cloned.1.call-start = ((), (), s32[]{:S(2)}) async-start(), calls=%async_computation.12 | async-start | bytes 8515584 | tf_op jit(solution)/shard_map/all_gather | solution.py:120
  9.4 21.3 %copy-start.97 = (bf16[256,1152]{1,0:T(8,128)(2,1)S(1)}, bf16[256,1152]{1,0:T(8,128)(2,1)}, u32[]{:S(2)}) copy-start(bf16[256,1152]{1,0:T(8,128)(2,1)} %param.31) | copy-start | bytes 1769476
  9.4 323.9 %all-gather.13.cloned.1.call-start = ((), (), s32[]{:S(2)}) async-start(), calls=%async_computation.14 | async-start | bytes 14598144 | tf_op jit(solution)/shard_map/all_gather | solution.py:120
  10.0 587.2 %all-reduce.5.cloned.1.call-start = ((), (), s32[]{:S(2)}) async-start(), calls=%async_computation.16 | async-start | bytes 23592960
  10.8 10.7 %collective-permute-start = (bf16[1,4,1152]{2,1,0:T(4,128)(2,1)S(1)}, bf16[1,4,1152]{2,1,0:T(4,128)(2,1)S(1)}, u32[]{:S(2)}, u32[]{:S(2)}) collective-permute-start(bf16[1,4,1152]{2,1,0:T(4,128)(2,1)S(1)} %fusion.87), channel_id=1, source_target_pairs={{0,1},{1,0},{2,3},{3,2},{4,5},{5,4},{6,7},{7,6},{8,9},{9,8},{10,11... | collective-permute-start | bytes 27656 | tf_op jit(solution)/shard_map/ppermute | solution.py:62
  17.5 28.2 %collective-permute-start.10 = (bf16[1,3012]{1,0:T(2,128)(2,1)S(1)}, bf16[1,3012]{1,0:T(2,128)(2,1)}, u32[]{:S(2)}, u32[]{:S(2)}) collective-permute-start(bf16[1,3012]{1,0:T(2,128)(2,1)S(1)} %broadcast_in_dim.31), channel_id=1, source_target_pairs={{0,1},{1,0},{2,3},{3,2},{4,5},{5,4},{6,7},{7,6},{8,9},{9,8},{10,11... | collective-permute-start | bytes 18080 | tf_op jit(solution)/shard_map/ppermute | solution.py:62
  22.2 5.0 collective-permute-start.1
  27.2 1.3 collective-permute-start.2
  27.4 54.3 %copy-start.111 = (f32[4,4]{1,0:T(4,128)}, f32[4,4]{1,0:T(4,128)S(1)}, u32[]{:S(2)}) copy-start(f32[4,4]{1,0:T(4,128)S(1)} %fusion.88) | copy-start | bytes 196
  27.4 3.6 copy-start.124
  27.7 230.7 %copy-start.13 = (bf16[256,1152]{0,1:T(8,128)(2,1)}, bf16[256,1152]{0,1:T(8,128)(2,1)S(1)}, u32[]{:S(2)}) copy-start(bf16[256,1152]{0,1:T(8,128)(2,1)S(1)} %copy.303) | copy-start | bytes 1769476
  28.6 4.5 collective-permute-start.3
  31.0 70.4 %copy-start.61 = (bf16[256,1152]{0,1:T(8,128)(2,1)}, bf16[256,1152]{0,1:T(8,128)(2,1)S(1)}, u32[]{:S(2)}) copy-start(bf16[256,1152]{0,1:T(8,128)(2,1)S(1)} %copy.321) | copy-start | bytes 1769476
  33.4 5.3 collective-permute-start.4
  35.2 68.5 %copy-start.116 = (f32[256]{0:T(256)}, f32[256]{0:T(256)S(1)}, u32[]{:S(2)}) copy-start(f32[256]{0:T(256)S(1)} %add_rsqrt_fusion.3) | copy-start | bytes 3076
  43.9 11.3 %collective-permute-start.5 = (f32[4,4,4,1728]{3,0,2,1:T(4,128)}, f32[4,4,4,1728]{3,0,2,1:T(4,128)}, u32[]{:S(2)}, u32[]{:S(2)}) collective-permute-start(f32[4,4,4,1728]{3,0,2,1:T(4,128)} %copy.306), channel_id=1, source_target_pairs={{0,16},{4,20},{8,24},{12,28},{16,0},{20,4},{24,8},{28,12},{1,17},{... | collective-permute-start | bytes 1327112 | tf_op jit(solution)/shard_map/ppermute | solution.py:62
  46.4 12.1 %collective-permute-start.11 = (bf16[2,3012]{1,0:T(2,128)(2,1)S(1)}, bf16[2,3012]{1,0:T(2,128)(2,1)S(1)}, u32[]{:S(2)}, u32[]{:S(2)}) collective-permute-start(bf16[2,3012]{1,0:T(2,128)(2,1)S(1)} %pad_maximum_fusion.20), channel_id=1, source_target_pairs={{0,2},{1,3},{2,0},{3,1},{4,6},{5,7},{6,4},{7,5},{8,10},{9,11},{10,... | collective-permute-start | bytes 36152 | tf_op jit(solution)/shard_map/ppermute | solution.py:62
  56.8 11.5 %collective-permute-start.6 = (f32[2,4,4,1728]{3,0,2,1:T(2,128)S(1)}, f32[2,4,4,1728]{3,0,2,1:T(2,128)S(1)}, u32[]{:S(2)}, u32[]{:S(2)}) collective-permute-start(f32[2,4,4,1728]{3,0,2,1:T(2,128)S(1)} %broadcast_select_fusion.4), channel_id=1, source_target_pairs={{0,8},{4,12},{8,0},{12,4},{16,24},{20,28},{24,16},{28,20},{1,9},{5... | collective-permute-start | bytes 663560 | tf_op jit(solution)/shard_map/ppermute | solution.py:62
  68.6 1.4 collective-permute-start.7
  70.3 5.4 collective-permute-start.8
  75.8 5.7 collective-permute-start.9
  86.3 173.0 %copy-start.33 = (f32[256,1152]{0,1:T(8,128)}, f32[256,1152]{0,1:T(8,128)S(1)}, u32[]{:S(2)}) copy-start(f32[256,1152]{0,1:T(8,128)S(1)} %copy.317) | copy-start | bytes 3538948
  103.7 69.9 %copy-start.54 = (bf16[256,1152]{0,1:T(8,128)(2,1)}, bf16[256,1152]{0,1:T(8,128)(2,1)S(1)}, u32[]{:S(2)}) copy-start(bf16[256,1152]{0,1:T(8,128)(2,1)S(1)} %get-tuple-element.91) | copy-start | bytes 1769476
  169.2 3.4 copy-start.27
  169.6 4.1 copy-start.29
  233.3 3.3 copy-start.21
  351.6 7.4 copy-start.57
  351.6 9.7 %copy-start.44 = (bf16[256,3072]{1,0:T(8,128)(2,1)}, bf16[256,3072]{1,0:T(8,128)(2,1)S(1)}, u32[]{:S(2)}) copy-start(bf16[256,3072]{1,0:T(8,128)(2,1)S(1)} %get-tuple-element.109) | copy-start | bytes 4718596
  374.5 3.8 copy-start.72
  374.5 3.8 copy-start.113
  382.5 5.7 copy-start.31
  388.2 4.2 copy-start.23
  425.1 7.6 copy-start.73
  425.1 7.6 copy-start.74
  425.1 7.6 copy-start.75
  425.1 7.6 copy-start.76
  435.0 231.2 %reduce-scatter.17.cloned.1.call-start = ((), (), s32[]{:S(2)}) async-start(), calls=%async_computation.10 | async-start | bytes 7962624 | tf_op jit(solution)/shard_map/reduce_scatter | solution.py:128
  444.5 327.1 %reduce-scatter.13.cloned.1.call-start = ((), (), s32[]{:S(2)}) async-start(), calls=%async_computation.8 | async-start | bytes 15925248 | tf_op jit(solution)/shard_map/reduce_scatter | solution.py:128
  456.0 339.7 %reduce-scatter.11.cloned.1.call-start = ((), (), s32[]{:S(2)}) async-start(), calls=%async_computation.7 | async-start | bytes 552960 | tf_op jit(solution)/shard_map/reduce_scatter | solution.py:129
  492.1 5.1 copy-start.84
  494.6 3.7 copy-start.85
  495.1 4.8 collective-permute-start.22
  499.4 3.9 collective-permute-start.12
  500.0 3.8 collective-permute-start.23
  503.8 2.1 collective-permute-start.24
  503.9 95.9 %collective-permute-start.13 = (bf16[1,2,4,1728]{3,2,1,0:T(4,128)(2,1)S(1)}, bf16[1,2,4,1728]{3,2,1,0:T(4,128)(2,1)S(1)}, u32[]{:S(2)}, u32[]{:S(2)}) collective-permute-start(bf16[1,2,4,1728]{3,2,1,0:T(4,128)(2,1)S(1)} %get-tuple-element.186), channel_id=1, source_target_pairs={{0,2},{1,3},{2,0},{3,1},{4,6},{5,7},{6,4},{7,5},{8,10},{9,11},{10,... | collective-permute-start | bytes 82952 | tf_op jit(solution)/shard_map/ppermute | solution.py:62
  505.9 94.0 %collective-permute-start.25 = (f32[1,3012]{1,0:T(1,128)S(1)}, f32[1,3012]{1,0:T(1,128)S(1)}, u32[]{:S(2)}, u32[]{:S(2)}) collective-permute-start(f32[1,3012]{1,0:T(1,128)S(1)} %add.307), channel_id=1, source_target_pairs={{0,8},{4,12},{8,0},{12,4},{16,24},{20,28},{24,16},{28,20},{1,9},{5... | collective-permute-start | bytes 36152 | tf_op jit(solution)/shard_map/ppermute | solution.py:62
  599.7 223.8 %reduce-scatter.9.cloned.1.call-start = ((), (), s32[]{:S(2)}) async-start(), calls=%async_computation.6 | async-start | bytes 1290240 | tf_op jit(solution)/shard_map/reduce_scatter | solution.py:129
  599.9 4.6 collective-permute-start.26
  604.2 244.7 %reduce-scatter.19.cloned.1.call-start = ((), (), s32[]{:S(2)}) async-start(), calls=%async_computation.11 | async-start | bytes 1105920 | tf_op jit(solution)/shard_map/reduce_scatter | solution.py:129
  604.4 1.4 collective-permute-start.14
  606.3 5.3 collective-permute-start.15
  612.2 54.3 %collective-permute-start.16 = (bf16[4,4,4,1728]{3,0,2,1:T(4,128)(2,1)S(1)}, bf16[4,4,4,1728]{3,0,2,1:T(4,128)(2,1)S(1)}, u32[]{:S(2)}, u32[]{:S(2)}) collective-permute-start(bf16[4,4,4,1728]{3,0,2,1:T(4,128)(2,1)S(1)} %pad_maximum_fusion.12), channel_id=1, source_target_pairs={{0,16},{4,20},{8,24},{12,28},{16,0},{20,4},{24,8},{28,12},{1,17},{... | collective-permute-start | bytes 663560 | tf_op jit(solution)/shard_map/ppermute | solution.py:62
  666.2 222.6 %reduce-scatter.15.cloned.1.call-start = ((), (), s32[]{:S(2)}) async-start(), calls=%async_computation.9 | async-start | bytes 2211840 | tf_op jit(solution)/shard_map/reduce_scatter | solution.py:129
  667.3 6.3 collective-permute-start.17
  673.6 4.0 collective-permute-start.18
  771.7 1.2 collective-permute-start.19
  772.4 8.6 copy-start.104
  772.9 3.8 collective-permute-start.20
  776.8 3.8 collective-permute-start.21
  (100 other events, 178.0 us)
Sparse Core Ops, SparseCore 0:
  10.8 66.3 all-gather.10
  80.1 71.7 all-gather.14
  154.7 74.7 all-gather.8
  232.2 101.1 all-gather.12
  435.1 162.0 all-reduce.4
  600.6 65.5 reduce-scatter.16
  669.8 101.7 reduce-scatter.12
  774.5 21.1 reduce-scatter.10
  798.0 25.4 reduce-scatter.8
  825.6 23.2 reduce-scatter.18
  851.2 37.5 reduce-scatter.14

commit v2 on v1

--- a/solution.py
+++ b/solution.py
@@ -1,6 +1,8 @@
 import jax
 import jax.numpy as jnp
 from jax import lax
+from jax.experimental import pallas as pl
+from jax.experimental.pallas import tpu as pltpu
 from jax.sharding import PartitionSpec as P
 
 HEADS = 16
@@ -134,7 +136,7 @@
     return jnp.where(same_item, scores * score_scale, -1e30)
 
 
-def make_per_device(dp_size, fsdp_size):
+def make_plain(dp_size, fsdp_size):
     def per_device(
         patches,
         conditions,
@@ -371,13 +373,748 @@
     return per_device
 
 
+PLANE = 4
+
+
+def cross(values, hop):
+    return lax.ppermute(values, "dp", [(k, k ^ (2 * hop)) for k in range(2 * PLANE)])
+
+
+def partner(values):
+    return lax.ppermute(values, "dp", [(k, k ^ 1) for k in range(2 * PLANE)])
+
+
+def along(values, hop, size):
+    return lax.ppermute(values, "fsdp", [(k, k ^ hop) for k in range(size)])
+
+
+def plane_blocks(values):
+    return [values] + [cross(values, hop) for hop in range(1, PLANE)]
+
+
+def plane_sum(blocks):
+    total = blocks[0]
+    for hop in range(1, PLANE):
+        total = total + cross(blocks[hop].astype(low), hop).astype(full)
+    return total
+
+
+def z_blocks(values, index, size):
+    blocks = jnp.stack([values] + [along(values, hop, size) for hop in range(1, size)])
+    return xor_order(blocks, index, size)
+
+
+def z_exchange(values, index, size):
+    values = xor_order(values, index, size)
+    moved = jnp.stack([values[0]] + [along(values[hop], hop, size) for hop in range(1, size)])
+    return xor_order(moved, index, size)
+
+
+def z_sum_own(values, index, size):
+    values = xor_order(values, index, size)
+    total = values[0].astype(full)
+    for hop in range(1, size):
+        total = total + along(values[hop], hop, size).astype(full)
+    return total
+
+
+class Place:
+    def __init__(self, y, x, core, z):
+        self.y, self.x, self.core, self.z = y, x, core, z
+        self.chip = 2 * y + x
+        self.dp = 2 * self.chip + core
+
+    def hop(self, dy, dx, dc, dz):
+        low_z, high_z = self.z % 2, self.z // 2
+        low_z = 1 - low_z if dz & 1 else low_z
+        high_z = 1 - high_z if dz & 2 else high_z
+        return Place(
+            1 - self.y if dy else self.y,
+            1 - self.x if dx else self.x,
+            1 - self.core if dc else self.core,
+            2 * high_z + low_z,
+        )
+
+
+SELF = (0, 0, 0, 0)
+PLANE_HOPS = [(0, 1, 0, 0), (1, 0, 0, 0), (1, 1, 0, 0)]
+Z_HOPS = [(0, 0, 0, 1), (0, 0, 0, 2), (0, 0, 0, 3)]
+CORE_HOP = (0, 0, 1, 0)
+DP_HOPS = [(dy, dx, dc, 0) for dy in (0, 1) for dx in (0, 1) for dc in (0, 1)]
+ALL_HOPS = [(dy, dx, dc, dz) for dz in range(4) for dy, dx, dc, _ in DP_HOPS]
+GROUP_HOPS = [(dy, dx, 0, dz) for dz in range(4) for dy in (0, 1) for dx in (0, 1)]
+
+
+def exchange(identity, inputs, out_shapes, plan):
+    hops = []
+    for move in plan:
+        if move[0] != SELF and move[0] not in hops:
+            hops.append(move[0])
+
+    def kernel(*refs):
+        ins, outs = refs[: len(inputs)], refs[len(inputs) : len(inputs) + len(out_shapes)]
+        send, recv = refs[-2:]
+        dp_index = lax.axis_index("dp")
+        me = Place(dp_index // 4, (dp_index // 2) % 2, dp_index % 2, lax.axis_index("fsdp"))
+
+        def target(hop):
+            peer = me.hop(*hop)
+            return peer, {"dp": peer.dp, "fsdp": peer.z}
+
+        barrier = pltpu.get_barrier_semaphore()
+        for hop in hops:
+            pl.semaphore_signal(
+                barrier, 1, device_id=target(hop)[1], device_id_type=pl.DeviceIdType.MESH
+            )
+        pl.semaphore_wait(barrier, len(hops))
+        copies = []
+        forwarded = set()
+        for number, (hop, source, source_at, out, out_at, after) in enumerate(plan):
+            peer, device = target(hop)
+            src = (ins if after is None else outs)[source]
+            src = src if source_at is None else src.at[source_at(me, peer)]
+            dst = outs[out]
+            dst = dst if out_at is None else dst.at[out_at(me, peer)]
+            for earlier in after or ():
+                if earlier not in forwarded:
+                    if plan[earlier][0] == SELF:
+                        copies[earlier].wait()
+                    else:
+                        copies[earlier].wait_recv()
+                    forwarded.add(earlier)
+            if hop == SELF:
+                copy = pltpu.make_async_copy(src, dst, send.at[number])
+            else:
+                copy = pltpu.make_async_remote_copy(
+                    src_ref=src,
+                    dst_ref=dst,
+                    send_sem=send.at[number],
+                    recv_sem=recv.at[number],
+                    device_id=device,
+                    device_id_type=pl.DeviceIdType.MESH,
+                )
+            copy.start()
+            copies.append(copy)
+        for number, copy in enumerate(copies):
+            if plan[number][0] == SELF:
+                if number not in forwarded:
+                    copy.wait()
+                continue
+            copy.wait_send()
+            if number not in forwarded:
+                copy.wait_recv()
+
+    anywhere = pl.BlockSpec(memory_space=pl.ANY)
+    return pl.pallas_call(
+        kernel,
+        out_shape=[jax.ShapeDtypeStruct(shape, dtype) for shape, dtype in out_shapes],
+        in_specs=[anywhere] * len(inputs),
+        out_specs=[anywhere] * len(out_shapes),
+        scratch_shapes=[
+            pltpu.SemaphoreType.DMA((len(plan),)),
+            pltpu.SemaphoreType.DMA((len(plan),)),
+        ],
+        compiler_params=pltpu.CompilerParams(collective_id=identity, has_side_effects=True),
+    )(*inputs)
+
+
+def gather_moves(hops, source, out, out_at):
+    return [(hop, source, None, out, out_at, None) for hop in hops]
+
+
+def by_chip(me, peer):
+    return (me.chip,)
+
+
+def by_dp(me, peer):
+    return (me.dp,)
+
+
+def by_z(me, peer):
+    return (me.z,)
+
+
+def by_core(me, peer):
+    return (me.core,)
+
+
+def tie(first, second):
+    return lax.optimization_barrier((first, second))
+
+
+def put(values, own, *at):
+    start = tuple(at) + (0,) * (values.ndim - len(at))
+    return lax.dynamic_update_slice(values, own.reshape((1,) * len(at) + own.shape), start)
+
+
+def slotted(hops, source, source_at, out):
+    return [
+        (hop, source, source_at, out, lambda me, peer, n=n: (n,), None)
+        for n, hop in enumerate(hops)
+    ]
+
+
+def to_chip(me, peer):
+    return (peer.chip,)
+
+
+def to_z(me, peer):
+    return (peer.z,)
+
+
+def make_plane(z_size):
+    def per_device(
+        patches,
+        conditions,
+        segment_ids,
+        grid_coords,
+        mod_weight,
+        mod_bias,
+        qkv_weight,
+        qkv_bias,
+        qk_gains,
+        proj_weight,
+        proj_bias,
+        up_weight,
+        up_bias,
+        down_weight,
+        down_bias,
+        out_cotangent,
+    ):
+        row_count, width = patches.shape
+        slots = conditions.shape[0]
+        spans = row_count // SPAN
+        head_size = width // HEADS
+        heads = HEADS // PLANE
+        part_cols = width // PLANE
+        score_scale = head_size ** (-0.5)
+        dp_index = lax.axis_index("dp")
+        z_index = lax.axis_index("fsdp")
+        chip = dp_index >> 1
+        core = dp_index & 1
+        upper = core == 1
+        mod_rows, mod_cols = mod_weight.shape
+        rows_all = PLANE * row_count
+        shard = qkv_weight.shape[0]
+
+        def core_order(mine, other):
+            return jnp.where(upper, other, mine), jnp.where(upper, mine, other)
+
+        def both_cores(first, second):
+            return jnp.concatenate(
+                [jnp.concatenate([first[j], second[j]], axis=0) for j in range(z_size)], axis=1
+            )
+
+        def scatter_columns(pieces):
+            ordered = xor_order(jnp.stack(pieces), chip, PLANE)
+            mine = jnp.stack(
+                [ordered[0]] + [cross(ordered[hop], hop) for hop in range(1, PLANE)]
+            )
+            first, second = core_order(mine, partner(mine))
+            both = xor_order(jnp.stack([first, second], axis=1), chip, PLANE)
+            return both.reshape(2 * PLANE * both.shape[2], both.shape[3])
+
+        cond_full = conditions.astype(full)
+        silu_low = jax.nn.silu(cond_full).astype(low)
+        vector = jnp.concatenate(
+            [qkv_bias, proj_bias, up_bias, down_bias, qk_gains[0], qk_gains[1]]
+        )[None]
+        meta = jnp.concatenate([segment_ids[None], grid_coords], axis=0)
+        cols_qkv = qkv_weight.shape[1]
+        cols_proj = proj_weight.shape[1]
+        plan = gather_moves(Z_HOPS + [SELF], 0, 0, lambda me, peer: (me.dp, me.z))
+        plan += gather_moves(Z_HOPS, 1, 1, by_z)
+        plan += gather_moves(Z_HOPS, 3, 3, by_z)
+        plan += gather_moves(Z_HOPS + [SELF], 4, 4, by_z)
+        plan += gather_moves(PLANE_HOPS + [SELF], 5, 5, by_chip)
+        plan += [(hop, 0, by_dp, 0, by_dp, (0, 1, 2, 3)) for hop in DP_HOPS if hop != SELF]
+        plan += gather_moves(PLANE_HOPS, 2, 2, by_chip)
+        silu_all, qkv_z, patch_all, proj_z, vectors, meta_all = exchange(
+            1,
+            [silu_low, qkv_weight, patches, proj_weight, vector, meta],
+            [
+                ((2 * PLANE, z_size, slots, width), low),
+                ((z_size, shard, cols_qkv), low),
+                ((PLANE, row_count, width), low),
+                ((z_size, shard, cols_proj), low),
+                ((z_size,) + vector.shape, low),
+                ((PLANE,) + meta.shape, jnp.int32),
+            ],
+            plan,
+        )
+
+        qkv_z, up_later = tie(qkv_z, up_weight)
+        up_z = lax.all_gather(up_later, "fsdp", axis=0, tiled=False)
+        qkv_z = put(qkv_z, qkv_weight, z_index)
+        proj_z = put(proj_z, proj_weight, z_index)
+        patch_all = put(patch_all, patches, chip)
+
+        silu_all = silu_all.reshape(-1, width)
+        silu_cols = lax.dynamic_slice_in_dim(silu_all, dp_index * mod_rows, mod_rows, axis=1)
+        mod_part = dot(silu_cols, mod_weight).reshape(2 * PLANE, z_size * slots, mod_cols)
+        qkv_wide = jnp.concatenate([qkv_z[j] for j in range(z_size)], axis=1)
+        qkv_pieces = jnp.stack(
+            [
+                jnp.concatenate(
+                    [
+                        qkv_wide[:, t * width + p * part_cols : t * width + (p + 1) * part_cols]
+                        for t in range(3)
+                    ],
+                    axis=1,
+                )
+                for p in range(PLANE)
+            ]
+        )
+        plan = [
+            (hop, 0, to_chip, 0, by_dp, None) for hop in PLANE_HOPS
+        ]
+        plan += [
+            (hop, 1, lambda me, peer: (peer.dp,), 1, lambda me, peer: (me.dp,), None)
+            for hop in DP_HOPS
+            if hop != SELF
+        ]
+        plan.append((CORE_HOP, 2, None, 2, None, None))
+        for number, (dy, dx, dc, dz) in enumerate(PLANE_HOPS):
+            from_hop = lambda me, peer, dy=dy, dx=dx: (me.hop(dy, dx, 0, 0).dp,)
+            plan.append((CORE_HOP, 0, from_hop, 0, from_hop, (number,)))
+        plan.append((CORE_HOP, 0, by_chip, 0, by_dp, None))
+        qkv_slice, mod_parts, proj_other = exchange(
+            2,
+            [qkv_pieces, mod_part, proj_z],
+            [
+                ((2 * PLANE, shard, 3 * part_cols), low),
+                (mod_part.shape, full),
+                (proj_z.shape, low),
+            ],
+            plan,
+        )
+        qkv_slice = put(
+            qkv_slice, lax.dynamic_index_in_dim(qkv_pieces, chip, 0, keepdims=False), dp_index
+        )
+        mod_parts = put(
+            mod_parts, lax.dynamic_index_in_dim(mod_part, dp_index, 0, keepdims=False), dp_index
+        )
+        qkv_slice = qkv_slice.reshape(-1, 3 * part_cols)
+        proj_slice = both_cores(*core_order(proj_z, proj_other))
+        mod_sum = (jnp.sum(mod_parts, axis=0) + mod_bias.astype(full)).reshape(
+            z_size, slots, mod_cols
+        )
+        plan = [
+            (hop, 0, to_z, 0, lambda me, peer: (me.chip, me.z), None) for hop in Z_HOPS + [SELF]
+        ]
+        plan += [(hop, 0, by_chip, 0, by_chip, (0, 1, 2, 3)) for hop in PLANE_HOPS]
+        (group_mod,) = exchange(
+            3, [mod_sum], [((PLANE, z_size, slots, mod_cols), full)], plan
+        )
+        group_mod = group_mod.transpose(0, 2, 1, 3).reshape(PLANE, slots, z_size * mod_cols)
+        modulation = lax.dynamic_index_in_dim(group_mod, chip, 0, keepdims=False)
+
+        group_mod, (cot_later, up_z) = tie(group_mod, (out_cotangent, up_z))
+        cot_all = xor_order(jnp.stack(plane_blocks(cot_later)), chip, PLANE)
+        cot_all = cot_all.reshape(rows_all, width)
+        half = up_weight.shape[1] * z_size // 2
+        part_units = half // PLANE
+        up_wide = jnp.concatenate([up_z[j] for j in range(z_size)], axis=1)
+        up_slice = scatter_columns(
+            [
+                jnp.concatenate(
+                    [
+                        up_wide[:, t * half + p * part_units : t * half + (p + 1) * part_units]
+                        for t in range(2)
+                    ],
+                    axis=1,
+                )
+                for p in range(PLANE)
+            ]
+        )
+        segments = meta_all[:, 0].reshape(-1)
+        tables = rotary_tables(meta_all[:, 1:].transpose(1, 0, 2).reshape(2, -1), head_size // 4)
+
+        gain_cols = qk_gains.shape[1]
+        sizes = [qkv_bias.shape[0], proj_bias.shape[0], up_bias.shape[0], down_bias.shape[0]]
+        vectors = vectors[:, 0].astype(full)
+        bounds = [0]
+        for size in sizes + [gain_cols, gain_cols]:
+            bounds.append(bounds[-1] + size)
+        pieces = [vectors[:, bounds[k] : bounds[k + 1]] for k in range(6)]
+        qkv_vector, proj_vector, up_vector, down_vector, gain_q, gain_k = [
+            p.reshape(-1) for p in pieces
+        ]
+
+        def own_columns(flat, groups):
+            parts = flat.reshape(groups, PLANE, -1)
+            return lax.dynamic_slice_in_dim(parts, chip, 1, axis=1).reshape(-1)
+
+        seg_spans = segments.reshape(PLANE, spans, SPAN)[:, :, 0]
+        hot = (seg_spans[:, :, None] == jnp.arange(slots, dtype=jnp.int32)).astype(full)
+        group_spans = jnp.sum(hot[:, :, :, None] * group_mod[:, None], axis=2)
+        own_spans_ids = segment_ids.reshape(spans, SPAN)[:, 0]
+        own_hot = (own_spans_ids[:, None] == jnp.arange(slots, dtype=jnp.int32)).astype(full)
+        own_spans = jnp.sum(own_hot[:, :, None] * modulation[None], axis=1)
+
+        def spread(values):
+            count = values.shape[0]
+            return jnp.broadcast_to(values[:, None, :], (count, SPAN, width)).reshape(
+                count * SPAN, width
+            )
+
+        def per_row(k):
+            return spread(own_spans[:, k * width : (k + 1) * width])
+
+        def per_row_all(k):
+            return spread(
+                group_spans[:, :, k * width : (k + 1) * width].reshape(PLANE * spans, width)
+            )
+
+        patch_all = patch_all.reshape(rows_all, width).astype(full)
+        hidden_one = (
+            patch_all * rms_scale(patch_all) * (1.0 + per_row_all(1)) + per_row_all(0)
+        ).astype(low)
+
+        def core_swap(source, out, count):
+            return [
+                (
+                    CORE_HOP,
+                    source,
+                    lambda me, peer, k=k: (k, peer.core),
+                    out,
+                    lambda me, peer, k=k: (k,),
+                    None,
+                )
+                for k in range(count)
+            ]
+
+        def half_of(parts):
+            return ((parts.shape[0],) + parts.shape[2:], low)
+
+        def sum_cores(parts, other):
+            mine = jnp.where(upper, parts[:, 1], parts[:, 0])
+            return (mine.astype(full) + other.astype(full)).astype(low)
+
+        def row_parts(left, right):
+            cols = right.shape[1] // z_size
+            parts = jnp.stack(
+                [
+                    outer_grad(left, right[:, j * cols : (j + 1) * cols]).astype(low)
+                    for j in range(z_size)
+                ]
+            )
+            return parts.reshape(z_size, 2, -1, cols)
+
+        def widen(moved, groups):
+            moved = moved.reshape(PLANE, shard, groups, -1)
+            wide = jnp.concatenate(
+                [moved[p, :, t] for t in range(groups) for p in range(PLANE)], axis=1
+            )
+            cols = wide.shape[1] // z_size
+            return jnp.stack([wide[:, j * cols : (j + 1) * cols] for j in range(z_size)])
+
+        def own_of(values, index):
+            return lax.dynamic_index_in_dim(values, index, 0, keepdims=False)
+
+        def z_sum_of(blocks, sent):
+            return block_sum(blocks, own_of(sent, z_index))
+
+        def plane_gather(identity, values, *more):
+            (out,) = exchange(
+                identity,
+                [values],
+                [((PLANE,) + values.shape, low)],
+                gather_moves(PLANE_HOPS, 0, 0, by_chip),
+            )
+            return put(out, values, chip).reshape(rows_all, width)
+
+        scatter_plan = slotted(PLANE_HOPS, 0, to_chip, 0)
+        others = (PLANE - 1, row_count, width)
+
+        def plane_scatter(values):
+            return values.astype(low).reshape(PLANE, row_count, width)
+
+        def block_sum(blocks, own):
+            return own.astype(full) + jnp.sum(blocks.astype(full), axis=0)
+
+        def plane_sum_of(blocks, sent):
+            return block_sum(blocks, lax.dynamic_index_in_dim(sent, chip, 0, keepdims=False))
+
+        head_shape = (rows_all, heads, head_size)
+        block_shape = (PLANE, row_count, heads, head_size)
+        qkv_rows = dot(hidden_one, qkv_slice) + own_columns(qkv_vector, 3)
+        query_raw = qkv_rows[:, 0:part_cols].reshape(head_shape)
+        key_raw = qkv_rows[:, part_cols : 2 * part_cols].reshape(head_shape)
+        value_low = qkv_rows[:, 2 * part_cols :].astype(low).reshape(block_shape)
+        query_scale = rms_scale(query_raw)
+        query_unit = query_raw * query_scale
+        key_scale = rms_scale(key_raw)
+        key_unit = key_raw * key_scale
+        query_low = rotate(query_unit * gain_q, tables, 1.0).astype(low).reshape(block_shape)
+        key_low = rotate(key_unit * gain_k, tables, 1.0).astype(low).reshape(block_shape)
+        seg_blocks = segments.reshape(PLANE, row_count)
+        same_item = (seg_blocks[:, :, None] == seg_blocks[:, None, :])[:, None]
+        scores = jnp.einsum("bqhd,bkhd->bhqk", query_low, key_low, preferred_element_type=full)
+        scores = jnp.where(same_item, scores * score_scale, -1e30)
+        exponentials = jnp.exp(scores - jnp.max(scores, axis=-1, keepdims=True))
+        probs = exponentials / jnp.sum(exponentials, axis=-1, keepdims=True)
+        probs_low = probs.astype(low)
+        attended_low = (
+            jnp.einsum("bhqk,bkhd->bqhd", probs_low, value_low, preferred_element_type=full)
+            .astype(low)
+            .reshape(rows_all, part_cols)
+        )
+        attn_terms = plane_scatter(dot(attended_low, proj_slice))
+        attn_terms, (cot_all, up_slice) = tie(attn_terms, (cot_all, up_slice))
+        cot_all = cot_all.astype(full)
+        branch_blocks, down_z = exchange(
+            4,
+            [attn_terms, down_weight],
+            [
+                (others, low),
+                ((z_size,) + down_weight.shape, low),
+            ],
+            scatter_plan + gather_moves(Z_HOPS, 1, 1, by_z),
+        )
+        down_z = put(down_z, down_weight, z_index)
+        branch_attn = plane_sum_of(branch_blocks, attn_terms) + proj_vector
+
+        patch_full = patches.astype(full)
+        scale_one = rms_scale(patch_full)
+        normed_one = patch_full * scale_one
+        middle = patch_full + per_row(2) * branch_attn
+        scale_two = rms_scale(middle)
+        normed_two = middle * scale_two
+        hidden_two = (normed_two * (1.0 + per_row(4)) + per_row(3)).astype(low)
+
+        hidden_all, down_other = exchange(
+            5,
+            [hidden_two, down_z],
+            [((PLANE, row_count, width), low), (down_z.shape, low)],
+            gather_moves(PLANE_HOPS, 0, 0, by_chip) + [(CORE_HOP, 1, None, 1, None, None)],
+        )
+        hidden_all = put(hidden_all, hidden_two, chip).reshape(rows_all, width)
+        down_slice = both_cores(*core_order(down_z, down_other))
+        grad_branch_ffn = (cot_all * per_row_all(5)).astype(low)
+        grad_gated = dot_t(grad_branch_ffn, down_slice)
+        gate_up = dot(hidden_all, up_slice) + own_columns(up_vector, 2)
+        gate_part = gate_up[:, :part_units]
+        up_part = gate_up[:, part_units:]
+        gated_low = (jax.nn.silu(gate_part) * up_part).astype(low)
+        grad_gate_up = jnp.concatenate(
+            [grad_gated * up_part * silu_slope(gate_part), grad_gated * jax.nn.silu(gate_part)],
+            axis=1,
+        ).astype(low)
+        hidden_two_terms = plane_scatter(dot_t(grad_gate_up, up_slice))
+        down_parts = row_parts(gated_low, grad_branch_ffn)
+        up_parts = outer_grad(hidden_all, grad_gate_up).astype(low).reshape(PLANE, 2, shard, -1)
+        hidden_two_blocks, down_other, up_other = exchange(
+            6,
+            [hidden_two_terms, down_parts, up_parts],
+            [(others, low), half_of(down_parts), half_of(up_parts)],
+            scatter_plan + core_swap(1, 1, z_size) + core_swap(2, 2, PLANE),
+        )
+        grad_hidden_two = plane_sum_of(hidden_two_blocks, hidden_two_terms)
+        down_mine = sum_cores(down_parts, down_other)
+        up_mine = sum_cores(up_parts, up_other)
+        ffn_terms = plane_scatter(dot(gated_low, down_slice))
+
+        grad_out = out_cotangent.astype(full)
+        own_gbf = (grad_out * per_row(5)).astype(low).astype(full)
+        down_bias_grad = jnp.sum(own_gbf, axis=0)
+        up_bias_cols = jnp.sum(grad_gate_up.astype(full), axis=0)
+        grad_middle = grad_out + norm_backward(
+            grad_hidden_two * (1.0 + per_row(4)), normed_two, scale_two
+        )
+        grad_gate_attn = grad_middle * branch_attn
+        grad_branch_attn = (grad_middle * per_row(2)).astype(low)
+        proj_bias_grad = jnp.sum(grad_branch_attn.astype(full), axis=0)
+        grad_branch_all, down_blocks = exchange(
+            7,
+            [grad_branch_attn, down_mine],
+            [
+                ((PLANE, row_count, width), low),
+                ((z_size - 1,) + down_mine.shape[1:], low),
+            ],
+            gather_moves(PLANE_HOPS, 0, 0, by_chip) + slotted(Z_HOPS, 1, to_z, 1),
+        )
+        grad_branch_all = put(grad_branch_all, grad_branch_attn, chip).reshape(rows_all, width)
+        down_grad = z_sum_of(down_blocks, down_mine)
+
+        grad_branch_all, (ffn_terms, up_mine) = tie(grad_branch_all, (ffn_terms, up_mine))
+        ffn_terms = xor_order(ffn_terms, chip, PLANE)
+        branch_ffn = ffn_terms[0].astype(full)
+        for hop in range(1, PLANE):
+            branch_ffn = branch_ffn + cross(ffn_terms[hop], hop).astype(full)
+        branch_ffn = branch_ffn + down_vector
+        block_out = (middle + per_row(5) * branch_ffn).astype(low)
+        grad_gate_ffn = grad_out * branch_ffn
+        up_mine = xor_order(up_mine, chip, PLANE)
+        up_moved = jnp.stack([up_mine[0]] + [cross(up_mine[hop], hop) for hop in range(1, PLANE)])
+        up_wide = widen(xor_order(up_moved, chip, PLANE), 2)
+
+        grad_attended = dot_t(grad_branch_all, proj_slice).astype(low).reshape(block_shape)
+        proj_parts = row_parts(attended_low, grad_branch_all)
+        grad_probs = jnp.einsum(
+            "bqhd,bkhd->bhqk", grad_attended, value_low, preferred_element_type=full
+        )
+        row_dot = jnp.sum(probs * grad_probs, axis=-1, keepdims=True)
+        grad_scores = (probs * (grad_probs - row_dot)).astype(low)
+        grad_values = jnp.einsum(
+            "bhqk,bqhd->bkhd", probs_low, grad_attended, preferred_element_type=full
+        )
+        grad_query_rot = score_scale * jnp.einsum(
+            "bhqk,bkhd->bqhd", grad_scores, key_low, preferred_element_type=full
+        )
+        grad_key_rot = score_scale * jnp.einsum(
+            "bhqk,bqhd->bkhd", grad_scores, query_low, preferred_element_type=full
+        )
+        back_query = rotate(grad_query_rot.reshape(head_shape), tables, -1.0)
+        back_key = rotate(grad_key_rot.reshape(head_shape), tables, -1.0)
+        gain_q_grad = jnp.sum(back_query * query_unit, axis=(0, 1))
+        gain_k_grad = jnp.sum(back_key * key_unit, axis=(0, 1))
+        grad_query_raw = norm_backward(back_query * gain_q, query_unit, query_scale)
+        grad_key_raw = norm_backward(back_key * gain_k, key_unit, key_scale)
+        grad_qkv = jnp.concatenate(
+            [
+                grad_query_raw.reshape(rows_all, part_cols),
+                grad_key_raw.reshape(rows_all, part_cols),
+                grad_values.reshape(rows_all, part_cols),
+            ],
+            axis=1,
+        ).astype(low)
+        qkv_bias_cols = jnp.sum(grad_qkv.astype(full), axis=0)
+        qkv_parts = outer_grad(hidden_one, grad_qkv).astype(low).reshape(PLANE, 2, shard, -1)
+        hidden_one_terms = plane_scatter(dot_t(grad_qkv, qkv_slice))
+        hidden_one_terms, (block_out, grad_gate_ffn, up_wide) = tie(
+            hidden_one_terms, (block_out, grad_gate_ffn, up_wide)
+        )
+        up_grad = lax.psum_scatter(up_wide, "fsdp", scatter_dimension=0, tiled=False).astype(full)
+        hidden_one_blocks, qkv_other, proj_other = exchange(
+            8,
+            [hidden_one_terms, qkv_parts, proj_parts],
+            [(others, low), half_of(qkv_parts), half_of(proj_parts)],
+            scatter_plan + core_swap(1, 1, PLANE) + core_swap(2, 2, z_size),
+        )
+        grad_hidden_one = plane_sum_of(hidden_one_blocks, hidden_one_terms)
+        qkv_mine = sum_cores(qkv_parts, qkv_other)
+        proj_mine = sum_cores(proj_parts, proj_other)
+        patch_grad = (
+            grad_middle + norm_backward(grad_hidden_one * (1.0 + per_row(1)), normed_one, scale_one)
+        ).astype(low)
+
+        def span_sum(values):
+            return jnp.sum(values.reshape(spans, SPAN, width), axis=1)
+
+        grad_spans = jnp.concatenate(
+            [
+                span_sum(grad_hidden_one),
+                span_sum(grad_hidden_one * normed_one),
+                span_sum(grad_gate_attn),
+                span_sum(grad_hidden_two),
+                span_sum(grad_hidden_two * normed_two),
+                span_sum(grad_gate_ffn),
+            ],
+            axis=1,
+        )
+        grad_modulation = jnp.sum(own_hot[:, :, None] * grad_spans[:, None, :], axis=0).astype(low)
+        grad_mod = grad_modulation.reshape(slots, z_size, mod_cols).transpose(1, 0, 2)
+
+        def place(flat, groups):
+            spot = (jnp.arange(PLANE) == chip).astype(full)
+            return (flat.reshape(groups, 1, -1) * spot[None, :, None]).reshape(-1)
+
+        rows = [
+            place(qkv_bias_cols, 3),
+            proj_bias_grad,
+            place(up_bias_cols, 2),
+            down_bias_grad,
+            gain_q_grad,
+            gain_k_grad,
+        ]
+        vector_grad = jnp.concatenate([r.reshape(z_size, 1, -1) for r in rows], axis=2)
+        plan = [
+            (hop, 1, to_z, 1, lambda me, peer: (me.dp, me.z), None) for hop in Z_HOPS + [SELF]
+        ]
+        plan += [(hop, 2, to_z, 2, by_z, None) for hop in Z_HOPS + [SELF]]
+        plan += [(hop, 0, to_chip, 0, by_chip, None) for hop in PLANE_HOPS]
+        plan += [(hop, 1, by_dp, 1, by_dp, (0, 1, 2, 3)) for hop in DP_HOPS if hop != SELF]
+        plan += slotted(Z_HOPS, 3, to_z, 3)
+        qkv_moved, grad_mod, vector_parts, proj_blocks = exchange(
+            9,
+            [qkv_mine, grad_mod, vector_grad, proj_mine],
+            [
+                (qkv_mine.shape, low),
+                ((2 * PLANE, z_size, slots, mod_cols), low),
+                (vector_grad.shape, full),
+                ((z_size - 1,) + proj_mine.shape[1:], low),
+            ],
+            plan,
+        )
+        proj_grad = z_sum_of(proj_blocks, proj_mine)
+        qkv_wide = widen(put(qkv_moved, own_of(qkv_mine, chip), chip), 3)
+        grad_mod = grad_mod.reshape(-1, mod_cols)
+        vector_sum = jnp.sum(vector_parts, axis=0)
+        cond_part = dot_t(grad_mod, mod_weight).reshape(2 * PLANE, z_size, slots, mod_rows)
+        plan = slotted(Z_HOPS, 0, to_z, 0)
+        plan += [
+            (
+                hop,
+                1,
+                lambda me, peer: (peer.dp, peer.z),
+                1,
+                lambda me, peer: (me.dp, me.z),
+                None,
+            )
+            for hop in ALL_HOPS
+        ]
+        plan += gather_moves(DP_HOPS, 2, 2, by_dp)
+        qkv_blocks, cond_parts, vector_parts = exchange(
+            10,
+            [qkv_wide, cond_part, vector_sum],
+            [
+                ((z_size - 1,) + qkv_wide.shape[1:], low),
+                (cond_part.shape, full),
+                ((2 * PLANE,) + vector_sum.shape, full),
+            ],
+            plan,
+        )
+        qkv_grad = z_sum_of(qkv_blocks, qkv_wide)
+        mod_bias_grad = jnp.sum(grad_mod.astype(full), axis=0)
+        mod_grad = outer_grad(silu_cols, grad_mod)
+        cond_part = jnp.sum(cond_parts, axis=1)
+        cond_grad = (
+            cond_part.transpose(1, 0, 2).reshape(slots, width) * silu_slope(cond_full)
+        ).astype(low)
+        vector_grad = jnp.sum(vector_parts, axis=0)[0]
+        out = [vector_grad[bounds[k] : bounds[k + 1]] for k in range(6)]
+        return (
+            block_out,
+            patch_grad,
+            cond_grad,
+            mod_grad,
+            mod_bias_grad,
+            qkv_grad,
+            out[0],
+            jnp.stack([out[4], out[5]]),
+            proj_grad,
+            out[1],
+            up_grad,
+            out[2],
+            down_grad,
+            out[3],
+        )
+
+    return per_device
+
+
 def solution(mesh):
+    if mesh.shape["dp"] == 2 * PLANE and mesh.shape["fsdp"] == 4:
+        body = make_plane(mesh.shape["fsdp"])
+    else:
+        body = make_plain(mesh.shape["dp"], mesh.shape["fsdp"])
     rows = P(("dp", "fsdp"), None)
     matrix = P("dp", "fsdp")
     vector = P("fsdp")
     gains = P(None, "fsdp")
     return jax.shard_map(
-        make_per_device(mesh.shape["dp"], mesh.shape["fsdp"]),
+        body,
         mesh=mesh,
         in_specs=(
             rows,

time: 908 us -> 670 us (0.74)
  waiting for transfers between devices: 555 us -> 3.04 us
  Pallas kernels: 0 us -> 276 us
  other arithmetic: 66.5 us -> 119 us
  starting transfers between devices: 37.4 us -> 14.1 us
    pallas_call x0 -> x10, Pallas kernels: none -> 276 us  [exchange(): pl.pallas_call(kernel, out_shape=[jax.ShapeDtypeStruct(shape, dtype) for...]
    reduce_scatter x6 -> x1, waiting for transfers between devices: 249 us -> 0.01 us  [per_device(): lax.psum_scatter(up_wide, 'fsdp', scatter_dimension=0, tiled=False)]
    all_gather x4 -> x1, waiting for transfers between devices: 170 us -> 0.01 us  [per_device(): up_z = lax.all_gather(up_later, 'fsdp', axis=0, tiled=False)]
    unnamed x12 -> x2, waiting for transfers between devices: 92.7 us -> 0.03 us
    ppermute x27 -> x13, waiting for transfers between devices: 43.7 us -> 3.01 us  [the longest x12 3 us: cross(): lax.ppermute(values, 'dp', [(k, k ^ 2 * hop) for k in range(2 * PLANE)])]
    concatenate x2 -> x19, local copies, waits for them, and re-layouts: 0.28 us -> 33.4 us  [the longest x16 26.2 us: rotate(): return jnp.concatenate(pieces_out, axis=-1)]
    ppermute x27 -> x13, starting transfers between devices: 36.2 us -> 14 us  [the longest x12 14 us: cross(): lax.ppermute(values, 'dp', [(k, k ^ 2 * hop) for k in range(2 * PLANE)])]
    convert_element_type x9 -> x17, other arithmetic: 8.42 us -> 29.1 us  [the longest x4 9.82 us: sum_cores(): return (mine.astype(full) + other.astype(full)).astype(low)]
  transfers between devices with their start and end apart: 38 -> 15, of which waited for: 28 -> 2; matrix products, arithmetic and copies ran while one was open for 19% -> 32% of each run, Pallas kernels for 0% -> 18%
where the time goes in v2:
time: 670 us; the launch traced here: 662 us
  Pallas kernels  276 us (41%)
  local copies, waits for them, and re-layouts  151 us (23%)
  other arithmetic  119 us (18%)
  matrix products  82.8 us (12%)
  between operations  16.4 us (2%)
  starting transfers between devices  14.1 us (2%)
    pallas_call x10, Pallas kernels, exchange(): pl.pallas_call(kernel, out_shape=[jax.ShapeDtypeStruct(shape, dtype) for...  276 us
    concatenate x16, local copies, waits for them, and re-layouts, rotate(): return jnp.concatenate(pieces_out, axis=-1)  26.2 us
    dot_general x11, matrix products, outer_grad(): lax.dot_general(left, right, (((0,), (0,)), ((), ())), preferred_element_...  24.1 us
    dot_general x5, matrix products, dot_t(): lax.dot_general(left, right, (((1,), (1,)), ((), ())), preferred_element_...  24 us
    unnamed x275, local copies, waits for them, and re-layouts  23.7 us
    dot_general x5, matrix products, dot(): return jnp.dot(left, right, preferred_element_type=full)  17.6 us
    ppermute x12, starting transfers between devices, cross(): lax.ppermute(values, 'dp', [(k, k ^ 2 * hop) for k in range(2 * PLANE)])  14 us
  transfers between devices with their start and end apart: 15, of which 2 were waited for; matrix products, arithmetic and copies ran while one was open for 32% of the time, Pallas kernels for 18%

profile of v2, /device:TPU:0, one launch (start us, length us, event | category | flops | bytes accessed | tf_op | source)
XLA Modules:
  0.0 661.9 jit_solution(8105840419213438895)
XLA Ops:
  8.0 2.8 concatenate.139
  14.0 41.7 %shard_map.263 = (bf16[8,4,4,1152]{3,2,1,0:T(4,128)(2,1)}, bf16[4,144,864]{2,1,0:T(8,128)(2,1)}, bf16[4,256,1152]{2,1,0:T(8,128)(2,1)}, bf16[4,144,288]{2,1,0:T(...) custom-call(bf16[4,1152]{1,0:T(4,128)(2,1)} %fusion.77.refs_0_, bf16[144,864]{1,0:T(8,128)(2,1)} %refs_1_.2, ...), custom_call_target="tpu_custom_call" | custom-call | tf_op jit(solution)/shard_map/pallas_call | solution.py:508
  62.7 2.3 slice_bitcast_fusion.27
  66.2 1.9 fusion.109
  74.9 2.2 fusion.72
  78.3 24.8 %shard_map.264 = (bf16[8,144,864]{2,1,0:T(8,128)(2,1)}, f32[8,16,1728]{2,1,0:T(8,128)}, bf16[4,144,288]{2,1,0:T(8,128)(2,1)}) custom-call(bf16[4,144,864]{2,1,0:T(8,128)(2,1)} %pad_maximum_fusion.11.refs_0_, f32[8,16,1728]{2,1,0:T(8,128)} %bitcast.553, bf16[4,144,288]{2,1,0:T(8,128)(2,1)} %bitcast_dynamic-update-slice_fusion.5.refs_2_), custom_call_target="tpu_custom_call" | custom-call | tf_op jit(solution)/shard_map/pallas_call | solution.py:508
  126.1 13.5 %shard_map.265 = f32[4,4,4,1728]{3,2,1,0:T(4,128)} custom-call(f32[4,4,1728]{2,1,0:T(4,128)} %broadcast_add_fusion.refs_0_), custom_call_target="tpu_custom_call" | custom-call | tf_op jit(solution)/shard_map/pallas_call | solution.py:508
  139.6 1.9 copy.679
  141.5 2.2 reshape.731
  143.8 2.4 concatenate.159
  154.7 2.3 multiply_reduce_fusion.2
  160.1 1.9 add_convert_fusion
  162.0 2.6 convolution_add_fusion.1
  174.3 2.8 reshape.737
  210.0 6.0 fusion.111
  216.0 2.8 fusion.23
  220.6 2.8 pad_maximum_fusion.5
  223.4 2.9 convolution_convert_fusion.4
  227.9 3.1 fusion.1
  231.9 1.9 pad_maximum_fusion.2
  236.2 2.1 broadcast_select_fusion.1
  239.5 2.4 reverse_select_fusion
  241.9 28.9 %shard_map.266 = (bf16[3,256,1152]{2,1,0:T(8,128)(2,1)}, bf16[4,384,288]{2,1,0:T(8,128)(2,1)}) custom-call(bf16[4,256,1152]{2,1,0:T(8,128)(2,1)} %bitcast.548, bf16[384,288]{1,0:T(8,128)(2,1)} %copy.699.refs_1_), custom_call_target="tpu_custom_call" | custom-call | tf_op jit(solution)/shard_map/pallas_call | solution.py:508
  270.9 1.9 convert_reduce_fusion.4
  273.8 2.1 multiply_reduce_fusion.8
  277.0 29.1 %shard_map.267 = (bf16[4,256,1152]{2,1,0:T(8,128)(2,1)}, bf16[4,384,288]{2,1,0:T(8,128)(2,1)}) custom-call(bf16[256,1152]{1,0:T(8,128)(2,1)} %fusion.34.refs_0_, bf16[4,384,288]{2,1,0:T(8,128)(2,1)} %bitcast_dynamic-update-slice_fusion.3.refs_1_), custom_call_target="tpu_custom_call" | custom-call | tf_op jit(solution)/shard_map/pallas_call | solution.py:508
  310.3 2.1 fusion.2
  315.0 6.2 convolution_add_fusion
  321.2 4.1 concatenate.168
  325.3 7.4 %multiply_convert_fusion.3 = (bf16[1024,768]{0,1:T(8,128)(2,1)S(1)}, bf16[1024,768]{0,1:T(8,128)(2,1)S(1)}, bf16[1024,768]{0,1:T(8,128)(2,1)S(1)}) fusion(f32[1024,1536]{0,1:T(8,128)} %convolution_add_fusion, bf16[1024,1152]{1,0:T(8,128)(2,1)} %fusion.2, bf16[768,1152]{1,0:T(8,128)(2,1)} %concatenate.168), kind=kOutput, calls=%fused_computation.39 | convolution fusion | flops 1823735808 | bytes 15138816 | tf_op jit(solution)/shard_map/dot_general | solution.py:51
  332.8 5.6 convolution_convert_fusion.3
  340.0 6.6 convolution_convert_fusion
  352.7 3.7 convolution_convert_fusion.2
  358.0 2.1 copy.702
  360.1 2.1 copy.703
  362.2 2.3 dynamic-slice_convert_fusion.1
  367.3 28.4 %shard_map.268 = (bf16[3,256,1152]{2,1,0:T(8,128)(2,1)}, bf16[4,384,288]{2,1,0:T(8,128)(2,1)}, bf16[4,144,1536]{2,1,0:T(8,128)(2,1)}) custom-call(bf16[4,256,1152]{2,1,0:T(8,128)(2,1)} %bitcast.533, bf16[4,2,384,288]{3,2,1,0:T(8,128)(2,1)} %copy.706.refs_1_, bf16[4,2,144,1536]{3,2,1,0:T(8,128)(2,1)} %bitcast.521), custom_call_target="tpu_custom_call" | custom-call | tf_op jit(solution)/shard_map/pallas_call | solution.py:508
  395.7 4.6 fusion.4
  403.9 2.8 convert_reduce_fusion.8
  406.7 27.6 %shard_map.269 = (bf16[4,256,1152]{2,1,0:T(8,128)(2,1)}, bf16[3,384,288]{2,1,0:T(8,128)(2,1)}) custom-call(bf16[256,1152]{1,0:T(8,128)(2,1)} %get-tuple-element.275.refs_0_, bf16[4,384,288]{2,1,0:T(8,128)(2,1)} %fusion.9.refs_1_), custom_call_target="tpu_custom_call" | custom-call | tf_op jit(solution)/shard_map/pallas_call | solution.py:508
  434.4 1.9 bitcast_dynamic-update-slice_fusion
  436.3 3.7 convolution_convert_fusion.7
  445.2 2.4 reshape.753
  447.6 4.1 fusion.24
  458.6 2.7 bitcast_reduce_fusion.1
  461.3 1.9 bitcast_reduce_fusion.2
  463.8 2.9 fusion.8
  470.5 2.4 collective-permute-start.12
  493.7 4.0 convolution_convert_fusion.5
  500.1 4.2 copy.716
  504.3 6.2 convolution_convert_fusion.1
  514.4 4.8 reshape_reshape.45
  519.3 5.5 fusion.95
  526.8 1.9 collective-permute-done.8
  529.6 3.2 convert_multiply_fusion.2
  533.0 2.2 dynamic-slice_convert_fusion
  535.2 29.8 %shard_map.270 = (bf16[3,256,1152]{2,1,0:T(8,128)(2,1)}, bf16[4,144,864]{2,1,0:T(8,128)(2,1)}, bf16[4,144,288]{2,1,0:T(8,128)(2,1)}) custom-call(bf16[4,256,1152]{2,1,0:T(8,128)(2,1)} %bitcast.528, bf16[4,2,144,864]{3,2,1,0:T(8,128)(2,1)} %bitcast.519, bf16[4,2,144,288]{3,2,1,0:T(8,128)(2,1)} %copy.717.refs_2_), custom_call_target="tpu_custom_call" | custom-call | tf_op jit(solution)/shard_map/pallas_call | solution.py:508
  565.0 2.3 fusion.50.refs_3_
  575.4 20.0 %shard_map.271 = (bf16[4,144,864]{2,1,0:T(8,128)(2,1)}, bf16[8,4,4,1728]{3,2,1,0:T(4,128)(2,1)}, f32[4,1,3012]{2,1,0:T(1,128)}, bf16[3,144,288]{2,1,0:T(8,128)(2,1)}) custom-call(bf16[4,144,864]{2,1,0:T(8,128)(2,1)} %fusion.13.refs_0_, bf16[4,4,1728]{2,1,0:T(4,128)(2,1)} %bitcast.595, f32[4,1,3012]{2,1,0:T(1,128)} %concatenate.180.refs_2_, ...), custom_call_target="tpu_custom_call" | custom-call | tf_op jit(solution)/shard_map/pallas_call | solution.py:508
  599.8 3.9 reshape.774
  603.7 2.0 fusion.94
  608.9 31.8 %shard_map.272 = (bf16[3,144,864]{2,1,0:T(8,128)(2,1)}, f32[8,4,4,144]{3,2,1,0:T(4,128)}, f32[8,1,3012]{2,1,0:T(1,128)}) custom-call(bf16[4,144,864]{2,1,0:T(8,128)(2,1)} %pad_maximum_fusion.12.refs_0_, f32[8,4,4,144]{3,2,1,0:T(4,128)} %fusion.65.refs_1_, f32[1,3012]{1,0:T(1,128)} %bitcast.609), custom_call_target="tpu_custom_call" | custom-call | tf_op jit(solution)/shard_map/pallas_call | solution.py:508
  649.7 2.3 fusion.70
  652.6 2.0 bitcast_convert_fusion
  (529 shorter events, 200.0 us)
Async XLA Ops:
  7.2 67.7 %copy-start = (bf16[144,1728]{1,0:T(8,128)(2,1)S(1)}, bf16[144,1728]{1,0:T(8,128)(2,1)}, u32[]{:S(2)}) copy-start(bf16[144,1728]{1,0:T(8,128)(2,1)} %param.20) | copy-start | bytes 1492996
  7.2 145.1 %all-gather.3.cloned.1.call-start = ((), (), s32[]{:S(2)}) async-start(), calls=%async_computation.2 | async-start | bytes 2211840 | tf_op jit(solution)/shard_map/all_gather | solution.py:647
  55.7 9.3 %copy-start.1 = (bf16[256,1152]{1,0:T(8,128)(2,1)S(1)}, bf16[256,1152]{1,0:T(8,128)(2,1)}, u32[]{:S(2)}) copy-start(bf16[256,1152]{1,0:T(8,128)(2,1)} %refs_2_.1) | copy-start | bytes 1769476
  55.7 9.3 %copy-start.4 = (bf16[4,256,1152]{2,1,0:T(8,128)(2,1)S(1)}, bf16[4,256,1152]{2,1,0:T(8,128)(2,1)}, u32[]{:S(2)}) copy-start(bf16[4,256,1152]{2,1,0:T(8,128)(2,1)} %get-tuple-element.57) | copy-start | bytes 7077892
  55.8 596.9 %reduce-scatter.2.cloned.1.call-start = ((), (), s32[]{:S(2)}) async-start(), calls=%async_computation.1 | async-start | bytes 2211840 | tf_op jit(solution)/shard_map/reduce_scatter | solution.py:988
  120.4 19.2 %copy-start.108 = (f32[72]{0:T(128)}, f32[72]{0:T(128)S(1)}, u32[]{:S(2)}) copy-start(f32[72]{0:T(128)S(1)} %mul.698) | copy-start | bytes 868
  121.1 4.1 copy-start.106
  141.5 7.3 %copy-start.100 = (f32[4,4]{1,0:T(4,128)S(1)}, f32[4,4]{1,0:T(4,128)}, u32[]{:S(2)}) copy-start(f32[4,4]{1,0:T(4,128)} %fusion.86) | copy-start | bytes 196
  141.5 7.7 %copy-start.104 = (s32[4,3,256]{2,1,0:T(4,128)S(1)}, s32[4,3,256]{2,1,0:T(4,128)}, u32[]{:S(2)}) copy-start(s32[4,3,256]{2,1,0:T(4,128)} %get-tuple-element.58) | copy-start | bytes 36868
  141.5 8.6 %copy-start.115 = (f32[18]{0:T(128)S(1)}, f32[18]{0:T(128)}, u32[]{:S(2)}) copy-start(f32[18]{0:T(128)} %multiply_power_fusion) | copy-start | bytes 220
  146.2 13.9 %copy-start.98 = (f32[16,64]{1,0:T(8,128)S(1)}, f32[16,64]{1,0:T(8,128)}, u32[]{:S(2)}) copy-start(f32[16,64]{1,0:T(8,128)} %rsqrt.48) | copy-start | bytes 12292
  152.3 78.6 %collective-permute-start.2 = (bf16[256,1152]{1,0:T(8,128)(2,1)}, bf16[256,1152]{1,0:T(8,128)(2,1)}, u32[]{:S(2)}, u32[]{:S(2)}) collective-permute-start(bf16[256,1152]{1,0:T(8,128)(2,1)} %param.31), channel_id=1, source_target_pairs={{0,24},{4,28},{8,16},{12,20},{16,8},{20,12},{24,0},{28,4},{1,25},{... | collective-permute-start | bytes 1769480 | tf_op jit(solution)/shard_map/ppermute | solution.py:380
  154.1 76.8 %collective-permute-start.1 = (bf16[256,1152]{1,0:T(8,128)(2,1)}, bf16[256,1152]{1,0:T(8,128)(2,1)}, u32[]{:S(2)}, u32[]{:S(2)}) collective-permute-start(bf16[256,1152]{1,0:T(8,128)(2,1)} %param.31), channel_id=1, source_target_pairs={{0,16},{4,20},{8,24},{12,28},{16,0},{20,4},{24,8},{28,12},{1,17},{... | collective-permute-start | bytes 1769480 | tf_op jit(solution)/shard_map/ppermute | solution.py:380
  164.6 2.8 copy-start.18
  165.6 2.7 copy-start.48
  170.9 48.5 %collective-permute-start.5 = (bf16[144,1536]{1,0:T(8,128)(2,1)}, bf16[144,1536]{1,0:T(8,128)(2,1)}, u32[]{:S(2)}, u32[]{:S(2)}) collective-permute-start(bf16[144,1536]{1,0:T(8,128)(2,1)} %get-tuple-element.328), channel_id=1, source_target_pairs={{0,24},{4,28},{8,16},{12,20},{16,8},{20,12},{24,0},{28,4},{1,25},{... | collective-permute-start | bytes 1327112 | tf_op jit(solution)/shard_map/ppermute | solution.py:380
  172.3 48.2 %collective-permute-start.4 = (bf16[144,1536]{1,0:T(8,128)(2,1)}, bf16[144,1536]{1,0:T(8,128)(2,1)}, u32[]{:S(2)}, u32[]{:S(2)}) collective-permute-start(bf16[144,1536]{1,0:T(8,128)(2,1)} %get-tuple-element.329), channel_id=1, source_target_pairs={{0,16},{4,20},{8,24},{12,28},{16,0},{20,4},{24,8},{28,12},{1,17},{... | collective-permute-start | bytes 1327112 | tf_op jit(solution)/shard_map/ppermute | solution.py:380
  173.5 47.1 %collective-permute-start.3 = (bf16[144,1536]{1,0:T(8,128)(2,1)}, bf16[144,1536]{1,0:T(8,128)(2,1)}, u32[]{:S(2)}, u32[]{:S(2)}) collective-permute-start(bf16[144,1536]{1,0:T(8,128)(2,1)} %get-tuple-element.330), channel_id=1, source_target_pairs={{0,8},{4,12},{8,0},{12,4},{16,24},{20,28},{24,16},{28,20},{1,9},{5... | collective-permute-start | bytes 1327112 | tf_op jit(solution)/shard_map/ppermute | solution.py:380
  192.5 3.2 copy-start.33
  192.5 3.2 copy-start.36
  192.5 3.2 copy-start.58
  192.5 3.2 copy-start.60
  219.3 4.0 copy-start.73
  219.4 12.6 %collective-permute-start = (bf16[256,1152]{1,0:T(8,128)(2,1)}, bf16[256,1152]{1,0:T(8,128)(2,1)}, u32[]{:S(2)}, u32[]{:S(2)}) collective-permute-start(bf16[256,1152]{1,0:T(8,128)(2,1)} %param.31), channel_id=1, source_target_pairs={{0,8},{4,12},{8,0},{12,4},{16,24},{20,28},{24,16},{28,20},{1,9},{5... | collective-permute-start | bytes 1769480 | tf_op jit(solution)/shard_map/ppermute | solution.py:380
  220.6 2.8 copy-start.71
  223.4 12.9 %collective-permute-start.6 = (bf16[4,144,1536]{2,1,0:T(8,128)(2,1)}, bf16[4,144,1536]{2,1,0:T(8,128)(2,1)}, u32[]{:S(2)}, u32[]{:S(2)}) collective-permute-start(bf16[4,144,1536]{2,1,0:T(8,128)(2,1)} %pad_maximum_fusion.5), channel_id=1, source_target_pairs={{0,4},{4,0},{8,12},{12,8},{16,20},{20,16},{24,28},{28,24},{1,5},{5... | collective-permute-start | bytes 5308424 | tf_op jit(solution)/shard_map/ppermute | solution.py:384
  270.9 2.8 copy-start.88
  270.9 2.8 copy-start.90
  272.8 3.2 copy-start.11
  276.0 30.1 %copy-start.23 = (bf16[4,384,288]{2,1,0:T(8,128)(2,1)S(1)}, bf16[4,384,288]{2,1,0:T(8,128)(2,1)}, u32[]{:S(2)}) copy-start(bf16[4,384,288]{2,1,0:T(8,128)(2,1)} %bitcast_dynamic-update-slice_fusion.3.refs_1_) | copy-start | bytes 2654212
  310.3 4.1 copy-start.117
  325.3 7.4 %copy-start.30 = (bf16[1,2,2,2,144,1536]{5,4,3,2,1,0:T(8,128)(2,1)S(1)}, bf16[1,2,2,2,144,1536]{5,4,3,2,1,0:T(8,128)(2,1)}, u32[]{:S(2)}) copy-start(bf16[1,2,2,2,144,1536]{5,4,3,2,1,0:T(8,128)(2,1)} %reverse_select_fusion) | copy-start | bytes 10616836
  340.0 6.6 copy-start.42
  395.7 4.7 copy-start.3
  395.7 4.7 copy-start.53
  436.3 3.7 copy-start.74
  436.3 3.7 copy-start.119
  444.0 3.6 copy-start.102
  447.6 4.1 copy-start.26
  447.6 4.1 copy-start.72
  447.6 4.1 copy-start.76
  458.6 2.7 copy-start.12
  469.2 4.8 copy-start.75
  470.5 4.9 copy-start.61
  470.5 40.0 %collective-permute-start.12 = (bf16[144,1536]{1,0:T(8,128)(2,1)}, bf16[144,1536]{1,0:T(8,128)(2,1)}, u32[]{:S(2)}, u32[]{:S(2)}) collective-permute-start(bf16[144,1536]{1,0:T(8,128)(2,1)} %get-tuple-element.324), channel_id=1, source_target_pairs={{0,24},{4,28},{8,16},{12,20},{16,8},{20,12},{24,0},{28,4},{1,25},{... | collective-permute-start | bytes 1327112 | tf_op jit(solution)/shard_map/ppermute | solution.py:380
  472.8 38.2 %collective-permute-start.11 = (bf16[144,1536]{1,0:T(8,128)(2,1)}, bf16[144,1536]{1,0:T(8,128)(2,1)}, u32[]{:S(2)}, u32[]{:S(2)}) collective-permute-start(bf16[144,1536]{1,0:T(8,128)(2,1)} %get-tuple-element.325), channel_id=1, source_target_pairs={{0,16},{4,20},{8,24},{12,28},{16,0},{20,4},{24,8},{28,12},{1,17},{... | collective-permute-start | bytes 1327112 | tf_op jit(solution)/shard_map/ppermute | solution.py:380
  473.2 37.9 %collective-permute-start.10 = (bf16[144,1536]{1,0:T(8,128)(2,1)}, bf16[144,1536]{1,0:T(8,128)(2,1)}, u32[]{:S(2)}, u32[]{:S(2)}) collective-permute-start(bf16[144,1536]{1,0:T(8,128)(2,1)} %get-tuple-element.326), channel_id=1, source_target_pairs={{0,8},{4,12},{8,0},{12,4},{16,24},{20,28},{24,16},{28,20},{1,9},{5... | collective-permute-start | bytes 1327112 | tf_op jit(solution)/shard_map/ppermute | solution.py:380
  477.7 3.2 copy-start.13
  481.0 4.2 copy-start.25
  482.2 3.1 copy-start.24
  482.2 44.6 %collective-permute-start.7 = (bf16[256,1152]{1,0:T(8,128)(2,1)}, bf16[256,1152]{1,0:T(8,128)(2,1)}, u32[]{:S(2)}, u32[]{:S(2)}) collective-permute-start(bf16[256,1152]{1,0:T(8,128)(2,1)} %get-tuple-element.298), channel_id=1, source_target_pairs={{0,8},{4,12},{8,0},{12,4},{16,24},{20,28},{24,16},{28,20},{1,9},{5... | collective-permute-start | bytes 1769480 | tf_op jit(solution)/shard_map/ppermute | solution.py:380
  483.4 43.4 %collective-permute-start.9 = (bf16[256,1152]{1,0:T(8,128)(2,1)}, bf16[256,1152]{1,0:T(8,128)(2,1)}, u32[]{:S(2)}, u32[]{:S(2)}) collective-permute-start(bf16[256,1152]{1,0:T(8,128)(2,1)} %get-tuple-element.299), channel_id=1, source_target_pairs={{0,24},{4,28},{8,16},{12,20},{16,8},{20,12},{24,0},{28,4},{1,25},{... | collective-permute-start | bytes 1769480 | tf_op jit(solution)/shard_map/ppermute | solution.py:380
  493.0 4.7 copy-start.44
  493.0 4.7 copy-start.46
  500.1 4.2 copy-start.41
  500.1 4.2 copy-start.45
  504.3 6.7 %copy-start.49 = (bf16[1,144,1536]{2,1,0:T(8,128)(2,1)S(1)}, bf16[1,144,1536]{2,1,0:T(8,128)(2,1)}, u32[]{:S(2)}) copy-start(bf16[1,144,1536]{2,1,0:T(8,128)(2,1)} %get-tuple-element.323) | copy-start | bytes 1327108
  510.5 18.3 %collective-permute-start.8 = (bf16[256,1152]{1,0:T(8,128)(2,1)}, bf16[256,1152]{1,0:T(8,128)(2,1)S(1)}, u32[]{:S(2)}, u32[]{:S(2)}) collective-permute-start(bf16[256,1152]{1,0:T(8,128)(2,1)} %get-tuple-element.300), channel_id=1, source_target_pairs={{0,16},{4,20},{8,24},{12,28},{16,0},{20,4},{24,8},{28,12},{1,17},{... | collective-permute-start | bytes 1769480 | tf_op jit(solution)/shard_map/ppermute | solution.py:380
  525.3 4.3 copy-start.91
  525.3 4.3 copy-start.97
  535.2 32.2 %copy-start.8 = (bf16[1152,864]{1,0:T(8,128)(2,1)S(1)}, bf16[1152,864]{1,0:T(8,128)(2,1)}, u32[]{:S(2)}) copy-start(bf16[1152,864]{1,0:T(8,128)(2,1)} %copy.716) | copy-start | bytes 5971972
  607.8 37.6 %copy-start.79 = (bf16[3,144,288]{2,1,0:T(8,128)(2,1)S(1)}, bf16[3,144,288]{2,1,0:T(8,128)(2,1)}, u32[]{:S(2)}) copy-start(bf16[3,144,288]{2,1,0:T(8,128)(2,1)} %get-tuple-element.97) | copy-start | bytes 746500
  640.7 5.5 copy-start.70
  646.3 5.7 copy-start.96
  (72 other events, 121.2 us)
Sparse Core Ops, SparseCore 0:
  55.9 38.8 all-gather.2
  533.0 37.4 reduce-scatter.1

commit v3 on v2

--- a/solution.py
+++ b/solution.py
@@ -1,5 +1,8 @@
+import functools
+
 import jax
 import jax.numpy as jnp
+import numpy as np
 from jax import lax
 from jax.experimental import pallas as pl
 from jax.experimental.pallas import tpu as pltpu
@@ -7,6 +10,7 @@
 
 HEADS = 16
 SPAN = 64
+SIDE = 16
 
 epsilon = 1e-06
 low = jnp.bfloat16
@@ -547,6 +551,38 @@
     return lax.dynamic_update_slice(values, own.reshape((1,) * len(at) + own.shape), start)
 
 
+HOP_X, HOP_Y = PLANE_HOPS[0], PLANE_HOPS[1]
+
+
+def relayed(source, out, place, first):
+    def at(hop, half):
+        return lambda me, peer: (place(me, hop), half)
+
+    def onto(hop, half):
+        return lambda me, peer: (place(peer, hop), half)
+
+    def part(half):
+        return lambda me, peer: (half,)
+
+    diagonal = PLANE_HOPS[2]
+    return [
+        (HOP_X, source, part(0), out, onto(HOP_X, 0), None),
+        (HOP_Y, source, part(1), out, onto(HOP_Y, 1), None),
+        (HOP_X, source, part(1), out, onto(HOP_X, 1), None),
+        (HOP_Y, source, part(0), out, onto(HOP_Y, 0), None),
+        (HOP_Y, out, at(HOP_X, 0), out, onto(diagonal, 0), (first,)),
+        (HOP_X, out, at(HOP_Y, 1), out, onto(diagonal, 1), (first + 1,)),
+    ]
+
+
+def chip_place(me, hop):
+    return me.hop(*hop).chip
+
+
+def hop_place(me, hop):
+    return PLANE_HOPS.index(hop)
+
+
 def slotted(hops, source, source_at, out):
     return [
         (hop, source, source_at, out, lambda me, peer, n=n: (n,), None)
@@ -560,6 +596,265 @@
 
 def to_z(me, peer):
     return (peer.z,)
+
+
+LANES = 128
+
+
+def head_of(values, number, head_size):
+    part = values[:, number * head_size : (number + 1) * head_size]
+    pad = jnp.zeros((values.shape[0], LANES - head_size), values.dtype)
+    return jnp.concatenate([part, pad], axis=1)
+
+
+def pair_of(values, head_size):
+    quarter = head_size // 4
+    lane = lax.broadcasted_iota(jnp.int32, values.shape, 1)
+    second = (lane // quarter) % 2 == 1
+    return jnp.where(
+        second, pltpu.roll(values, quarter, 1), pltpu.roll(values, LANES - quarter, 1)
+    )
+
+
+def unit_of(raw, head_size):
+    factor = lax.rsqrt(jnp.sum(raw * raw, axis=1, keepdims=True) * (1.0 / head_size) + epsilon)
+    return raw * factor, factor
+
+
+def head_probs(query, key, same, score_scale):
+    scores = jnp.where(same, dot_t(query, key) * score_scale, -1e30)
+    exponentials = jnp.exp(scores - jnp.max(scores, axis=1, keepdims=True))
+    return exponentials * (1.0 / jnp.sum(exponentials, axis=1, keepdims=True))
+
+
+def rotary_rows(head_size):
+    quarter = head_size // 4
+    frequencies = np.float32(10000.0) ** (-np.arange(quarter, dtype=np.float32) / quarter)
+    angles = np.arange(SIDE, dtype=np.float32)[:, None] * frequencies.astype(np.float32)
+    cosine = np.zeros((2, SIDE, LANES), np.float32)
+    sine = np.zeros((2, SIDE, LANES), np.float32)
+    for k in range(2):
+        first = 2 * quarter * k
+        cosine[k, :, first : first + 2 * quarter] = np.tile(np.cos(angles), (1, 2))
+        sine[k, :, first : first + quarter] = -np.sin(angles)
+        sine[k, :, first + quarter : first + 2 * quarter] = np.sin(angles)
+    return jnp.asarray(cosine.reshape(-1, LANES)), jnp.asarray(sine.reshape(-1, LANES))
+
+
+def rotary_of(meta, cosine_rows, sine_rows):
+    place = lax.broadcasted_iota(jnp.int32, (meta.shape[0], 2 * SIDE), 1)
+    hot = (meta[:, 1:2] == place) | (meta[:, 2:3] + SIDE == place)
+    hot = hot.astype(full)
+    take = functools.partial(jnp.dot, preferred_element_type=full, precision=lax.Precision.HIGHEST)
+    return take(hot, cosine_rows), take(hot, sine_rows)
+
+
+def attention_block(head_size, heads, refs):
+    (rows, gains, cosine, sine, seg_row, seg_col) = refs
+    same = seg_row == seg_col
+    gain_q, gain_k = gains[0:1], gains[1:2]
+    for h in range(heads):
+        query_unit, query_factor = unit_of(head_of(rows, h, head_size), head_size)
+        key_unit, key_factor = unit_of(head_of(rows, heads + h, head_size), head_size)
+        query = query_unit * gain_q
+        key = key_unit * gain_k
+        query = (query * cosine + pair_of(query, head_size) * sine).astype(low)
+        key = (key * cosine + pair_of(key, head_size) * sine).astype(low)
+        value = head_of(rows, 2 * heads + h, head_size).astype(low)
+        probs = head_probs(query, key, same, head_size ** (-0.5))
+        yield query_unit, query_factor, key_unit, key_factor, query, key, value, probs
+
+
+def fill_rows(target, mine, other):
+    rows = mine.shape[1]
+    core = lax.axis_index("dp") % 2
+    for source, place in ((mine, core), (other, 1 - core)):
+        target[pl.ds(pl.multiple_of(place * rows, 16), rows), :] = jnp.concatenate(
+            [source[j] for j in range(source.shape[0])], axis=1
+        )
+
+
+def attention_forward_kernel(head_size, heads, *refs):
+    (patch, shift, scale, weight, bias, gains, cos_rows, sin_rows, meta, seg_col) = refs[:10]
+    proj_mine, proj_other = refs[10:12]
+    hidden_out, rows_out, attended_out, terms_out, proj = refs[12:]
+
+    @pl.when(pl.program_id(0) == 0)
+    def _():
+        fill_rows(proj, proj_mine, proj_other)
+
+    cosine, sine = rotary_of(meta[0], cos_rows[...], sin_rows[...])
+    values = patch[0].astype(full)
+    count, width = values.shape
+    normed = values * lax.rsqrt(jnp.mean(values * values, axis=1, keepdims=True) + epsilon)
+    hidden = normed.reshape(count // SPAN, SPAN, width) * (1.0 + scale[0]) + shift[0]
+    hidden = hidden.reshape(count, width).astype(low)
+    hidden_out[0] = hidden
+    rows = dot(hidden, weight[...]) + bias[...]
+    rows_out[0] = rows
+    pieces = []
+    refs = (rows, gains[...], cosine, sine, meta[0, :, 0:1], seg_col[0])
+    for *_, value, probs in attention_block(head_size, heads, refs):
+        pieces.append(dot(probs.astype(low), value)[:, :head_size])
+    attended = jnp.concatenate(pieces, axis=1).astype(low)
+    attended_out[0] = attended
+    terms_out[0] = dot(attended, proj[...]).astype(low)
+
+
+def cut_columns(parts, total):
+    cols = parts.shape[3]
+    for j in range(parts.shape[0]):
+        parts[j] = total[:, j * cols : (j + 1) * cols].astype(low).reshape(parts.shape[1:])
+
+
+def attention_backward_kernel(head_size, heads, *refs):
+    (grad, rows, weight, gains, cos_rows, sin_rows, meta, seg_col, proj) = refs[:9]
+    hidden, attended = refs[9:11]
+    terms_out, bias_out, gains_out, qkv_parts, proj_parts = refs[11:16]
+    qkv_total, proj_total = refs[16:]
+
+    @pl.when(pl.program_id(0) == 0)
+    def _():
+        bias_out[...] = jnp.zeros_like(bias_out)
+        gains_out[...] = jnp.zeros_like(gains_out)
+        qkv_total[...] = jnp.zeros_like(qkv_total)
+        proj_total[...] = jnp.zeros_like(proj_total)
+
+    score_scale = head_size ** (-0.5)
+    gain_values = gains[...]
+    cos_tab, sin_tab = rotary_of(meta[0], cos_rows[...], sin_rows[...])
+    grad_attended = dot_t(grad[0], proj[...])
+    values = rows[0]
+    grad_queries, grad_keys, grad_values = [], [], []
+    gain_sums = [jnp.zeros((1, LANES), full), jnp.zeros((1, LANES), full)]
+
+    def raw_grad(rotated, unit, factor, which):
+        back = rotated * cos_tab - pair_of(rotated, head_size) * sin_tab
+        gain_sums[which] = gain_sums[which] + jnp.sum(back * unit, axis=0, keepdims=True)
+        turned = back * gain_values[which : which + 1]
+        mean = jnp.sum(turned * unit, axis=1, keepdims=True) * (1.0 / head_size)
+        return ((turned - unit * mean) * factor)[:, :head_size]
+
+    refs = (values, gain_values, cos_tab, sin_tab, meta[0, :, 0:1], seg_col[0])
+    for h, parts in enumerate(attention_block(head_size, heads, refs)):
+        query_unit, query_factor, key_unit, key_factor, query, key, value, probs = parts
+        grad_head = head_of(grad_attended, h, head_size).astype(low)
+        grad_probs = dot_t(grad_head, value)
+        row_dot = jnp.sum(probs * grad_probs, axis=1, keepdims=True)
+        grad_scores = (probs * (grad_probs - row_dot)).astype(low)
+        grad_values.append(outer_grad(probs.astype(low), grad_head)[:, :head_size])
+        grad_queries.append(
+            raw_grad(dot(grad_scores, key) * score_scale, query_unit, query_factor, 0)
+        )
+        grad_keys.append(
+            raw_grad(outer_grad(grad_scores, query) * score_scale, key_unit, key_factor, 1)
+        )
+    result = jnp.concatenate(grad_queries + grad_keys + grad_values, axis=1).astype(low)
+    bias_out[...] += jnp.sum(result.astype(full), axis=0, keepdims=True)
+    gains_out[0:1, :] += gain_sums[0]
+    gains_out[1:2, :] += gain_sums[1]
+    terms_out[0] = dot_t(result, weight[...]).astype(low)
+    qkv_total[...] += outer_grad(hidden[0], result)
+    proj_total[...] += outer_grad(attended[0], grad[0])
+
+    @pl.when(pl.program_id(0) == pl.num_programs(0) - 1)
+    def _():
+        qkv_parts[...] = qkv_total[...].astype(low).reshape(qkv_parts.shape)
+        cut_columns(proj_parts, proj_total[...])
+
+
+def ffn_kernel(*refs):
+    (own_hidden, hiddens, own_cot, cots, gate, up, down_mine, down_other, bias) = refs[:9]
+    hidden_terms, ffn_terms, bias_out, up_parts, down_parts = refs[9:14]
+    down, up_total, down_total = refs[14:]
+    step = pl.program_id(0)
+
+    @pl.when(step == 0)
+    def _():
+        bias_out[...] = jnp.zeros_like(bias_out)
+        up_total[...] = jnp.zeros_like(up_total)
+        down_total[...] = jnp.zeros_like(down_total)
+        fill_rows(down, down_mine, down_other)
+
+    count, width = own_hidden.shape
+    units = down.shape[0]
+    hidden = jnp.where(step == 0, own_hidden[...], hiddens[0])
+    cot = jnp.where(step == 0, own_cot[...], cots[0])
+    grad_branch = cot.astype(full).reshape(count // SPAN, SPAN, width) * gate[0]
+    grad_branch = grad_branch.reshape(count, width).astype(low)
+    grad_gated = dot_t(grad_branch, down[...])
+    gate_up = dot(hidden, up[...]) + bias[...]
+    gate_part, up_part = gate_up[:, :units], gate_up[:, units:]
+    sigmoid = jax.nn.sigmoid(gate_part)
+    silu = gate_part * sigmoid
+    gated = (silu * up_part).astype(low)
+    slope = sigmoid * (1.0 + gate_part * (1.0 - sigmoid))
+    grad_gate = (grad_gated * up_part * slope).astype(low)
+    grad_up = (grad_gated * silu).astype(low)
+    grads = jnp.concatenate([grad_gate, grad_up], axis=1)
+    bias_out[...] += jnp.sum(grads.astype(full), axis=0, keepdims=True)
+    hidden_terms[0] = dot_t(grads, up[...]).astype(low)
+    ffn_terms[0] = dot(gated, down[...]).astype(low)
+    up_total[...] += outer_grad(hidden, grads)
+    down_total[...] += outer_grad(gated, grad_branch)
+
+    @pl.when(step == pl.num_programs(0) - 1)
+    def _():
+        up_parts[...] = up_total[...].astype(low).reshape(up_parts.shape)
+        cut_columns(down_parts, down_total[...])
+
+
+def split_kernel(groups, source, target):
+    count, _, cols = source.shape
+    part = cols // groups
+    for p in range(count):
+        pieces = []
+        for t in range(groups):
+            block, at = divmod(t * count + p, groups)
+            pieces.append(source[block, :, at * part : (at + 1) * part])
+        target[p] = jnp.concatenate(pieces, axis=1)
+
+
+def merge_kernel(groups, source, target):
+    count, _, cols = source.shape
+    part = cols // groups
+    for z in range(count):
+        pieces = []
+        for at in range(groups):
+            t, p = divmod(z * groups + at, count)
+            pieces.append(source[p, :, t * part : (t + 1) * part])
+        target[z] = jnp.concatenate(pieces, axis=1)
+
+
+def whole_call(kernel, values):
+    return pl.pallas_call(kernel, out_shape=jax.ShapeDtypeStruct(values.shape, values.dtype))(values)
+
+
+def block_call(kernel, inputs, blocked, out_blocks, out_whole, scratch, steps, flops):
+    def block_spec(shape, mark=1):
+        tail = (0,) * (len(shape) - 1)
+        if mark == 2:
+            return pl.BlockSpec((1,) + shape[1:], lambda p: (jnp.maximum(p - 1, 0),) + tail)
+        return pl.BlockSpec((1,) + shape[1:], lambda p: (p,) + tail)
+
+    def whole_spec(shape):
+        return pl.BlockSpec(shape, lambda p: (0,) * len(shape))
+
+    return pl.pallas_call(
+        kernel,
+        grid=(steps,),
+        out_shape=[jax.ShapeDtypeStruct(*o) for o in out_blocks + out_whole],
+        in_specs=[
+            block_spec(v.shape, b) if b else whole_spec(v.shape) for v, b in zip(inputs, blocked)
+        ],
+        out_specs=[block_spec(o[0]) for o in out_blocks] + [whole_spec(o[0]) for o in out_whole],
+        scratch_shapes=[pltpu.VMEM(*o) for o in scratch],
+        cost_estimate=pl.CostEstimate(
+            flops=flops,
+            bytes_accessed=sum(v.size * v.dtype.itemsize for v in inputs),
+            transcendentals=flops // 1024,
+        ),
+    )(*inputs)
 
 
 def make_plane(z_size):
@@ -597,22 +892,11 @@
         rows_all = PLANE * row_count
         shard = qkv_weight.shape[0]
 
+        def halves(values):
+            return values.reshape(2, row_count // 2, width)
+
         def core_order(mine, other):
             return jnp.where(upper, other, mine), jnp.where(upper, mine, other)
-
-        def both_cores(first, second):
-            return jnp.concatenate(
-                [jnp.concatenate([first[j], second[j]], axis=0) for j in range(z_size)], axis=1
-            )
-
-        def scatter_columns(pieces):
-            ordered = xor_order(jnp.stack(pieces), chip, PLANE)
-            mine = jnp.stack(
-                [ordered[0]] + [cross(ordered[hop], hop) for hop in range(1, PLANE)]
-            )
-            first, second = core_order(mine, partner(mine))
-            both = xor_order(jnp.stack([first, second], axis=1), chip, PLANE)
-            return both.reshape(2 * PLANE * both.shape[2], both.shape[3])
 
         cond_full = conditions.astype(full)
         silu_low = jax.nn.silu(cond_full).astype(low)
@@ -628,14 +912,14 @@
         plan += gather_moves(Z_HOPS + [SELF], 4, 4, by_z)
         plan += gather_moves(PLANE_HOPS + [SELF], 5, 5, by_chip)
         plan += [(hop, 0, by_dp, 0, by_dp, (0, 1, 2, 3)) for hop in DP_HOPS if hop != SELF]
-        plan += gather_moves(PLANE_HOPS, 2, 2, by_chip)
+        plan += relayed(2, 2, chip_place, len(plan))
         silu_all, qkv_z, patch_all, proj_z, vectors, meta_all = exchange(
             1,
-            [silu_low, qkv_weight, patches, proj_weight, vector, meta],
+            [silu_low, qkv_weight, halves(patches), proj_weight, vector, meta],
             [
                 ((2 * PLANE, z_size, slots, width), low),
                 ((z_size, shard, cols_qkv), low),
-                ((PLANE, row_count, width), low),
+                ((PLANE, 2, row_count // 2, width), low),
                 ((z_size, shard, cols_proj), low),
                 ((z_size,) + vector.shape, low),
                 ((PLANE,) + meta.shape, jnp.int32),
@@ -647,24 +931,12 @@
         up_z = lax.all_gather(up_later, "fsdp", axis=0, tiled=False)
         qkv_z = put(qkv_z, qkv_weight, z_index)
         proj_z = put(proj_z, proj_weight, z_index)
-        patch_all = put(patch_all, patches, chip)
+        patch_all = put(patch_all.reshape(PLANE, row_count, width), patches, chip)
 
         silu_all = silu_all.reshape(-1, width)
         silu_cols = lax.dynamic_slice_in_dim(silu_all, dp_index * mod_rows, mod_rows, axis=1)
         mod_part = dot(silu_cols, mod_weight).reshape(2 * PLANE, z_size * slots, mod_cols)
-        qkv_wide = jnp.concatenate([qkv_z[j] for j in range(z_size)], axis=1)
-        qkv_pieces = jnp.stack(
-            [
-                jnp.concatenate(
-                    [
-                        qkv_wide[:, t * width + p * part_cols : t * width + (p + 1) * part_cols]
-                        for t in range(3)
-                    ],
-                    axis=1,
-                )
-                for p in range(PLANE)
-            ]
-        )
+        qkv_pieces = whole_call(functools.partial(split_kernel, 3), qkv_z)
         plan = [
             (hop, 0, to_chip, 0, by_dp, None) for hop in PLANE_HOPS
         ]
@@ -695,7 +967,6 @@
             mod_parts, lax.dynamic_index_in_dim(mod_part, dp_index, 0, keepdims=False), dp_index
         )
         qkv_slice = qkv_slice.reshape(-1, 3 * part_cols)
-        proj_slice = both_cores(*core_order(proj_z, proj_other))
         mod_sum = (jnp.sum(mod_parts, axis=0) + mod_bias.astype(full)).reshape(
             z_size, slots, mod_cols
         )
@@ -710,25 +981,22 @@
         modulation = lax.dynamic_index_in_dim(group_mod, chip, 0, keepdims=False)
 
         group_mod, (cot_later, up_z) = tie(group_mod, (out_cotangent, up_z))
-        cot_all = xor_order(jnp.stack(plane_blocks(cot_later)), chip, PLANE)
-        cot_all = cot_all.reshape(rows_all, width)
-        half = up_weight.shape[1] * z_size // 2
-        part_units = half // PLANE
-        up_wide = jnp.concatenate([up_z[j] for j in range(z_size)], axis=1)
-        up_slice = scatter_columns(
-            [
-                jnp.concatenate(
-                    [
-                        up_wide[:, t * half + p * part_units : t * half + (p + 1) * part_units]
-                        for t in range(2)
-                    ],
-                    axis=1,
-                )
-                for p in range(PLANE)
-            ]
-        )
+        cot_blocks = [cross(cot_later, hop) for hop in range(1, PLANE)]
+        units = up_weight.shape[1] // 2
+
+        def up_piece(hop):
+            to = chip ^ hop
+            parts = []
+            for t in range(2):
+                block = lax.dynamic_index_in_dim(up_z, 2 * t + (to >> 1), 0, keepdims=False)
+                parts.append(jnp.where((to & 1) == 1, block[:, units:], block[:, :units]))
+            return jnp.concatenate(parts, axis=1)
+
+        up_blocks = [up_piece(0)] + [cross(up_piece(hop), hop) for hop in range(1, PLANE)]
         segments = meta_all[:, 0].reshape(-1)
-        tables = rotary_tables(meta_all[:, 1:].transpose(1, 0, 2).reshape(2, -1), head_size // 4)
+        meta_rows = meta_all.transpose(0, 2, 1)
+        seg_col = meta_all[:, 0][:, None, :]
+        cos_rows, sin_rows = rotary_rows(head_size)
 
         gain_cols = qk_gains.shape[1]
         sizes = [qkv_bias.shape[0], proj_bias.shape[0], up_bias.shape[0], down_bias.shape[0]]
@@ -765,11 +1033,6 @@
             return spread(
                 group_spans[:, :, k * width : (k + 1) * width].reshape(PLANE * spans, width)
             )
-
-        patch_all = patch_all.reshape(rows_all, width).astype(full)
-        hidden_one = (
-            patch_all * rms_scale(patch_all) * (1.0 + per_row_all(1)) + per_row_all(0)
-        ).astype(low)
 
         def core_swap(source, out, count):
             return [
@@ -791,24 +1054,6 @@
             mine = jnp.where(upper, parts[:, 1], parts[:, 0])
             return (mine.astype(full) + other.astype(full)).astype(low)
 
-        def row_parts(left, right):
-            cols = right.shape[1] // z_size
-            parts = jnp.stack(
-                [
-                    outer_grad(left, right[:, j * cols : (j + 1) * cols]).astype(low)
-                    for j in range(z_size)
-                ]
-            )
-            return parts.reshape(z_size, 2, -1, cols)
-
-        def widen(moved, groups):
-            moved = moved.reshape(PLANE, shard, groups, -1)
-            wide = jnp.concatenate(
-                [moved[p, :, t] for t in range(groups) for p in range(PLANE)], axis=1
-            )
-            cols = wide.shape[1] // z_size
-            return jnp.stack([wide[:, j * cols : (j + 1) * cols] for j in range(z_size)])
-
         def own_of(values, index):
             return lax.dynamic_index_in_dim(values, index, 0, keepdims=False)
 
@@ -836,42 +1081,58 @@
         def plane_sum_of(blocks, sent):
             return block_sum(blocks, lax.dynamic_index_in_dim(sent, chip, 0, keepdims=False))
 
-        head_shape = (rows_all, heads, head_size)
-        block_shape = (PLANE, row_count, heads, head_size)
-        qkv_rows = dot(hidden_one, qkv_slice) + own_columns(qkv_vector, 3)
-        query_raw = qkv_rows[:, 0:part_cols].reshape(head_shape)
-        key_raw = qkv_rows[:, part_cols : 2 * part_cols].reshape(head_shape)
-        value_low = qkv_rows[:, 2 * part_cols :].astype(low).reshape(block_shape)
-        query_scale = rms_scale(query_raw)
-        query_unit = query_raw * query_scale
-        key_scale = rms_scale(key_raw)
-        key_unit = key_raw * key_scale
-        query_low = rotate(query_unit * gain_q, tables, 1.0).astype(low).reshape(block_shape)
-        key_low = rotate(key_unit * gain_k, tables, 1.0).astype(low).reshape(block_shape)
-        seg_blocks = segments.reshape(PLANE, row_count)
-        same_item = (seg_blocks[:, :, None] == seg_blocks[:, None, :])[:, None]
-        scores = jnp.einsum("bqhd,bkhd->bhqk", query_low, key_low, preferred_element_type=full)
-        scores = jnp.where(same_item, scores * score_scale, -1e30)
-        exponentials = jnp.exp(scores - jnp.max(scores, axis=-1, keepdims=True))
-        probs = exponentials / jnp.sum(exponentials, axis=-1, keepdims=True)
-        probs_low = probs.astype(low)
-        attended_low = (
-            jnp.einsum("bhqk,bkhd->bqhd", probs_low, value_low, preferred_element_type=full)
-            .astype(low)
-            .reshape(rows_all, part_cols)
-        )
-        attn_terms = plane_scatter(dot(attended_low, proj_slice))
-        attn_terms, (cot_all, up_slice) = tie(attn_terms, (cot_all, up_slice))
-        cot_all = cot_all.astype(full)
-        branch_blocks, down_z = exchange(
+        def group_span(k):
+            return group_spans[:, :, None, k * width : (k + 1) * width]
+
+        gain_pad = jnp.zeros((2, LANES), full)
+        gains = lax.dynamic_update_slice(gain_pad, jnp.stack([gain_q, gain_k]), (0, 0))
+        hidden_one, qkv_rows, attended_low, attn_terms, proj_slice = block_call(
+            functools.partial(attention_forward_kernel, head_size, heads),
+            [
+                patch_all,
+                group_span(0),
+                group_span(1),
+                qkv_slice,
+                own_columns(qkv_vector, 3)[None],
+                gains,
+                cos_rows,
+                sin_rows,
+                meta_rows,
+                seg_col,
+                proj_z,
+                proj_other,
+            ],
+            [1, 1, 1, 0, 0, 0, 0, 0, 1, 1, 0, 0],
+            [
+                ((PLANE, row_count, width), low),
+                ((PLANE, row_count, 3 * part_cols), full),
+                ((PLANE, row_count, part_cols), low),
+                ((PLANE, row_count, width), low),
+            ],
+            [((part_cols, width), low)],
+            [],
+            PLANE,
+            rows_all * width * 8 * part_cols,
+        )
+        attn_terms, (cot_blocks, up_blocks) = tie(attn_terms, (cot_blocks, up_blocks))
+        plan = scatter_plan + gather_moves(Z_HOPS, 1, 1, by_z)
+        for number, hop in enumerate([SELF] + PLANE_HOPS):
+            plan.append(
+                (CORE_HOP, 2 + number, None, 2, lambda me, peer, hop=hop: (me.hop(*hop).dp,), None)
+            )
+        branch_blocks, down_z, up_slice = exchange(
             4,
-            [attn_terms, down_weight],
+            [attn_terms, down_weight] + up_blocks,
             [
                 (others, low),
                 ((z_size,) + down_weight.shape, low),
+                ((2 * PLANE,) + up_weight.shape, low),
             ],
-            scatter_plan + gather_moves(Z_HOPS, 1, 1, by_z),
-        )
+            plan,
+        )
+        for hop in range(PLANE):
+            up_slice = put(up_slice, up_blocks[hop], dp_index ^ (2 * hop))
+        up_slice = up_slice.reshape(-1, up_weight.shape[1])
         down_z = put(down_z, down_weight, z_index)
         branch_attn = plane_sum_of(branch_blocks, attn_terms) + proj_vector
 
@@ -883,42 +1144,54 @@
         normed_two = middle * scale_two
         hidden_two = (normed_two * (1.0 + per_row(4)) + per_row(3)).astype(low)
 
-        hidden_all, down_other = exchange(
+        hidden_blocks, down_other = exchange(
             5,
-            [hidden_two, down_z],
-            [((PLANE, row_count, width), low), (down_z.shape, low)],
-            gather_moves(PLANE_HOPS, 0, 0, by_chip) + [(CORE_HOP, 1, None, 1, None, None)],
-        )
-        hidden_all = put(hidden_all, hidden_two, chip).reshape(rows_all, width)
-        down_slice = both_cores(*core_order(down_z, down_other))
-        grad_branch_ffn = (cot_all * per_row_all(5)).astype(low)
-        grad_gated = dot_t(grad_branch_ffn, down_slice)
-        gate_up = dot(hidden_all, up_slice) + own_columns(up_vector, 2)
-        gate_part = gate_up[:, :part_units]
-        up_part = gate_up[:, part_units:]
-        gated_low = (jax.nn.silu(gate_part) * up_part).astype(low)
-        grad_gate_up = jnp.concatenate(
-            [grad_gated * up_part * silu_slope(gate_part), grad_gated * jax.nn.silu(gate_part)],
-            axis=1,
-        ).astype(low)
-        hidden_two_terms = plane_scatter(dot_t(grad_gate_up, up_slice))
-        down_parts = row_parts(gated_low, grad_branch_ffn)
-        up_parts = outer_grad(hidden_all, grad_gate_up).astype(low).reshape(PLANE, 2, shard, -1)
+            [halves(hidden_two), down_z],
+            [((PLANE - 1, 2, row_count // 2, width), low), (down_z.shape, low)],
+            relayed(0, 0, hop_place, 0) + [(CORE_HOP, 1, None, 1, None, None)],
+        )
+        gate_spans = xor_order(group_spans[:, :, 5 * width :], chip, PLANE)
+        hidden_two_terms, ffn_terms, up_bias_cols, up_parts, down_parts = block_call(
+            ffn_kernel,
+            [
+                hidden_two,
+                hidden_blocks.reshape(others),
+                out_cotangent,
+                jnp.stack(cot_blocks),
+                gate_spans[:, :, None],
+                up_slice,
+                down_z,
+                down_other,
+                own_columns(up_vector, 2)[None],
+            ],
+            [0, 2, 0, 2, 1, 0, 0, 0, 0],
+            [((PLANE, row_count, width), low), ((PLANE, row_count, width), low)],
+            [
+                ((1, 2 * units), full),
+                ((PLANE, 2, shard, 2 * units), low),
+                ((z_size, 2) + down_weight.shape, low),
+            ],
+            [((units, width), low), ((width, 2 * units), full), ((units, width), full)],
+            PLANE,
+            rows_all * width * 18 * units,
+        )
+        hop_scatter = [
+            (hop, 0, lambda me, peer, n=n: (n + 1,), 0, lambda me, peer, n=n: (n,), None)
+            for n, hop in enumerate(PLANE_HOPS)
+        ]
         hidden_two_blocks, down_other, up_other = exchange(
             6,
             [hidden_two_terms, down_parts, up_parts],
             [(others, low), half_of(down_parts), half_of(up_parts)],
-            scatter_plan + core_swap(1, 1, z_size) + core_swap(2, 2, PLANE),
-        )
-        grad_hidden_two = plane_sum_of(hidden_two_blocks, hidden_two_terms)
+            hop_scatter + core_swap(1, 1, z_size) + core_swap(2, 2, PLANE),
+        )
+        grad_hidden_two = block_sum(hidden_two_blocks, hidden_two_terms[0])
         down_mine = sum_cores(down_parts, down_other)
         up_mine = sum_cores(up_parts, up_other)
-        ffn_terms = plane_scatter(dot(gated_low, down_slice))
 
         grad_out = out_cotangent.astype(full)
         own_gbf = (grad_out * per_row(5)).astype(low).astype(full)
         down_bias_grad = jnp.sum(own_gbf, axis=0)
-        up_bias_cols = jnp.sum(grad_gate_up.astype(full), axis=0)
         grad_middle = grad_out + norm_backward(
             grad_hidden_two * (1.0 + per_row(4)), normed_two, scale_two
         )
@@ -927,63 +1200,66 @@
         proj_bias_grad = jnp.sum(grad_branch_attn.astype(full), axis=0)
         grad_branch_all, down_blocks = exchange(
             7,
-            [grad_branch_attn, down_mine],
-            [
-                ((PLANE, row_count, width), low),
+            [halves(grad_branch_attn), down_mine],
+            [
+                ((PLANE, 2, row_count // 2, width), low),
                 ((z_size - 1,) + down_mine.shape[1:], low),
             ],
-            gather_moves(PLANE_HOPS, 0, 0, by_chip) + slotted(Z_HOPS, 1, to_z, 1),
-        )
-        grad_branch_all = put(grad_branch_all, grad_branch_attn, chip).reshape(rows_all, width)
+            relayed(0, 0, chip_place, 0) + slotted(Z_HOPS, 1, to_z, 1),
+        )
+        grad_branch_all = put(
+            grad_branch_all.reshape(PLANE, row_count, width), grad_branch_attn, chip
+        )
         down_grad = z_sum_of(down_blocks, down_mine)
 
         grad_branch_all, (ffn_terms, up_mine) = tie(grad_branch_all, (ffn_terms, up_mine))
-        ffn_terms = xor_order(ffn_terms, chip, PLANE)
-        branch_ffn = ffn_terms[0].astype(full)
-        for hop in range(1, PLANE):
-            branch_ffn = branch_ffn + cross(ffn_terms[hop], hop).astype(full)
-        branch_ffn = branch_ffn + down_vector
-        block_out = (middle + per_row(5) * branch_ffn).astype(low)
-        grad_gate_ffn = grad_out * branch_ffn
-        up_mine = xor_order(up_mine, chip, PLANE)
-        up_moved = jnp.stack([up_mine[0]] + [cross(up_mine[hop], hop) for hop in range(1, PLANE)])
-        up_wide = widen(xor_order(up_moved, chip, PLANE), 2)
-
-        grad_attended = dot_t(grad_branch_all, proj_slice).astype(low).reshape(block_shape)
-        proj_parts = row_parts(attended_low, grad_branch_all)
-        grad_probs = jnp.einsum(
-            "bqhd,bkhd->bhqk", grad_attended, value_low, preferred_element_type=full
-        )
-        row_dot = jnp.sum(probs * grad_probs, axis=-1, keepdims=True)
-        grad_scores = (probs * (grad_probs - row_dot)).astype(low)
-        grad_values = jnp.einsum(
-            "bhqk,bqhd->bkhd", probs_low, grad_attended, preferred_element_type=full
-        )
-        grad_query_rot = score_scale * jnp.einsum(
-            "bhqk,bkhd->bqhd", grad_scores, key_low, preferred_element_type=full
-        )
-        grad_key_rot = score_scale * jnp.einsum(
-            "bhqk,bqhd->bkhd", grad_scores, query_low, preferred_element_type=full
-        )
-        back_query = rotate(grad_query_rot.reshape(head_shape), tables, -1.0)
-        back_key = rotate(grad_key_rot.reshape(head_shape), tables, -1.0)
-        gain_q_grad = jnp.sum(back_query * query_unit, axis=(0, 1))
-        gain_k_grad = jnp.sum(back_key * key_unit, axis=(0, 1))
-        grad_query_raw = norm_backward(back_query * gain_q, query_unit, query_scale)
-        grad_key_raw = norm_backward(back_key * gain_k, key_unit, key_scale)
-        grad_qkv = jnp.concatenate(
-            [
-                grad_query_raw.reshape(rows_all, part_cols),
-                grad_key_raw.reshape(rows_all, part_cols),
-                grad_values.reshape(rows_all, part_cols),
+        ffn_blocks = [cross(ffn_terms[hop], hop) for hop in range(1, PLANE)]
+        up_moved = [cross(own_of(up_mine, chip ^ hop), hop) for hop in range(1, PLANE)]
+
+        hidden_one_terms, qkv_bias_cols, gain_grads, qkv_parts, proj_parts = block_call(
+            functools.partial(attention_backward_kernel, head_size, heads),
+            [
+                grad_branch_all,
+                qkv_rows,
+                qkv_slice,
+                gains,
+                cos_rows,
+                sin_rows,
+                meta_rows,
+                seg_col,
+                proj_slice,
+                hidden_one,
+                attended_low,
             ],
-            axis=1,
-        ).astype(low)
-        qkv_bias_cols = jnp.sum(grad_qkv.astype(full), axis=0)
-        qkv_parts = outer_grad(hidden_one, grad_qkv).astype(low).reshape(PLANE, 2, shard, -1)
-        hidden_one_terms = plane_scatter(dot_t(grad_qkv, qkv_slice))
-        hidden_one_terms, (block_out, grad_gate_ffn, up_wide) = tie(
-            hidden_one_terms, (block_out, grad_gate_ffn, up_wide)
+            [1, 1, 0, 0, 0, 0, 1, 1, 0, 1, 1],
+            [((PLANE, row_count, width), low)],
+            [
+                ((1, 3 * part_cols), full),
+                ((2, LANES), full),
+                ((PLANE, 2, shard, 3 * part_cols), low),
+                ((z_size, 2) + proj_weight.shape, low),
+            ],
+            [((width, 3 * part_cols), full), ((part_cols, width), full)],
+            PLANE,
+            rows_all * width * 18 * part_cols,
+        )
+        gain_q_grad, gain_k_grad = gain_grads[0, :head_size], gain_grads[1, :head_size]
+        hidden_one_terms, (ffn_blocks, up_moved) = tie(hidden_one_terms, (ffn_blocks, up_moved))
+        up_moved = [own_of(up_mine, chip)] + up_moved
+
+        def up_columns(p, t):
+            parts = [v[:, t * units : (t + 1) * units] for v in up_moved]
+            odd, high = ((chip ^ p) & 1) == 1, ((chip ^ p) & 2) == 2
+            return jnp.where(
+                high, jnp.where(odd, parts[3], parts[2]), jnp.where(odd, parts[1], parts[0])
+            )
+
+        up_wide = jnp.stack(
+            [
+                jnp.concatenate([up_columns(p, t), up_columns(p + 1, t)], axis=1)
+                for t in range(2)
+                for p in (0, 2)
+            ]
         )
         up_grad = lax.psum_scatter(up_wide, "fsdp", scatter_dimension=0, tiled=False).astype(full)
         hidden_one_blocks, qkv_other, proj_other = exchange(
@@ -993,6 +1269,11 @@
             scatter_plan + core_swap(1, 1, PLANE) + core_swap(2, 2, z_size),
         )
         grad_hidden_one = plane_sum_of(hidden_one_blocks, hidden_one_terms)
+        branch_ffn = ffn_terms[0].astype(full) + down_vector
+        for block in ffn_blocks:
+            branch_ffn = branch_ffn + block.astype(full)
+        block_out = (middle + per_row(5) * branch_ffn).astype(low)
+        grad_gate_ffn = grad_out * branch_ffn
         qkv_mine = sum_cores(qkv_parts, qkv_other)
         proj_mine = sum_cores(proj_parts, proj_other)
         patch_grad = (
@@ -1048,7 +1329,9 @@
             plan,
         )
         proj_grad = z_sum_of(proj_blocks, proj_mine)
-        qkv_wide = widen(put(qkv_moved, own_of(qkv_mine, chip), chip), 3)
+        qkv_wide = whole_call(
+            functools.partial(merge_kernel, 3), put(qkv_moved, own_of(qkv_mine, chip), chip)
+        )
         grad_mod = grad_mod.reshape(-1, mod_cols)
         vector_sum = jnp.sum(vector_parts, axis=0)
         cond_part = dot_t(grad_mod, mod_weight).reshape(2 * PLANE, z_size, slots, mod_rows)

time: 670 us -> 554 us (0.83)
  local copies, waits for them, and re-layouts: 151 us -> 45.5 us
  Pallas kernels: 276 us -> 376 us
  matrix products: 82.8 us -> 4.61 us
  other arithmetic: 119 us -> 77.9 us
  waiting for transfers between devices: 3.04 us -> 10 us
    pallas_call x0 -> x5, Pallas kernels: none -> 103 us  [the longest x3 97.9 us: block_call(): pl.pallas_call(kernel, grid=(steps,), out_shape=[jax.ShapeDtypeStruct(*o)...]
    concatenate x18 -> x0, local copies, waits for them, and re-layouts: 32.7 us -> none  [the longest x16 26.2 us: rotate(): return jnp.concatenate(pieces_out, axis=-1)]
    dot_general x5 -> x1, matrix products: 24 us -> 1.1 us  [dot_t(): lax.dot_general(left, right, (((1,), (1,)), ((), ())), preferred_element_...]
    dot_general x11 -> x1, matrix products: 24.1 us -> 2.26 us  [outer_grad(): lax.dot_general(left, right, (((0,), (0,)), ((), ())), preferred_element_...]
    unnamed x275 -> x125, local copies, waits for them, and re-layouts: 23.7 us -> 6.6 us
    dot_general x5 -> x1, matrix products: 17.6 us -> 1.25 us  [dot(): return jnp.dot(left, right, preferred_element_type=full)]
    slice x12 -> x2, local copies, waits for them, and re-layouts: 15.6 us -> 0.79 us  [the longest x1 0.77 us: per_device(): gain_grads[1, :head_size]]
    dot_general x5 -> x0, matrix products: 11.2 us -> none  [the longest x1 4.11 us: per_device(): jnp.einsum('bhqk,bqhd->bkhd', probs_low, grad_attended, preferred_element...]
  transfers between devices with their start and end apart: 15 -> 14, of which waited for: 2 -> 3; matrix products, arithmetic and copies ran while one was open for 32% -> 15% of each run, Pallas kernels for 18% -> 36%
where the time goes in v3:
time: 554 us; the launch traced here: 544 us
  Pallas kernels  376 us (68%)
  other arithmetic  77.9 us (14%)
  local copies, waits for them, and re-layouts  45.5 us (8%)
  between operations  15.4 us (3%)
  starting transfers between devices  14.1 us (3%)
  waiting for transfers between devices  10 us (2%)
    pallas_call x10, Pallas kernels, exchange(): pl.pallas_call(kernel, out_shape=[jax.ShapeDtypeStruct(shape, dtype) for...  273 us
    pallas_call x3, Pallas kernels, block_call(): pl.pallas_call(kernel, grid=(steps,), out_shape=[jax.ShapeDtypeStruct(*o)...  97.9 us
    ppermute x12, starting transfers between devices, cross(): lax.ppermute(values, 'dp', [(k, k ^ 2 * hop) for k in range(2 * PLANE)])  14 us
    dynamic_update_slice x12, local copies, waits for them, and re-layouts, put(): lax.dynamic_update_slice(values, own.reshape((1,) * len(at) + own.shape),...  12.1 us
  transfers between devices with their start and end apart: 14, of which 3 were waited for; matrix products, arithmetic and copies ran while one was open for 15% of the time, Pallas kernels for 36%

profile of v3, /device:TPU:0, one launch (start us, length us, event | category | flops | bytes accessed | tf_op | source)
XLA Modules:
  0.0 543.7 jit_solution(2477296745109978600)
XLA Ops:
  8.0 2.8 concatenate.36
  11.4 1.3 fusion.38.refs_0_
  12.7 1.3 pad_add_fusion.refs_5_
  14.0 41.7 %shard_map.281 = (bf16[8,4,4,1152]{3,2,1,0:T(4,128)(2,1)}, bf16[4,144,864]{2,1,0:T(8,128)(2,1)}, bf16[4,2,128,1152]{3,2,1,0:T(8,128)(2,1)}, bf16[4,144,288]{2,1,...) custom-call(bf16[4,1152]{1,0:T(4,128)(2,1)} %fusion.38.refs_0_, bf16[144,864]{1,0:T(8,128)(2,1)} %refs_1_.2, ...), custom_call_target="tpu_custom_call" | custom-call | tf_op jit(solution)/shard_map/pallas_call | solution.py:512
  56.9 1.3 fusion.52
  58.2 1.8 copy.131
  61.0 2.5 shard_map.282.refs_0_
  64.2 1.3 fusion.33
  65.4 24.8 %shard_map.283 = (bf16[8,144,864]{2,1,0:T(8,128)(2,1)}, f32[8,16,1728]{2,1,0:T(8,128)}, bf16[4,144,288]{2,1,0:T(8,128)(2,1)}) custom-call(bf16[4,144,864]{2,1,0:T(8,128)(2,1)} %shard_map.282.refs_0_, f32[8,16,1728]{2,1,0:T(8,128)} %bitcast.226, bf16[4,144,288]{2,1,0:T(8,128)(2,1)} %bitcast_dynamic-update-slice_fusion.8.refs_2_.refs_10_), custom_call_target="tpu_custom_call" | custom-call | tf_op jit(solution)/shard_map/pallas_call | solution.py:512
  90.3 1.6 dynamic-slice_dynamic-update-slice_fusion.2
  93.8 14.3 %shard_map.284 = f32[4,4,4,1728]{3,2,1,0:T(4,128)} custom-call(f32[4,4,1728]{2,1,0:T(4,128)} %broadcast_add_fusion.refs_0_), custom_call_target="tpu_custom_call" | custom-call | tf_op jit(solution)/shard_map/pallas_call | solution.py:512
  114.4 1.7 dynamic-slice_dynamic-update-slice_fusion.1
  119.2 1.5 collective-permute-start.1
  121.7 2.3 dynamic-slice_bitcast_fusion.5
  124.8 1.9 collective-permute-start.5
  131.0 24.2 %shard_map.285 = (bf16[4,256,1152]{2,1,0:T(8,128)(2,1)}, f32[4,256,864]{2,1,0:T(8,128)}, bf16[4,256,288]{2,1,0:T(8,128)(2,1)}, bf16[4,256,1152]{2,1,0:T(8,128)(2,1)}, bf16[288,1152]{1,0:T(8,128)(2,1)}) custom-call(bf16[4,256,1152]{2,1,0:T(8,128)(2,1)} %bitcast_dynamic-update-slice_fusion.1.refs_0_, f32[4,4,1,1152]{3,2,1,0:T(1,128)} %broadcast_in_dim.21.refs_1_, ...), custom_call_target="tpu_custom_call" | custom-call | flops 2717908992 | bytes 5214592 | tf_op jit(solution)/shard_map/pallas_call | solution.py:843
  157.7 7.3 %collective-permute-done.4.refs_4_ = bf16[144,1536]{1,0:T(8,128)(2,1)S(1)} collective-permute-done((bf16[144,1536]{1,0:T(8,128)(2,1)}, bf16[144,1536]{1,0:T(8,128)(2,1)S(1)}, u32[]{:S(2)}, u32[]{:S(2)}) %collective-permute-start.4) | collective-permute-done | bytes 442400 | tf_op jit(solution)/shard_map/ppermute | solution.py:384
  166.7 28.6 %shard_map.286 = (bf16[3,256,1152]{2,1,0:T(8,128)(2,1)}, bf16[4,384,288]{2,1,0:T(8,128)(2,1)}, bf16[8,144,1536]{2,1,0:T(8,128)(2,1)}) custom-call(bf16[4,256,1152]{2,1,0:T(8,128)(2,1)} %get-tuple-element.96.refs_0_, bf16[384,288]{1,0:T(8,128)(2,1)} %copy.132.refs_1_, bf16[144,1536]{1,0:T(8,128)(2,1)} %pad_maximum_fusion.2.refs_2_, ...), custom_call_target="tpu_custom_call" | custom-call | tf_op jit(solution)/shard_map/pallas_call | solution.py:512
  196.1 1.9 convert_reduce_fusion.2
  198.1 2.5 multiply_reduce_fusion.2
  204.9 22.2 %shard_map.287 = (bf16[3,2,128,1152]{3,2,1,0:T(8,128)(2,1)}, bf16[4,384,288]{2,1,0:T(8,128)(2,1)}) custom-call(bf16[2,128,1152]{2,1,0:T(8,128)(2,1)} %bitcast.228, bf16[4,384,288]{2,1,0:T(8,128)(2,1)} %bitcast_dynamic-update-slice_fusion.6.refs_1_.refs_6_), custom_call_target="tpu_custom_call" | custom-call | tf_op jit(solution)/shard_map/pallas_call | solution.py:512
  227.2 2.9 pad_maximum_fusion.refs_3_
  230.0 29.2 %shard_map.288 = (bf16[4,256,1152]{2,1,0:T(8,128)(2,1)}, bf16[4,256,1152]{2,1,0:T(8,128)(2,1)}, f32[1,1536]{1,0:T(1,128)}, bf16[4,2,144,1536]{3,2,1,0:T(8,128)(2,1)}, bf16[4,2,384,288]{3,2,1,0:T(8,128)(2,1)}) custom-call(bf16[256,1152]{1,0:T(8,128)(2,1)} %fusion.18.refs_0_, bf16[3,256,1152]{2,1,0:T(8,128)(2,1)} %bitcast.256, bf16[256,1152]{1,0:T(8,128)(2,1)} %refs_2_.1, ...), custom_call_target="tpu_custom_call" | custom-call | flops 16307453952 | bytes 10106880 | tf_op jit(solution)/shard_map/pallas_call | solution.py:843
  259.2 2.2 slice_convert_fusion
  261.3 28.6 %shard_map.289 = (bf16[3,256,1152]{2,1,0:T(8,128)(2,1)}, bf16[4,384,288]{2,1,0:T(8,128)(2,1)}, bf16[4,144,1536]{2,1,0:T(8,128)(2,1)}) custom-call(bf16[4,256,1152]{2,1,0:T(8,128)(2,1)} %get-tuple-element.109.refs_0_, bf16[4,2,384,288]{3,2,1,0:T(8,128)(2,1)} %get-tuple-element.110.refs_1_, bf16[4,2,144,1536]{3,2,1,0:T(8,128)(2,1)} %get-tuple-element.111.refs_2_), custom_call_target="tpu_custom_call" | custom-call | tf_op jit(solution)/shard_map/pallas_call | solution.py:512
  290.0 2.0 convert_reduce_fusion.1
  292.6 1.4 copy-done.6
  293.9 1.5 fusion.1.refs_1_
  295.4 2.5 convert_reduce_fusion.6
  297.9 30.4 %shard_map.290 = (bf16[4,2,128,1152]{3,2,1,0:T(8,128)(2,1)}, bf16[3,384,288]{2,1,0:T(8,128)(2,1)}) custom-call(bf16[2,128,1152]{2,1,0:T(8,128)(2,1)} %bitcast.223, bf16[4,384,288]{2,1,0:T(8,128)(2,1)} %fusion.1.refs_1_), custom_call_target="tpu_custom_call" | custom-call | tf_op jit(solution)/shard_map/pallas_call | solution.py:512
  328.3 1.4 convert_reduce_fusion.3
  329.6 1.9 convert_add_fusion.8
  331.5 2.0 copy.149
  333.5 3.4 fusion
  337.8 1.3 slice_bitcast_fusion
  339.1 1.4 collective-permute-start.6
  341.2 1.4 collective-permute-start.8
  342.6 1.3 dynamic-slice_bitcast_fusion
  343.9 1.4 collective-permute-start.10
  345.3 1.4 collective-permute-start.11
  346.7 44.6 %shard_map.291 = (bf16[4,256,1152]{2,1,0:T(8,128)(2,1)}, f32[1,864]{1,0:T(1,128)}, f32[2,128]{1,0:T(2,128)}, bf16[4,2,144,864]{3,2,1,0:T(8,128)(2,1)}, bf16[4,2,144,288]{3,2,1,0:T(8,128)(2,1)}) custom-call(bf16[4,256,1152]{2,1,0:T(8,128)(2,1)} %bitcast_dynamic-update-slice_fusion.refs_0_, f32[4,256,864]{2,1,0:T(8,128)} %get-tuple-element.119.refs_1_, ...), custom_call_target="tpu_custom_call" | custom-call | flops 6115295232 | bytes 11551744 | tf_op jit(solution)/shard_map/pallas_call | solution.py:843
  399.2 2.7 bitcast_reduce_fusion.1
  402.0 2.0 bitcast_reduce_fusion.2
  404.7 1.7 collective-permute-done.9
  407.7 1.5 select_select_fusion.4
  410.6 1.5 pad_maximum_fusion.1
  412.1 2.2 dynamic-slice_convert_fusion
  414.2 28.7 %shard_map.292 = (bf16[3,256,1152]{2,1,0:T(8,128)(2,1)}, bf16[4,144,864]{2,1,0:T(8,128)(2,1)}, bf16[4,144,288]{2,1,0:T(8,128)(2,1)}) custom-call(bf16[4,256,1152]{2,1,0:T(8,128)(2,1)} %get-tuple-element.128.refs_0_, bf16[4,2,144,864]{3,2,1,0:T(8,128)(2,1)} %get-tuple-element.129.refs_1_, bf16[4,2,144,288]{3,2,1,0:T(8,128)(2,1)} %get-tuple-element.130.refs_2_), custom_call_target="tpu_custom_call" | custom-call | tf_op jit(solution)/shard_map/pallas_call | solution.py:512
  442.9 2.0 convert_reduce_fusion
  445.0 1.7 bitcast_reduce_fusion.3
  446.9 1.9 bitcast_reduce_fusion
  449.0 2.7 fusion.15
  452.5 2.2 fusion.25.refs_3_
  454.7 2.9 fusion.2.refs_0_
  457.6 20.8 %shard_map.293 = (bf16[4,144,864]{2,1,0:T(8,128)(2,1)}, bf16[8,4,4,1728]{3,2,1,0:T(4,128)(2,1)}, f32[4,1,3012]{2,1,0:T(1,128)}, bf16[3,144,288]{2,1,0:T(8,128)(2,1)}) custom-call(bf16[4,144,864]{2,1,0:T(8,128)(2,1)} %fusion.2.refs_0_, bf16[4,4,1728]{2,1,0:T(4,128)(2,1)} %bitcast.233, f32[4,1,3012]{2,1,0:T(1,128)} %concatenate.43.refs_2_, ...), custom_call_target="tpu_custom_call" | custom-call | tf_op jit(solution)/shard_map/pallas_call | solution.py:512
  478.5 1.7 dynamic-slice_dynamic-update-slice_fusion.source
  480.2 2.5 shard_map.294.refs_0_
  485.4 33.1 %shard_map.295 = (bf16[3,144,864]{2,1,0:T(8,128)(2,1)}, f32[8,4,4,144]{3,2,1,0:T(4,128)}, f32[8,1,3012]{2,1,0:T(1,128)}) custom-call(bf16[4,144,864]{2,1,0:T(8,128)(2,1)} %shard_map.294.refs_0_, f32[8,4,4,144]{3,2,1,0:T(4,128)} %fusion.27.refs_1_, f32[1,3012]{1,0:T(1,128)} %bitcast.244), custom_call_target="tpu_custom_call" | custom-call | tf_op jit(solution)/shard_map/pallas_call | solution.py:512
  520.5 1.6 fusion.7
  522.1 2.4 fusion.11
  528.0 1.7 convert_add_fusion.10
  529.7 1.8 convert_add_fusion.9
  531.5 2.3 fusion.31
  534.4 2.0 bitcast_convert_fusion
  (247 shorter events, 54.1 us)
Async XLA Ops:
  7.2 57.0 %copy-start = (bf16[144,1728]{1,0:T(8,128)(2,1)S(1)}, bf16[144,1728]{1,0:T(8,128)(2,1)}, u32[]{:S(2)}) copy-start(bf16[144,1728]{1,0:T(8,128)(2,1)} %param.22) | copy-start | bytes 1492996
  7.2 52.8 %copy-start.57 = (s32[256]{0:T(256)S(1)}, s32[256]{0:T(256)}, u32[]{:S(2)}) copy-start(s32[256]{0:T(256)} %param.20) | copy-start | bytes 3076
  7.2 111.0 %all-gather.3.cloned.1.call-start = ((), (), s32[]{:S(2)}) async-start(), calls=%async_computation.2 | async-start | bytes 2211840 | tf_op jit(solution)/shard_map/all_gather | solution.py:931
  55.8 4.3 copy-start.34
  55.8 4.4 copy-start.28
  55.8 478.5 %reduce-scatter.2.cloned.1.call-start = ((), (), s32[]{:S(2)}) async-start(), calls=%async_computation.1 | async-start | bytes 2211840 | tf_op jit(solution)/shard_map/reduce_scatter | solution.py:1264
  60.2 3.9 copy-start.31
  60.2 3.2 copy-start.32
  90.3 2.8 copy-start.56
  93.8 17.1 %copy-start.36 = (bf16[384,288]{0,1:T(8,128)(2,1)S(1)}, bf16[384,288]{0,1:T(8,128)(2,1)}, u32[]{:S(2)}) copy-start(bf16[384,288]{0,1:T(8,128)(2,1)} %param.31) | copy-start | bytes 663556
  109.7 7.6 %copy-start.1 = (bf16[256,1152]{1,0:T(8,128)(2,1)S(1)}, bf16[256,1152]{1,0:T(8,128)(2,1)}, u32[]{:S(2)}) copy-start(bf16[256,1152]{1,0:T(8,128)(2,1)} %param.18) | copy-start | bytes 1769476
  113.8 4.3 copy-start.15
  116.2 4.5 copy-start.51
  118.2 47.8 %collective-permute-start = (bf16[256,1152]{1,0:T(8,128)(2,1)S(1)}, bf16[256,1152]{1,0:T(8,128)(2,1)}, u32[]{:S(2)}, u32[]{:S(2)}) collective-permute-start(bf16[256,1152]{1,0:T(8,128)(2,1)S(1)} %copy-done.15), channel_id=1, source_target_pairs={{0,8},{4,12},{8,0},{12,4},{16,24},{20,28},{24,16},{28,20},{1,9},{5... | collective-permute-start | bytes 1769480 | tf_op jit(solution)/shard_map/ppermute | solution.py:384
  119.2 46.7 %collective-permute-start.1 = (bf16[256,1152]{1,0:T(8,128)(2,1)S(1)}, bf16[256,1152]{1,0:T(8,128)(2,1)}, u32[]{:S(2)}, u32[]{:S(2)}) collective-permute-start(bf16[256,1152]{1,0:T(8,128)(2,1)S(1)} %copy-done.15), channel_id=1, source_target_pairs={{0,16},{4,20},{8,24},{12,28},{16,0},{20,4},{24,8},{28,12},{1,17},{... | collective-permute-start | bytes 1769480 | tf_op jit(solution)/shard_map/ppermute | solution.py:384
  120.7 45.2 %collective-permute-start.2 = (bf16[256,1152]{1,0:T(8,128)(2,1)S(1)}, bf16[256,1152]{1,0:T(8,128)(2,1)}, u32[]{:S(2)}, u32[]{:S(2)}) collective-permute-start(bf16[256,1152]{1,0:T(8,128)(2,1)S(1)} %copy-done.15), channel_id=1, source_target_pairs={{0,24},{4,28},{8,16},{12,20},{16,8},{20,12},{24,0},{28,4},{1,25},{... | collective-permute-start | bytes 1769480 | tf_op jit(solution)/shard_map/ppermute | solution.py:384
  124.8 31.2 %collective-permute-start.5 = (bf16[144,1536]{1,0:T(8,128)(2,1)}, bf16[144,1536]{1,0:T(8,128)(2,1)S(1)}, u32[]{:S(2)}, u32[]{:S(2)}) collective-permute-start(bf16[144,1536]{1,0:T(8,128)(2,1)} %pad_maximum_fusion.5), channel_id=1, source_target_pairs={{0,24},{4,28},{8,16},{12,20},{16,8},{20,12},{24,0},{28,4},{1,25},{... | collective-permute-start | bytes 1327112 | tf_op jit(solution)/shard_map/ppermute | solution.py:384
  127.6 37.4 %collective-permute-start.4 = (bf16[144,1536]{1,0:T(8,128)(2,1)}, bf16[144,1536]{1,0:T(8,128)(2,1)S(1)}, u32[]{:S(2)}, u32[]{:S(2)}) collective-permute-start(bf16[144,1536]{1,0:T(8,128)(2,1)} %pad_maximum_fusion.4), channel_id=1, source_target_pairs={{0,16},{4,20},{8,24},{12,28},{16,0},{20,4},{24,8},{28,12},{1,17},{... | collective-permute-start | bytes 1327112 | tf_op jit(solution)/shard_map/ppermute | solution.py:384
  156.0 10.7 %copy-start.21 = (bf16[144,1536]{1,0:T(8,128)(2,1)}, bf16[144,1536]{1,0:T(8,128)(2,1)S(1)}, u32[]{:S(2)}) copy-start(bf16[144,1536]{1,0:T(8,128)(2,1)S(1)} %collective-permute-done.5.refs_5_) | copy-start | bytes 1327108
  156.0 9.9 %collective-permute-start.3 = (bf16[144,1536]{1,0:T(8,128)(2,1)S(1)}, bf16[144,1536]{1,0:T(8,128)(2,1)S(1)}, u32[]{:S(2)}, u32[]{:S(2)}) collective-permute-start(bf16[144,1536]{1,0:T(8,128)(2,1)S(1)} %pad_maximum_fusion.3), channel_id=1, source_target_pairs={{0,8},{4,12},{8,0},{12,4},{16,24},{20,28},{24,16},{28,20},{1,9},{5... | collective-permute-start | bytes 1327112 | tf_op jit(solution)/shard_map/ppermute | solution.py:384
  166.7 28.6 %copy-start.10 = (bf16[144,1536]{1,0:T(8,128)(2,1)S(1)}, bf16[144,1536]{1,0:T(8,128)(2,1)}, u32[]{:S(2)}) copy-start(bf16[144,1536]{1,0:T(8,128)(2,1)} %pad_maximum_fusion.2.refs_2_) | copy-start | bytes 1327108
  196.1 1.9 copy-start.39
  196.1 1.9 copy-start.40
  198.0 2.6 copy-start.4
  198.1 2.6 copy-start.14
  198.1 3.3 copy-start.26
  200.6 2.5 copy-start.22
  201.4 2.5 copy-start.35
  201.4 2.5 copy-start.41
  290.0 2.2 copy-start.7
  290.0 2.6 copy-start.27
  333.5 3.4 copy-start.8
  333.5 4.3 copy-start.12
  339.1 67.3 %collective-permute-start.6 = (bf16[256,1152]{1,0:T(8,128)(2,1)}, bf16[256,1152]{1,0:T(8,128)(2,1)}, u32[]{:S(2)}, u32[]{:S(2)}) collective-permute-start(bf16[256,1152]{1,0:T(8,128)(2,1)} %get-tuple-element.233), channel_id=1, source_target_pairs={{0,8},{4,12},{8,0},{12,4},{16,24},{20,28},{24,16},{28,20},{1,9},{5... | collective-permute-start | bytes 1769480 | tf_op jit(solution)/shard_map/ppermute | solution.py:384
  340.5 65.9 %collective-permute-start.7 = (bf16[256,1152]{1,0:T(8,128)(2,1)}, bf16[256,1152]{1,0:T(8,128)(2,1)}, u32[]{:S(2)}, u32[]{:S(2)}) collective-permute-start(bf16[256,1152]{1,0:T(8,128)(2,1)} %get-tuple-element.232), channel_id=1, source_target_pairs={{0,16},{4,20},{8,24},{12,28},{16,0},{20,4},{24,8},{28,12},{1,17},{... | collective-permute-start | bytes 1769480 | tf_op jit(solution)/shard_map/ppermute | solution.py:384
  341.2 65.3 %collective-permute-start.8 = (bf16[256,1152]{1,0:T(8,128)(2,1)}, bf16[256,1152]{1,0:T(8,128)(2,1)}, u32[]{:S(2)}, u32[]{:S(2)}) collective-permute-start(bf16[256,1152]{1,0:T(8,128)(2,1)} %get-tuple-element.231), channel_id=1, source_target_pairs={{0,24},{4,28},{8,16},{12,20},{16,8},{20,12},{24,0},{28,4},{1,25},{... | collective-permute-start | bytes 1769480 | tf_op jit(solution)/shard_map/ppermute | solution.py:384
  343.9 53.9 %collective-permute-start.10 = (bf16[144,1536]{1,0:T(8,128)(2,1)}, bf16[144,1536]{1,0:T(8,128)(2,1)}, u32[]{:S(2)}, u32[]{:S(2)}) collective-permute-start(bf16[144,1536]{1,0:T(8,128)(2,1)} %get-tuple-element.244), channel_id=1, source_target_pairs={{0,16},{4,20},{8,24},{12,28},{16,0},{20,4},{24,8},{28,12},{1,17},{... | collective-permute-start | bytes 1327112 | tf_op jit(solution)/shard_map/ppermute | solution.py:384
  345.3 59.4 %collective-permute-start.11 = (bf16[144,1536]{1,0:T(8,128)(2,1)}, bf16[144,1536]{1,0:T(8,128)(2,1)}, u32[]{:S(2)}, u32[]{:S(2)}) collective-permute-start(bf16[144,1536]{1,0:T(8,128)(2,1)} %get-tuple-element.243), channel_id=1, source_target_pairs={{0,24},{4,28},{8,16},{12,20},{16,8},{20,12},{24,0},{28,4},{1,25},{... | collective-permute-start | bytes 1327112 | tf_op jit(solution)/shard_map/ppermute | solution.py:384
  346.7 48.9 %copy-start.48 = (f32[1152]{0:T(1024)S(1)}, f32[1152]{0:T(1024)}, u32[]{:S(2)}) copy-start(f32[1152]{0:T(1024)} %get-tuple-element.226) | copy-start | bytes 13828
  397.7 8.7 %collective-permute-start.9 = (bf16[144,1536]{1,0:T(8,128)(2,1)}, bf16[144,1536]{1,0:T(8,128)(2,1)}, u32[]{:S(2)}, u32[]{:S(2)}) collective-permute-start(bf16[144,1536]{1,0:T(8,128)(2,1)} %get-tuple-element.245), channel_id=1, source_target_pairs={{0,8},{4,12},{8,0},{12,4},{16,24},{20,28},{24,16},{28,20},{1,9},{5... | collective-permute-start | bytes 1327112 | tf_op jit(solution)/shard_map/ppermute | solution.py:384
  399.2 2.7 copy-start.2
  399.2 2.7 copy-start.5
  401.9 2.0 copy-start.45
  401.9 2.0 copy-start.49
  401.9 2.0 copy-start.50
  401.9 2.0 copy-start.53
  401.9 2.0 copy-start.54
  401.9 2.8 copy-start.55
  401.9 4.5 copy-start.11
  442.9 2.0 copy-start.9
  444.9 1.8 copy-start.43
  444.9 1.8 copy-start.42
  444.9 1.9 copy-start.13
  445.0 2.0 copy-start.17
  446.9 1.9 copy-start.52
  451.7 3.0 copy-start.29
  478.5 4.2 copy-start.46
  480.2 3.1 copy-start.18
  485.4 35.1 %copy-start.38 = (f32[4,1152]{1,0:T(4,128)S(1)}, f32[4,1152]{1,0:T(4,128)}, u32[]{:S(2)}) copy-start(f32[4,1152]{1,0:T(4,128)} %get-tuple-element.259) | copy-start | bytes 55300
  522.1 5.0 copy-start.33
  522.1 5.0 copy-start.19
  524.5 3.4 copy-start.30
  528.0 3.5 copy-start.20
  529.7 4.1 copy-start.47
  (8 other events, 12.2 us)
Sparse Core Ops, SparseCore 0:
  56.0 38.8 all-gather.2
  412.2 39.4 reduce-scatter.1

commit v4 on v3

--- a/solution.py
+++ b/solution.py
@@ -449,64 +449,79 @@
 GROUP_HOPS = [(dy, dx, 0, dz) for dz in range(4) for dy in (0, 1) for dx in (0, 1)]
 
 
+class Copies:
+    def __init__(self, plan, ins, outs, send, recv):
+        self.plan, self.ins, self.outs, self.send, self.recv = plan, ins, outs, send, recv
+
+    def here(self):
+        dp_index = lax.axis_index("dp")
+        return Place(dp_index // 4, (dp_index // 2) % 2, dp_index % 2, lax.axis_index("fsdp"))
+
+    def greet(self):
+        hops = []
+        for move in self.plan:
+            if move[0] != SELF and move[0] not in hops:
+                hops.append(move[0])
+        barrier = pltpu.get_barrier_semaphore()
+        for hop in hops:
+            peer = self.here().hop(*hop)
+            pl.semaphore_signal(
+                barrier,
+                1,
+                device_id={"dp": peer.dp, "fsdp": peer.z},
+                device_id_type=pl.DeviceIdType.MESH,
+            )
+        pl.semaphore_wait(barrier, len(hops))
+
+    def copy(self, number):
+        hop, source, source_at, out, out_at, after = self.plan[number]
+        me = self.here()
+        peer = me.hop(*hop)
+        src = (self.ins if after is None else self.outs)[source]
+        src = src if source_at is None else src.at[source_at(me, peer)]
+        dst = self.outs[out]
+        dst = dst if out_at is None else dst.at[out_at(me, peer)]
+        if hop == SELF:
+            return pltpu.make_async_copy(src, dst, self.send.at[number])
+        return pltpu.make_async_remote_copy(
+            src_ref=src,
+            dst_ref=dst,
+            send_sem=self.send.at[number],
+            recv_sem=self.recv.at[number],
+            device_id={"dp": peer.dp, "fsdp": peer.z},
+            device_id_type=pl.DeviceIdType.MESH,
+        )
+
+    def start(self, number):
+        self.copy(number).start()
+
+    def wait_arrival(self, number):
+        if self.plan[number][0] == SELF:
+            self.copy(number).wait()
+        else:
+            self.copy(number).wait_recv()
+
+    def finish(self, arrived=()):
+        for number, move in enumerate(self.plan):
+            if number not in arrived:
+                self.wait_arrival(number)
+            if move[0] != SELF:
+                self.copy(number).wait_send()
+
+
 def exchange(identity, inputs, out_shapes, plan):
-    hops = []
-    for move in plan:
-        if move[0] != SELF and move[0] not in hops:
-            hops.append(move[0])
-
     def kernel(*refs):
         ins, outs = refs[: len(inputs)], refs[len(inputs) : len(inputs) + len(out_shapes)]
-        send, recv = refs[-2:]
-        dp_index = lax.axis_index("dp")
-        me = Place(dp_index // 4, (dp_index // 2) % 2, dp_index % 2, lax.axis_index("fsdp"))
-
-        def target(hop):
-            peer = me.hop(*hop)
-            return peer, {"dp": peer.dp, "fsdp": peer.z}
-
-        barrier = pltpu.get_barrier_semaphore()
-        for hop in hops:
-            pl.semaphore_signal(
-                barrier, 1, device_id=target(hop)[1], device_id_type=pl.DeviceIdType.MESH
-            )
-        pl.semaphore_wait(barrier, len(hops))
-        copies = []
-        forwarded = set()
-        for number, (hop, source, source_at, out, out_at, after) in enumerate(plan):
-            peer, device = target(hop)
-            src = (ins if after is None else outs)[source]
-            src = src if source_at is None else src.at[source_at(me, peer)]
-            dst = outs[out]
-            dst = dst if out_at is None else dst.at[out_at(me, peer)]
-            for earlier in after or ():
-                if earlier not in forwarded:
-                    if plan[earlier][0] == SELF:
-                        copies[earlier].wait()
-                    else:
-                        copies[earlier].wait_recv()
-                    forwarded.add(earlier)
-            if hop == SELF:
-                copy = pltpu.make_async_copy(src, dst, send.at[number])
-            else:
-                copy = pltpu.make_async_remote_copy(
-                    src_ref=src,
-                    dst_ref=dst,
-                    send_sem=send.at[number],
-                    recv_sem=recv.at[number],
-                    device_id=device,
-                    device_id_type=pl.DeviceIdType.MESH,
-                )
-            copy.start()
-            copies.append(copy)
-        for number, copy in enumerate(copies):
-            if plan[number][0] == SELF:
-                if number not in forwarded:
-                    copy.wait()
-                continue
-            copy.wait_send()
-            if number not in forwarded:
-                copy.wait_recv()
+        copies = Copies(plan, ins, outs, *refs[-2:])
+        copies.greet()
+        done = set()
+        for number, move in enumerate(plan):
+            for earlier in move[5] or ():
+                if earlier not in done:
+                    copies.wait_arrival(earlier)
+                    done.add(earlier)
+            copies.start(number)
+        copies.finish(done)
 
     anywhere = pl.BlockSpec(memory_space=pl.ANY)
     return pl.pallas_call(
@@ -674,13 +689,16 @@
         )
 
 
-def attention_forward_kernel(head_size, heads, *refs):
+def attention_forward_kernel(head_size, heads, copies, rest, *refs):
     (patch, shift, scale, weight, bias, gains, cos_rows, sin_rows, meta, seg_col) = refs[:10]
     proj_mine, proj_other = refs[10:12]
     hidden_out, rows_out, attended_out, terms_out, proj = refs[12:]
 
     @pl.when(pl.program_id(0) == 0)
     def _():
+        copies.greet()
+        for number in range(len(copies.plan)):
+            copies.start(number)
         fill_rows(proj, proj_mine, proj_other)
 
     cosine, sine = rotary_of(meta[0], cos_rows[...], sin_rows[...])
@@ -700,6 +718,10 @@
     attended_out[0] = attended
     terms_out[0] = dot(attended, proj[...]).astype(low)
 
+    @pl.when(pl.program_id(0) == pl.num_programs(0) - 1)
+    def _():
+        copies.finish()
+
 
 def cut_columns(parts, total):
     cols = parts.shape[3]
@@ -707,7 +729,7 @@
         parts[j] = total[:, j * cols : (j + 1) * cols].astype(low).reshape(parts.shape[1:])
 
 
-def attention_backward_kernel(head_size, heads, *refs):
+def attention_backward_kernel(head_size, heads, copies, rest, *refs):
     (grad, rows, weight, gains, cos_rows, sin_rows, meta, seg_col, proj) = refs[:9]
     hidden, attended = refs[9:11]
     terms_out, bias_out, gains_out, qkv_parts, proj_parts = refs[11:16]
@@ -719,6 +741,9 @@
         gains_out[...] = jnp.zeros_like(gains_out)
         qkv_total[...] = jnp.zeros_like(qkv_total)
         proj_total[...] = jnp.zeros_like(proj_total)
+        copies.greet()
+        for number in range(len(copies.plan)):
+            copies.start(number)
 
     score_scale = head_size ** (-0.5)
     gain_values = gains[...]
@@ -761,12 +786,15 @@
     def _():
         qkv_parts[...] = qkv_total[...].astype(low).reshape(qkv_parts.shape)
         cut_columns(proj_parts, proj_total[...])
-
-
-def ffn_kernel(*refs):
-    (own_hidden, hiddens, own_cot, cots, gate, up, down_mine, down_other, bias) = refs[:9]
-    hidden_terms, ffn_terms, bias_out, up_parts, down_parts = refs[9:14]
-    down, up_total, down_total = refs[14:]
+        copies.finish()
+
+
+def ffn_kernel(copies, rest, *refs):
+    (own_hidden, hiddens, own_cot, cots, gate, up_mine, up_other) = refs[:7]
+    (down_mine, down_other, bias) = refs[7:10]
+    ffn_terms, hidden_terms, bias_out, up_parts, down_parts = refs[10:15]
+    down, up, up_total, down_total, terms = refs[15:]
+    copies.ins = [terms]
     step = pl.program_id(0)
 
     @pl.when(step == 0)
@@ -774,12 +802,20 @@
         bias_out[...] = jnp.zeros_like(bias_out)
         up_total[...] = jnp.zeros_like(up_total)
         down_total[...] = jnp.zeros_like(down_total)
+        copies.greet()
         fill_rows(down, down_mine, down_other)
+        rows = up_mine.shape[1]
+        core = lax.axis_index("dp") % 2
+        for source, place in ((up_mine, core), (up_other, 1 - core)):
+            for p in range(source.shape[0]):
+                at = pl.multiple_of((2 * p + place) * rows, 16)
+                up[pl.ds(at, rows), :] = source[p]
 
     count, width = own_hidden.shape
+    last = pl.num_programs(0) - 1
     units = down.shape[0]
-    hidden = jnp.where(step == 0, own_hidden[...], hiddens[0])
-    cot = jnp.where(step == 0, own_cot[...], cots[0])
+    hidden = jnp.where(step == last, own_hidden[...], hiddens[0])
+    cot = jnp.where(step == last, own_cot[...], cots[0])
     grad_branch = cot.astype(full).reshape(count // SPAN, SPAN, width) * gate[0]
     grad_branch = grad_branch.reshape(count, width).astype(low)
     grad_gated = dot_t(grad_branch, down[...])
@@ -793,7 +829,22 @@
     grad_up = (grad_gated * silu).astype(low)
     grads = jnp.concatenate([grad_gate, grad_up], axis=1)
     bias_out[...] += jnp.sum(grads.astype(full), axis=0, keepdims=True)
-    hidden_terms[0] = dot_t(grads, up[...]).astype(low)
+
+    for number in range(PLANE - 1):
+        @pl.when(step == number + 1)
+        def _(number=number):
+            copies.start(number)
+
+    hidden_term = dot_t(grads, up[...]).astype(low)
+
+    @pl.when(step < last)
+    def _():
+        terms[step] = hidden_term
+
+    @pl.when(step == last)
+    def _():
+        hidden_terms[...] = hidden_term
+
     ffn_terms[0] = dot(gated, down[...]).astype(low)
     up_total[...] += outer_grad(hidden, grads)
     down_total[...] += outer_grad(gated, grad_branch)
@@ -802,6 +853,7 @@
     def _():
         up_parts[...] = up_total[...].astype(low).reshape(up_parts.shape)
         cut_columns(down_parts, down_total[...])
+        copies.finish()
 
 
 def split_kernel(groups, source, target):
@@ -830,31 +882,48 @@
     return pl.pallas_call(kernel, out_shape=jax.ShapeDtypeStruct(values.shape, values.dtype))(values)
 
 
-def block_call(kernel, inputs, blocked, out_blocks, out_whole, scratch, steps, flops):
+def block_call(
+    kernel, inputs, blocked, out_blocks, out_whole, scratch, steps, flops, identity, moved, landed, plan
+):
     def block_spec(shape, mark=1):
         tail = (0,) * (len(shape) - 1)
         if mark == 2:
-            return pl.BlockSpec((1,) + shape[1:], lambda p: (jnp.maximum(p - 1, 0),) + tail)
+            return pl.BlockSpec((1,) + shape[1:], lambda p: ((p + 2) % 3,) + tail)
         return pl.BlockSpec((1,) + shape[1:], lambda p: (p,) + tail)
 
     def whole_spec(shape):
         return pl.BlockSpec(shape, lambda p: (0,) * len(shape))
 
+    anywhere = pl.BlockSpec(memory_space=pl.ANY)
+    counts = [len(inputs), len(moved), len(out_blocks) + len(out_whole), len(landed)]
+    cuts = np.cumsum(counts).tolist()
+
+    def body(*refs):
+        ins, sources = refs[: cuts[0]], refs[cuts[0] : cuts[1]]
+        outs, targets = refs[cuts[1] : cuts[2]], refs[cuts[2] : cuts[3]]
+        rest, send, recv = refs[cuts[3] : -2], refs[-2], refs[-1]
+        kernel(Copies(plan, sources, targets, send, recv), rest, *ins, *outs, *rest)
+
     return pl.pallas_call(
-        kernel,
+        body,
         grid=(steps,),
-        out_shape=[jax.ShapeDtypeStruct(*o) for o in out_blocks + out_whole],
+        out_shape=[jax.ShapeDtypeStruct(*o) for o in out_blocks + out_whole + landed],
         in_specs=[
             block_spec(v.shape, b) if b else whole_spec(v.shape) for v, b in zip(inputs, blocked)
-        ],
-        out_specs=[block_spec(o[0]) for o in out_blocks] + [whole_spec(o[0]) for o in out_whole],
-        scratch_shapes=[pltpu.VMEM(*o) for o in scratch],
+        ]
+        + [anywhere] * len(moved),
+        out_specs=[block_spec(o[0]) for o in out_blocks]
+        + [whole_spec(o[0]) for o in out_whole]
+        + [anywhere] * len(landed),
+        scratch_shapes=[pltpu.VMEM(*o) for o in scratch]
+        + [pltpu.SemaphoreType.DMA((len(plan),)), pltpu.SemaphoreType.DMA((len(plan),))],
+        compiler_params=pltpu.CompilerParams(collective_id=identity, has_side_effects=True),
         cost_estimate=pl.CostEstimate(
             flops=flops,
             bytes_accessed=sum(v.size * v.dtype.itemsize for v in inputs),
             transcendentals=flops // 1024,
         ),
-    )(*inputs)
+    )(*inputs, *moved)
 
 
 def make_plane(z_size):
@@ -913,9 +982,18 @@
         plan += gather_moves(PLANE_HOPS + [SELF], 5, 5, by_chip)
         plan += [(hop, 0, by_dp, 0, by_dp, (0, 1, 2, 3)) for hop in DP_HOPS if hop != SELF]
         plan += relayed(2, 2, chip_place, len(plan))
-        silu_all, qkv_z, patch_all, proj_z, vectors, meta_all = exchange(
+        plan += relayed(6, 6, hop_place, len(plan))
+        silu_all, qkv_z, patch_all, proj_z, vectors, meta_all, cot_blocks = exchange(
             1,
-            [silu_low, qkv_weight, halves(patches), proj_weight, vector, meta],
+            [
+                silu_low,
+                qkv_weight,
+                halves(patches),
+                proj_weight,
+                vector,
+                meta,
+                halves(out_cotangent),
+            ],
             [
                 ((2 * PLANE, z_size, slots, width), low),
                 ((z_size, shard, cols_qkv), low),
@@ -923,6 +1001,7 @@
                 ((z_size, shard, cols_proj), low),
                 ((z_size,) + vector.shape, low),
                 ((PLANE,) + meta.shape, jnp.int32),
+                ((PLANE - 1, 2, row_count // 2, width), low),
             ],
             plan,
         )
@@ -980,19 +1059,8 @@
         group_mod = group_mod.transpose(0, 2, 1, 3).reshape(PLANE, slots, z_size * mod_cols)
         modulation = lax.dynamic_index_in_dim(group_mod, chip, 0, keepdims=False)
 
-        group_mod, (cot_later, up_z) = tie(group_mod, (out_cotangent, up_z))
-        cot_blocks = [cross(cot_later, hop) for hop in range(1, PLANE)]
         units = up_weight.shape[1] // 2
-
-        def up_piece(hop):
-            to = chip ^ hop
-            parts = []
-            for t in range(2):
-                block = lax.dynamic_index_in_dim(up_z, 2 * t + (to >> 1), 0, keepdims=False)
-                parts.append(jnp.where((to & 1) == 1, block[:, units:], block[:, :units]))
-            return jnp.concatenate(parts, axis=1)
-
-        up_blocks = [up_piece(0)] + [cross(up_piece(hop), hop) for hop in range(1, PLANE)]
+        up_pieces = whole_call(functools.partial(split_kernel, 2), up_z)
         segments = meta_all[:, 0].reshape(-1)
         meta_rows = meta_all.transpose(0, 2, 1)
         seg_col = meta_all[:, 0][:, None, :]
@@ -1086,7 +1154,7 @@
 
         gain_pad = jnp.zeros((2, LANES), full)
         gains = lax.dynamic_update_slice(gain_pad, jnp.stack([gain_q, gain_k]), (0, 0))
-        hidden_one, qkv_rows, attended_low, attn_terms, proj_slice = block_call(
+        hidden_one, qkv_rows, attended_low, attn_terms, proj_slice, up_same = block_call(
             functools.partial(attention_forward_kernel, head_size, heads),
             [
                 patch_all,
@@ -1113,26 +1181,23 @@
             [],
             PLANE,
             rows_all * width * 8 * part_cols,
-        )
-        attn_terms, (cot_blocks, up_blocks) = tie(attn_terms, (cot_blocks, up_blocks))
+            11,
+            [up_pieces],
+            [(up_pieces.shape, low)],
+            [(hop, 0, to_chip, 0, by_chip, None) for hop in PLANE_HOPS + [SELF]],
+        )
         plan = scatter_plan + gather_moves(Z_HOPS, 1, 1, by_z)
-        for number, hop in enumerate([SELF] + PLANE_HOPS):
-            plan.append(
-                (CORE_HOP, 2 + number, None, 2, lambda me, peer, hop=hop: (me.hop(*hop).dp,), None)
-            )
-        branch_blocks, down_z, up_slice = exchange(
+        plan.append((CORE_HOP, 2, None, 2, None, None))
+        branch_blocks, down_z, up_other = exchange(
             4,
-            [attn_terms, down_weight] + up_blocks,
+            [attn_terms, down_weight, up_same],
             [
                 (others, low),
                 ((z_size,) + down_weight.shape, low),
-                ((2 * PLANE,) + up_weight.shape, low),
+                (up_same.shape, low),
             ],
             plan,
         )
-        for hop in range(PLANE):
-            up_slice = put(up_slice, up_blocks[hop], dp_index ^ (2 * hop))
-        up_slice = up_slice.reshape(-1, up_weight.shape[1])
         down_z = put(down_z, down_weight, z_index)
         branch_attn = plane_sum_of(branch_blocks, attn_terms) + proj_vector
 
@@ -1150,44 +1215,49 @@
             [((PLANE - 1, 2, row_count // 2, width), low), (down_z.shape, low)],
             relayed(0, 0, hop_place, 0) + [(CORE_HOP, 1, None, 1, None, None)],
         )
+        steps = PLANE_HOPS[2:] + PLANE_HOPS[:2]
         gate_spans = xor_order(group_spans[:, :, 5 * width :], chip, PLANE)
-        hidden_two_terms, ffn_terms, up_bias_cols, up_parts, down_parts = block_call(
+        gate_spans = jnp.stack([gate_spans[k] for k in (3, 1, 2, 0)])
+        ffn_terms, own_terms, up_bias_cols, up_parts, down_parts, hidden_two_blocks = block_call(
             ffn_kernel,
             [
                 hidden_two,
                 hidden_blocks.reshape(others),
                 out_cotangent,
-                jnp.stack(cot_blocks),
+                cot_blocks.reshape(others),
                 gate_spans[:, :, None],
-                up_slice,
+                up_same,
+                up_other,
                 down_z,
                 down_other,
                 own_columns(up_vector, 2)[None],
             ],
-            [0, 2, 0, 2, 1, 0, 0, 0, 0],
-            [((PLANE, row_count, width), low), ((PLANE, row_count, width), low)],
-            [
+            [0, 2, 0, 2, 1, 0, 0, 0, 0, 0],
+            [((PLANE, row_count, width), low)],
+            [
+                ((row_count, width), low),
                 ((1, 2 * units), full),
                 ((PLANE, 2, shard, 2 * units), low),
                 ((z_size, 2) + down_weight.shape, low),
             ],
-            [((units, width), low), ((width, 2 * units), full), ((units, width), full)],
+            [
+                ((units, width), low),
+                ((width, 2 * units), low),
+                ((width, 2 * units), full),
+                ((units, width), full),
+                (others, low),
+            ],
             PLANE,
             rows_all * width * 18 * units,
-        )
-        hop_scatter = [
-            (hop, 0, lambda me, peer, n=n: (n + 1,), 0, lambda me, peer, n=n: (n,), None)
-            for n, hop in enumerate(PLANE_HOPS)
-        ]
-        hidden_two_blocks, down_other, up_other = exchange(
             6,
-            [hidden_two_terms, down_parts, up_parts],
-            [(others, low), half_of(down_parts), half_of(up_parts)],
-            hop_scatter + core_swap(1, 1, z_size) + core_swap(2, 2, PLANE),
-        )
-        grad_hidden_two = block_sum(hidden_two_blocks, hidden_two_terms[0])
-        down_mine = sum_cores(down_parts, down_other)
-        up_mine = sum_cores(up_parts, up_other)
+            [],
+            [(others, low)],
+            [
+                (hop, 0, lambda me, peer, k=k: (k,), 0, lambda me, peer, k=k: (k,), None)
+                for k, hop in enumerate(steps)
+            ],
+        )
+        grad_hidden_two = block_sum(hidden_two_blocks, own_terms)
 
         grad_out = out_cotangent.astype(full)
         own_gbf = (grad_out * per_row(5)).astype(low).astype(full)
@@ -1198,25 +1268,39 @@
         grad_gate_attn = grad_middle * branch_attn
         grad_branch_attn = (grad_middle * per_row(2)).astype(low)
         proj_bias_grad = jnp.sum(grad_branch_attn.astype(full), axis=0)
-        grad_branch_all, down_blocks = exchange(
+        grad_branch_all, down_swapped, up_swapped = exchange(
             7,
-            [halves(grad_branch_attn), down_mine],
+            [halves(grad_branch_attn), down_parts, up_parts],
             [
                 ((PLANE, 2, row_count // 2, width), low),
-                ((z_size - 1,) + down_mine.shape[1:], low),
-            ],
-            relayed(0, 0, chip_place, 0) + slotted(Z_HOPS, 1, to_z, 1),
-        )
+                half_of(down_parts),
+                half_of(up_parts),
+            ],
+            relayed(0, 0, chip_place, 0)
+            + core_swap(1, 1, z_size)
+            + core_swap(2, 2, PLANE),
+        )
+        down_mine = sum_cores(down_parts, down_swapped)
+        up_mine = sum_cores(up_parts, up_swapped)
         grad_branch_all = put(
             grad_branch_all.reshape(PLANE, row_count, width), grad_branch_attn, chip
         )
-        down_grad = z_sum_of(down_blocks, down_mine)
-
-        grad_branch_all, (ffn_terms, up_mine) = tie(grad_branch_all, (ffn_terms, up_mine))
-        ffn_blocks = [cross(ffn_terms[hop], hop) for hop in range(1, PLANE)]
-        up_moved = [cross(own_of(up_mine, chip ^ hop), hop) for hop in range(1, PLANE)]
-
-        hidden_one_terms, qkv_bias_cols, gain_grads, qkv_parts, proj_parts = block_call(
+        plan = [
+            (hop, 0, lambda me, peer, k=k: (k,), 0, lambda me, peer, k=k: (k,), None)
+            for k, hop in enumerate(steps)
+        ]
+        plan += [(hop, 1, to_chip, 1, by_chip, None) for hop in PLANE_HOPS + [SELF]]
+        plan += slotted(Z_HOPS, 2, to_z, 2)
+        (
+            hidden_one_terms,
+            qkv_bias_cols,
+            gain_grads,
+            qkv_parts,
+            proj_parts,
+            ffn_blocks,
+            up_moved,
+            down_blocks,
+        ) = block_call(
             functools.partial(attention_backward_kernel, head_size, heads),
             [
                 grad_branch_all,
@@ -1242,25 +1326,18 @@
             [((width, 3 * part_cols), full), ((part_cols, width), full)],
             PLANE,
             rows_all * width * 18 * part_cols,
+            12,
+            [ffn_terms, up_mine, down_mine],
+            [
+                (others, low),
+                (up_mine.shape, low),
+                ((z_size - 1,) + down_mine.shape[1:], low),
+            ],
+            plan,
         )
         gain_q_grad, gain_k_grad = gain_grads[0, :head_size], gain_grads[1, :head_size]
-        hidden_one_terms, (ffn_blocks, up_moved) = tie(hidden_one_terms, (ffn_blocks, up_moved))
-        up_moved = [own_of(up_mine, chip)] + up_moved
-
-        def up_columns(p, t):
-            parts = [v[:, t * units : (t + 1) * units] for v in up_moved]
-            odd, high = ((chip ^ p) & 1) == 1, ((chip ^ p) & 2) == 2
-            return jnp.where(
-                high, jnp.where(odd, parts[3], parts[2]), jnp.where(odd, parts[1], parts[0])
-            )
-
-        up_wide = jnp.stack(
-            [
-                jnp.concatenate([up_columns(p, t), up_columns(p + 1, t)], axis=1)
-                for t in range(2)
-                for p in (0, 2)
-            ]
-        )
+        up_wide = whole_call(functools.partial(merge_kernel, 2), up_moved)
+        hidden_one_terms, up_wide = tie(hidden_one_terms, up_wide)
         up_grad = lax.psum_scatter(up_wide, "fsdp", scatter_dimension=0, tiled=False).astype(full)
         hidden_one_blocks, qkv_other, proj_other = exchange(
             8,
@@ -1269,9 +1346,8 @@
             scatter_plan + core_swap(1, 1, PLANE) + core_swap(2, 2, z_size),
         )
         grad_hidden_one = plane_sum_of(hidden_one_blocks, hidden_one_terms)
-        branch_ffn = ffn_terms[0].astype(full) + down_vector
-        for block in ffn_blocks:
-            branch_ffn = branch_ffn + block.astype(full)
+        branch_ffn = block_sum(ffn_blocks, ffn_terms[PLANE - 1]) + down_vector
+        down_grad = z_sum_of(down_blocks, down_mine)
         block_out = (middle + per_row(5) * branch_ffn).astype(low)
         grad_gate_ffn = grad_out * branch_ffn
         qkv_mine = sum_cores(qkv_parts, qkv_other)

time: 554 us -> 517 us (0.933)
  other arithmetic: 77.9 us -> 57.9 us
  starting transfers between devices: 14.1 us -> 0.08 us
  Pallas kernels: 376 us -> 389 us
  waiting for transfers between devices: 10 us -> 0.04 us
    pallas_call x3, Pallas kernels: 97.9 us -> 124 us  [block_call(): pl.pallas_call(body, grid=(steps,), out_shape=[jax.ShapeDtypeStruct(*o) f...]
    pallas_call x10 -> x9, Pallas kernels: 273 us -> 255 us  [exchange(): pl.pallas_call(kernel, out_shape=[jax.ShapeDtypeStruct(shape, dtype) for...]
    ppermute x12 -> x0, starting transfers between devices: 14 us -> none  [cross(): lax.ppermute(values, 'dp', [(k, k ^ 2 * hop) for k in range(2 * PLANE)])]
    ppermute x12 -> x0, waiting for transfers between devices: 9.97 us -> none  [cross(): lax.ppermute(values, 'dp', [(k, k ^ 2 * hop) for k in range(2 * PLANE)])]
    pallas_call x2 -> x4, Pallas kernels: 4.97 us -> 10.7 us  [whole_call(): pl.pallas_call(kernel, out_shape=jax.ShapeDtypeStruct(values.shape, value...]
    unnamed x125 -> x87, local copies, waits for them, and re-layouts: 6.6 us -> 11.1 us
    dynamic_update_slice x12 -> x8, local copies, waits for them, and re-layouts: 12.1 us -> 8.84 us  [put(): lax.dynamic_update_slice(values, own.reshape((1,) * len(at) + own.shape),...]
  transfers between devices with their start and end apart: 14 -> 2, of which waited for: 3 -> 0; matrix products, arithmetic and copies ran while one was open for 15% -> 11% of each run, Pallas kernels for 36% -> 21%
where the time goes in v4:
time: 517 us; the launch traced here: 507 us
  Pallas kernels  389 us (75%)
  other arithmetic  57.9 us (11%)
  local copies, waits for them, and re-layouts  40.3 us (8%)
  between operations  15.1 us (3%)
    pallas_call x9, Pallas kernels, exchange(): pl.pallas_call(kernel, out_shape=[jax.ShapeDtypeStruct(shape, dtype) for...  255 us
    pallas_call x3, Pallas kernels, block_call(): pl.pallas_call(body, grid=(steps,), out_shape=[jax.ShapeDtypeStruct(*o) f...  124 us
    convert_element_type x4, other arithmetic, sum_cores(): return (mine.astype(full) + other.astype(full)).astype(low)  11.5 us
    unnamed x87, local copies, waits for them, and re-layouts  11.1 us
    pallas_call x4, Pallas kernels, whole_call(): pl.pallas_call(kernel, out_shape=jax.ShapeDtypeStruct(values.shape, value...  10.7 us
  transfers between devices with their start and end apart: 2, of which 0 were waited for; matrix products, arithmetic and copies ran while one was open for 11% of the time, Pallas kernels for 21%

profile of v4, /device:TPU:0, one launch (start us, length us, event | category | flops | bytes accessed | tf_op | source)
XLA Modules:
  0.0 507.1 jit_solution(14294479003496568642)
XLA Ops:
  7.3 1.4 fusion.36.refs_0_
  9.4 2.8 concatenate.12
  12.8 1.3 pad_add_fusion.refs_5_
  14.1 52.6 %shard_map.281 = (bf16[8,4,4,1152]{3,2,1,0:T(4,128)(2,1)}, bf16[4,144,864]{2,1,0:T(8,128)(2,1)}, bf16[4,2,128,1152]{3,2,1,0:T(8,128)(2,1)}, bf16[4,144,288]{2,1,...) custom-call(bf16[4,1152]{1,0:T(4,128)(2,1)} %fusion.36.refs_0_, ...), custom_call_target="tpu_custom_call" | custom-call | tf_op jit(solution)/shard_map/pallas_call | solution.py:527
  66.8 0.8 copy.157
  67.8 1.3 fusion.51
  69.1 1.7 copy.123
  71.6 2.5 shard_map.282.refs_0_
  75.0 1.3 fusion.31
  76.2 24.9 %shard_map.283 = (bf16[8,144,864]{2,1,0:T(8,128)(2,1)}, f32[8,16,1728]{2,1,0:T(8,128)}, bf16[4,144,288]{2,1,0:T(8,128)(2,1)}) custom-call(bf16[4,144,864]{2,1,0:T(8,128)(2,1)} %shard_map.282.refs_0_, f32[8,16,1728]{2,1,0:T(8,128)} %bitcast.162, bf16[4,144,288]{2,1,0:T(8,128)(2,1)} %bitcast_dynamic-update-slice_fusion.4.refs_2_.refs_10_), custom_call_target="tpu_custom_call" | custom-call | tf_op jit(solution)/shard_map/pallas_call | solution.py:527
  101.1 1.6 dynamic-slice_dynamic-update-slice_fusion.2
  102.6 1.2 reduce_sum.251
  104.6 14.8 %shard_map.284 = f32[4,4,4,1728]{3,2,1,0:T(4,128)} custom-call(f32[4,4,1728]{2,1,0:T(4,128)} %broadcast_add_fusion.refs_0_), custom_call_target="tpu_custom_call" | custom-call | tf_op jit(solution)/shard_map/pallas_call | solution.py:527
  119.4 1.1 copy.120
  121.3 1.2 multiply_reduce_fusion
  125.0 0.9 copy.124.refs_1_
  128.5 1.7 dynamic-slice_dynamic-update-slice_fusion.1
  130.6 0.9 bitcast_dynamic-update-slice_fusion.1.refs_0_
  131.5 2.9 shard_map.285.refs_12_
  134.4 26.7 %shard_map.286 = (bf16[4,256,1152]{2,1,0:T(8,128)(2,1)}, f32[4,256,864]{2,1,0:T(8,128)}, bf16[4,256,288]{2,1,0:T(8,128)(2,1)}, bf16[4,256,1152]{2,1,0:T(8,128)(2...) custom-call(bf16[4,256,1152]{2,1,0:T(8,128)(2,1)} %bitcast_dynamic-update-slice_fusion.1.refs_0_, ...), custom_call_target="tpu_custom_call" | custom-call | flops 2717908992 | bytes 5214592 | tf_op jit(solution)/shard_map/pallas_call | solution.py:907
  161.1 28.6 %shard_map.287 = (bf16[3,256,1152]{2,1,0:T(8,128)(2,1)}, bf16[4,384,288]{2,1,0:T(8,128)(2,1)}, bf16[4,144,1536]{2,1,0:T(8,128)(2,1)}) custom-call(bf16[4,256,1152]{2,1,0:T(8,128)(2,1)} %get-tuple-element.77.refs_0_, bf16[384,288]{1,0:T(8,128)(2,1)} %copy.124.refs_1_, bf16[4,144,1536]{2,1,0:T(8,128)(2,1)} %get-tuple-element.78.refs_2_.refs_5_), custom_call_target="tpu_custom_call" | custom-call | tf_op jit(solution)/shard_map/pallas_call | solution.py:527
  189.7 1.9 convert_reduce_fusion.3
  191.7 2.0 multiply_reduce_fusion.2
  195.0 1.0 fusion.18.refs_0_
  196.0 22.2 %shard_map.288 = (bf16[3,2,128,1152]{3,2,1,0:T(8,128)(2,1)}, bf16[4,384,288]{2,1,0:T(8,128)(2,1)}) custom-call(bf16[2,128,1152]{2,1,0:T(8,128)(2,1)} %bitcast.164, bf16[4,384,288]{2,1,0:T(8,128)(2,1)} %bitcast_dynamic-update-slice_fusion.2.refs_1_.refs_7_), custom_call_target="tpu_custom_call" | custom-call | tf_op jit(solution)/shard_map/pallas_call | solution.py:527
  218.3 44.0 %shard_map.289 = (bf16[4,256,1152]{2,1,0:T(8,128)(2,1)}, bf16[256,1152]{1,0:T(8,128)(2,1)}, f32[1,1536]{1,0:T(1,128)}, bf16[4,2,144,1536]{3,2,1,0:T(8,128)(2,1)}...) custom-call(bf16[256,1152]{1,0:T(8,128)(2,1)} %fusion.18.refs_0_, bf16[3,256,1152]{2,1,0:T(8,128)(2,1)} %bitcast.194, ...), custom_call_target="tpu_custom_call" | custom-call | flops 16307453952 | bytes 10106880 | tf_op jit(solution)/shard_map/pallas_call | solution.py:907
  262.3 1.9 convert_reduce_fusion.2
  265.7 2.4 convert_reduce_fusion.7
  268.2 21.8 %shard_map.290 = (bf16[4,2,128,1152]{3,2,1,0:T(8,128)(2,1)}, bf16[4,384,288]{2,1,0:T(8,128)(2,1)}, bf16[4,144,1536]{2,1,0:T(8,128)(2,1)}) custom-call(bf16[2,128,1152]{2,1,0:T(8,128)(2,1)} %bitcast.159, bf16[4,2,384,288]{3,2,1,0:T(8,128)(2,1)} %get-tuple-element.88.refs_1_, bf16[4,2,144,1536]{3,2,1,0:T(8,128)(2,1)} %get-tuple-element.89.refs_2_), custom_call_target="tpu_custom_call" | custom-call | tf_op jit(solution)/shard_map/pallas_call | solution.py:527
  290.0 0.9 bitcast_dynamic-update-slice_fusion.refs_0_
  290.8 4.6 fusion.refs_12_
  295.4 1.5 fusion.1.refs_13_
  296.9 53.1 %shard_map.291 = (bf16[4,256,1152]{2,1,0:T(8,128)(2,1)}, f32[1,864]{1,0:T(1,128)}, f32[2,128]{1,0:T(2,128)}, bf16[4,2,144,864]{3,2,1,0:T(8,128)(2,1)}, bf16[4,2,...) custom-call(bf16[4,256,1152]{2,1,0:T(8,128)(2,1)} %bitcast_dynamic-u, ...), custom_call_target="tpu_custom_call" | custom-call | flops 6115295232 | bytes 11551744 | tf_op jit(solution)/shard_map/pallas_call | solution.py:907
  350.0 2.8 shard_map.292
  352.8 2.2 dynamic-slice_convert_fusion
  354.9 28.7 %shard_map.293 = (bf16[3,256,1152]{2,1,0:T(8,128)(2,1)}, bf16[4,144,864]{2,1,0:T(8,128)(2,1)}, bf16[4,144,288]{2,1,0:T(8,128)(2,1)}) custom-call(bf16[4,256,1152]{2,1,0:T(8,128)(2,1)} %get-tuple-element.100.refs_0_, bf16[4,2,144,864]{3,2,1,0:T(8,128)(2,1)} %get-tuple-element.101.refs_1_, bf16[4,2,144,288]{3,2,1,0:T(8,128)(2,1)} %get-tuple-element.102.refs_2_), custom_call_target="tpu_custom_call" | custom-call | tf_op jit(solution)/shard_map/pallas_call | solution.py:527
  383.6 2.0 convert_reduce_fusion
  385.9 1.0 copy-done.3
  387.3 2.5 bitcast_reduce_fusion.1
  389.7 2.6 fusion.7
  394.5 2.0 bitcast_reduce_fusion.3
  398.1 2.2 fusion.23.refs_3_
  400.9 1.3 constant_dynamic-update-slice_fusion.3
  402.2 1.3 constant_dynamic-update-slice_fusion.2
  403.6 1.3 constant_dynamic-update-slice_fusion.1
  405.5 1.1 multiply_reduce_fusion.3
  406.6 2.4 fusion.11
  409.8 0.8 mul.233
  410.6 0.8 reshape.330
  413.2 3.2 fusion.2.refs_0_
  416.4 25.2 %shard_map.294 = (bf16[4,144,864]{2,1,0:T(8,128)(2,1)}, bf16[8,4,4,1728]{3,2,1,0:T(4,128)(2,1)}, f32[4,1,3012]{2,1,0:T(1,128)}, bf16[3,144,288]{2,1,0:T(8,128)(2,1)}) custom-call(bf16[4,144,864]{2,1,0:T(8,128)(2,1)} %fusion.2.refs_0_, bf16[4,4,1728]{2,1,0:T(4,128)(2,1)} %bitcast.172, f32[4,1,3012]{2,1,0:T(1,128)} %concatenate.15.refs_2_, ...), custom_call_target="tpu_custom_call" | custom-call | tf_op jit(solution)/shard_map/pallas_call | solution.py:527
  441.6 1.7 dynamic-slice_dynamic-update-slice_fusion.source
  443.3 2.5 shard_map.295.refs_0_
  446.6 1.1 fusion.25.refs_1_
  447.7 36.0 %shard_map.296 = (bf16[3,144,864]{2,1,0:T(8,128)(2,1)}, f32[8,4,4,144]{3,2,1,0:T(4,128)}, f32[8,1,3012]{2,1,0:T(1,128)}) custom-call(bf16[4,144,864]{2,1,0:T(8,128)(2,1)} %shard_map.295.refs_0_, f32[8,4,4,144]{3,2,1,0:T(4,128)} %fusion.25.refs_1_, f32[1,3012]{1,0:T(1,128)} %bitcast.182), custom_call_target="tpu_custom_call" | custom-call | tf_op jit(solution)/shard_map/pallas_call | solution.py:527
  483.7 0.9 reduce_sum.275
  484.8 1.0 reduce_sum.278
  485.9 1.1 convert_add_fusion.9
  487.0 1.0 copy.139
  490.6 0.8 convert_reduce_fusion.8
  491.5 1.6 convert_add_fusion.11
  493.1 1.8 convert_add_fusion.10
  494.9 2.3 fusion.29
  497.8 2.0 bitcast_convert_fusion
  (163 shorter events, 25.6 us)
Async XLA Ops:
  7.2 67.8 %copy-start = (bf16[144,1728]{1,0:T(8,128)(2,1)S(1)}, bf16[144,1728]{1,0:T(8,128)(2,1)}, u32[]{:S(2)}) copy-start(bf16[144,1728]{1,0:T(8,128)(2,1)} %param.22) | copy-start | bytes 1492996
  7.2 59.6 %copy-start.35 = (s32[256]{0:T(256)S(1)}, s32[256]{0:T(256)}, u32[]{:S(2)}) copy-start(s32[256]{0:T(256)} %param.20) | copy-start | bytes 3076
  7.2 124.3 %all-gather.3.cloned.1.call-start = ((), (), s32[]{:S(2)}) async-start(), calls=%async_computation.2 | async-start | bytes 2211840 | tf_op jit(solution)/shard_map/all_gather | solution.py:1010
  14.1 56.8 %copy-start.19 = (bf16[144,864]{1,0:T(8,128)(2,1)S(1)}, bf16[144,864]{1,0:T(8,128)(2,1)}, u32[]{:S(2)}) copy-start(bf16[144,864]{1,0:T(8,128)(2,1)} %refs_1_.2) | copy-start | bytes 746500
  66.7 431.1 %reduce-scatter.2.cloned.1.call-start = ((), (), s32[]{:S(2)}) async-start(), calls=%async_computation.1 | async-start | bytes 2211840 | tf_op jit(solution)/shard_map/reduce_scatter | solution.py:1341
  70.9 3.3 copy-start.25
  71.6 2.6 copy-start.23
  74.2 26.9 %copy-start.22 = (bf16[128,1152]{1,0:T(8,128)(2,1)}, bf16[128,1152]{1,0:T(8,128)(2,1)S(1)}, u32[]{:S(2)}) copy-start(bf16[128,1152]{1,0:T(8,128)(2,1)S(1)} %reshape.306) | copy-start | bytes 884740
  101.1 2.8 copy-start.34
  121.0 4.0 copy-start.26
  122.7 8.0 %copy-start.1 = (bf16[256,1152]{1,0:T(8,128)(2,1)S(1)}, bf16[256,1152]{1,0:T(8,128)(2,1)}, u32[]{:S(2)}) copy-start(bf16[256,1152]{1,0:T(8,128)(2,1)} %param.18) | copy-start | bytes 1769476
  130.2 4.2 copy-start.30
  191.6 2.0 copy-start.5
  191.7 2.6 copy-start.15
  262.3 1.9 copy-start.12
  264.2 1.1 copy-start.2
  264.2 1.5 copy-start.10
  268.2 21.8 %copy-start.9 = (bf16[256,1152]{1,0:T(8,128)(2,1)S(1)}, bf16[256,1152]{1,0:T(8,128)(2,1)}, u32[]{:S(2)}) copy-start(bf16[256,1152]{1,0:T(8,128)(2,1)} %get-tuple-element.197) | copy-start | bytes 1769476
  290.8 4.6 copy-start.7
  290.8 4.6 copy-start.18
  383.6 2.0 copy-start.17
  385.6 1.3 copy-start.3
  385.7 1.4 copy-start.11
  385.7 1.6 copy-start.13
  387.2 2.5 copy-start.8
  387.2 2.5 copy-start.32
  389.7 3.1 copy-start.14
  392.9 1.3 copy-start.4
  392.9 1.6 copy-start.6
  394.5 2.0 copy-start.36
  394.5 2.1 copy-start.33
  394.5 2.2 copy-start.37
  400.3 4.6 copy-start.27
  400.3 5.2 %copy-start.31 = (f32[4,4]{1,0:T(4,128)S(1)}, f32[4,4]{1,0:T(4,128)}, u32[]{:S(2)}) copy-start(f32[4,4]{1,0:T(4,128)} %copy-done.30) | copy-start | bytes 196
  406.6 5.6 %copy-start.38 = (f32[2,128]{1,0:T(2,128)S(1)}, f32[2,128]{1,0:T(2,128)}, u32[]{:S(2)}) copy-start(f32[2,128]{1,0:T(2,128)} %get-tuple-element.107) | copy-start | bytes 3076
  441.6 4.2 copy-start.28
  443.3 3.2 copy-start.16
  447.7 38.0 %copy-start.20 = (bf16[3,384,288]{2,1,0:T(8,128)(2,1)S(1)}, bf16[3,384,288]{2,1,0:T(8,128)(2,1)}, u32[]{:S(2)}) copy-start(bf16[3,384,288]{2,1,0:T(8,128)(2,1)} %get-tuple-element.117) | copy-start | bytes 1990660
  485.9 4.6 copy-start.24
  487.0 4.4 copy-start.21
  493.1 4.1 copy-start.29
Sparse Core Ops, SparseCore 0:
  66.8 38.7 all-gather.2
  400.4 45.7 reduce-scatter.1

commit v5 on v4

--- a/solution.py
+++ b/solution.py
@@ -690,19 +690,22 @@
 
 
 def attention_forward_kernel(head_size, heads, copies, rest, *refs):
-    (patch, shift, scale, weight, bias, gains, cos_rows, sin_rows, meta, seg_col) = refs[:10]
-    proj_mine, proj_other = refs[10:12]
-    hidden_out, rows_out, attended_out, terms_out, proj = refs[12:]
-
-    @pl.when(pl.program_id(0) == 0)
+    (own_patch, patches, shift, scale, weight, bias, gains, cos_rows, sin_rows) = refs[:9]
+    meta, seg_col, proj_mine, proj_other = refs[9:13]
+    hidden_out, rows_out, attended_out, own_terms, proj, terms = refs[13:]
+    copies.ins = list(copies.ins) + [terms]
+    step, last = pl.program_id(0), pl.num_programs(0) - 1
+    first = len(copies.plan) - (PLANE - 1)
+
+    @pl.when(step == 0)
     def _():
         copies.greet()
-        for number in range(len(copies.plan)):
+        for number in range(first):
             copies.start(number)
         fill_rows(proj, proj_mine, proj_other)
 
     cosine, sine = rotary_of(meta[0], cos_rows[...], sin_rows[...])
-    values = patch[0].astype(full)
+    values = jnp.where(step == last, own_patch[...], patches[0]).astype(full)
     count, width = values.shape
     normed = values * lax.rsqrt(jnp.mean(values * values, axis=1, keepdims=True) + epsilon)
     hidden = normed.reshape(count // SPAN, SPAN, width) * (1.0 + scale[0]) + shift[0]
@@ -716,10 +719,21 @@
         pieces.append(dot(probs.astype(low), value)[:, :head_size])
     attended = jnp.concatenate(pieces, axis=1).astype(low)
     attended_out[0] = attended
-    terms_out[0] = dot(attended, proj[...]).astype(low)
-
-    @pl.when(pl.program_id(0) == pl.num_programs(0) - 1)
+
+    for number in range(PLANE - 1):
+        @pl.when(step == number + 1)
+        def _(number=number):
+            copies.start(first + number)
+
+    term = dot(attended, proj[...]).astype(low)
+
+    @pl.when(step < last)
     def _():
+        terms[step] = term
+
+    @pl.when(step == last)
+    def _():
+        own_terms[...] = term
         copies.finish()
 
 
@@ -730,10 +744,10 @@
 
 
 def attention_backward_kernel(head_size, heads, copies, rest, *refs):
-    (grad, rows, weight, gains, cos_rows, sin_rows, meta, seg_col, proj) = refs[:9]
-    hidden, attended = refs[9:11]
-    terms_out, bias_out, gains_out, qkv_parts, proj_parts = refs[11:16]
-    qkv_total, proj_total = refs[16:]
+    (own_grad, grads, rows, weight, gains, cos_rows, sin_rows, meta, seg_col, proj) = refs[:10]
+    hidden, attended = refs[10:12]
+    terms_out, bias_out, gains_out, qkv_parts, proj_parts = refs[12:17]
+    qkv_total, proj_total = refs[17:]
 
     @pl.when(pl.program_id(0) == 0)
     def _():
@@ -748,7 +762,9 @@
     score_scale = head_size ** (-0.5)
     gain_values = gains[...]
     cos_tab, sin_tab = rotary_of(meta[0], cos_rows[...], sin_rows[...])
-    grad_attended = dot_t(grad[0], proj[...])
+    own_step = pl.program_id(0) == pl.num_programs(0) - 1
+    grad = jnp.where(own_step, own_grad[...], grads[0])
+    grad_attended = dot_t(grad, proj[...])
     values = rows[0]
     grad_queries, grad_keys, grad_values = [], [], []
     gain_sums = [jnp.zeros((1, LANES), full), jnp.zeros((1, LANES), full)]
@@ -780,7 +796,7 @@
     gains_out[1:2, :] += gain_sums[1]
     terms_out[0] = dot_t(result, weight[...]).astype(low)
     qkv_total[...] += outer_grad(hidden[0], result)
-    proj_total[...] += outer_grad(attended[0], grad[0])
+    proj_total[...] += outer_grad(attended[0], grad)
 
     @pl.when(pl.program_id(0) == pl.num_programs(0) - 1)
     def _():
@@ -856,15 +872,67 @@
         copies.finish()
 
 
-def split_kernel(groups, source, target):
-    count, _, cols = source.shape
-    part = cols // groups
-    for p in range(count):
-        pieces = []
-        for t in range(groups):
-            block, at = divmod(t * count + p, groups)
-            pieces.append(source[block, :, at * part : (at + 1) * part])
-        target[p] = jnp.concatenate(pieces, axis=1)
+def tail_kernel(*refs):
+    (patch, cot, middle, branch, grad_middle, grad_two, one_blocks, one_own) = refs[:8]
+    ffn_blocks, ffn_own, spans, bias, patch_grad, block_out, sums = refs[8:]
+
+    def total(own, blocks):
+        return own[0].astype(full) + sum(blocks[k].astype(full) for k in range(PLANE - 1))
+
+    def mean(values):
+        return jnp.mean(values, axis=1, keepdims=True)
+
+    values, mid, grad_mid = patch[...].astype(full), middle[...], grad_middle[...]
+    scale_one = lax.rsqrt(mean(values * values) + epsilon)
+    normed_one = values * scale_one
+    grad_one = total(one_own, one_blocks)
+    scaled = grad_one * (1.0 + spans[0, 1:2])
+    backward = scale_one * (scaled - normed_one * mean(scaled * normed_one))
+    patch_grad[...] = (grad_mid + backward).astype(low)
+    normed_two = mid * lax.rsqrt(mean(mid * mid) + epsilon)
+    branch_ffn = total(ffn_own, ffn_blocks) + bias[...]
+    block_out[...] = (mid + spans[0, 5:6] * branch_ffn).astype(low)
+    grads = [
+        grad_one,
+        grad_one * normed_one,
+        grad_mid * branch[...],
+        grad_two[...],
+        grad_two[...] * normed_two,
+        cot[...].astype(full) * branch_ffn,
+    ]
+    for k, values in enumerate(grads):
+        sums[0, k : k + 1] = jnp.sum(values, axis=0, keepdims=True)
+
+
+def tail_call(rows, groups, spans, bias):
+    count, _, width = spans.shape
+    row = pl.BlockSpec((SPAN, width), lambda p: (p, 0))
+    group = pl.BlockSpec((PLANE - 1, SPAN, width), lambda p: (0, p, 0))
+    own = pl.BlockSpec((1, SPAN, width), lambda p: (PLANE - 1, p, 0))
+    span = pl.BlockSpec((1,) + spans.shape[1:], lambda p: (p, 0, 0))
+    whole = pl.BlockSpec((1, width), lambda p: (0, 0))
+    result = jax.ShapeDtypeStruct(rows[0].shape, low)
+    return pl.pallas_call(
+        tail_kernel,
+        grid=(count,),
+        out_shape=[result, result, jax.ShapeDtypeStruct(spans.shape, full)],
+        in_specs=[row] * 6 + [group, own, group, own, span, whole],
+        out_specs=[row, row, span],
+    )(*rows, *groups, spans, bias)
+
+
+def split_kernel(groups, *refs):
+    target, first = refs[-1], 0
+    for source in refs[:-1]:
+        count, rows, cols = source.shape
+        part = cols // groups
+        for p in range(count):
+            pieces = []
+            for t in range(groups):
+                block, at = divmod(t * count + p, groups)
+                pieces.append(source[block, :, at * part : (at + 1) * part])
+            target[p, first : first + rows] = jnp.concatenate(pieces, axis=1)
+        first += rows
 
 
 def merge_kernel(groups, source, target):
@@ -878,8 +946,12 @@
         target[z] = jnp.concatenate(pieces, axis=1)
 
 
-def whole_call(kernel, values):
-    return pl.pallas_call(kernel, out_shape=jax.ShapeDtypeStruct(values.shape, values.dtype))(values)
+def whole_call(kernel, *values):
+    count, _, cols = values[0].shape
+    rows = sum(v.shape[1] for v in values)
+    return pl.pallas_call(
+        kernel, out_shape=jax.ShapeDtypeStruct((count, rows, cols), values[0].dtype)
+    )(*values)
 
 
 def block_call(
@@ -976,14 +1048,14 @@
         cols_qkv = qkv_weight.shape[1]
         cols_proj = proj_weight.shape[1]
         plan = gather_moves(Z_HOPS + [SELF], 0, 0, lambda me, peer: (me.dp, me.z))
-        plan += gather_moves(Z_HOPS, 1, 1, by_z)
-        plan += gather_moves(Z_HOPS, 3, 3, by_z)
+        plan += gather_moves(Z_HOPS + [SELF], 1, 1, by_z)
+        plan += gather_moves(Z_HOPS + [SELF], 3, 3, by_z)
         plan += gather_moves(Z_HOPS + [SELF], 4, 4, by_z)
         plan += gather_moves(PLANE_HOPS + [SELF], 5, 5, by_chip)
         plan += [(hop, 0, by_dp, 0, by_dp, (0, 1, 2, 3)) for hop in DP_HOPS if hop != SELF]
-        plan += relayed(2, 2, chip_place, len(plan))
+        plan += relayed(2, 2, hop_place, len(plan))
         plan += relayed(6, 6, hop_place, len(plan))
-        silu_all, qkv_z, patch_all, proj_z, vectors, meta_all, cot_blocks = exchange(
+        silu_all, qkv_z, patch_blocks, proj_z, vectors, meta_all, cot_blocks = exchange(
             1,
             [
                 silu_low,
@@ -997,7 +1069,7 @@
             [
                 ((2 * PLANE, z_size, slots, width), low),
                 ((z_size, shard, cols_qkv), low),
-                ((PLANE, 2, row_count // 2, width), low),
+                ((PLANE - 1, 2, row_count // 2, width), low),
                 ((z_size, shard, cols_proj), low),
                 ((z_size,) + vector.shape, low),
                 ((PLANE,) + meta.shape, jnp.int32),
@@ -1006,11 +1078,10 @@
             plan,
         )
 
-        qkv_z, up_later = tie(qkv_z, up_weight)
-        up_z = lax.all_gather(up_later, "fsdp", axis=0, tiled=False)
-        qkv_z = put(qkv_z, qkv_weight, z_index)
-        proj_z = put(proj_z, proj_weight, z_index)
-        patch_all = put(patch_all.reshape(PLANE, row_count, width), patches, chip)
+        up_cut = shard // 48 * 32
+        up_cols = up_weight.shape[1]
+        up_part = lambda me, peer: (pl.ds(0, up_cut),)
+        up_rest = lambda me, peer: (pl.ds(up_cut, shard - up_cut),)
 
         silu_all = silu_all.reshape(-1, width)
         silu_cols = lax.dynamic_slice_in_dim(silu_all, dp_index * mod_rows, mod_rows, axis=1)
@@ -1022,28 +1093,24 @@
         plan += [
             (hop, 1, lambda me, peer: (peer.dp,), 1, lambda me, peer: (me.dp,), None)
             for hop in DP_HOPS
-            if hop != SELF
         ]
         plan.append((CORE_HOP, 2, None, 2, None, None))
+        plan.append((SELF, 0, to_chip, 0, by_dp, None))
+        plan += [(hop, 3, up_part, 3, by_z, None) for hop in Z_HOPS + [SELF]]
         for number, (dy, dx, dc, dz) in enumerate(PLANE_HOPS):
             from_hop = lambda me, peer, dy=dy, dx=dx: (me.hop(dy, dx, 0, 0).dp,)
             plan.append((CORE_HOP, 0, from_hop, 0, from_hop, (number,)))
         plan.append((CORE_HOP, 0, by_chip, 0, by_dp, None))
-        qkv_slice, mod_parts, proj_other = exchange(
+        qkv_slice, mod_parts, proj_other, up_z_part = exchange(
             2,
-            [qkv_pieces, mod_part, proj_z],
+            [qkv_pieces, mod_part, proj_z, up_weight],
             [
                 ((2 * PLANE, shard, 3 * part_cols), low),
                 (mod_part.shape, full),
                 (proj_z.shape, low),
+                ((z_size, up_cut, up_cols), low),
             ],
             plan,
-        )
-        qkv_slice = put(
-            qkv_slice, lax.dynamic_index_in_dim(qkv_pieces, chip, 0, keepdims=False), dp_index
-        )
-        mod_parts = put(
-            mod_parts, lax.dynamic_index_in_dim(mod_part, dp_index, 0, keepdims=False), dp_index
         )
         qkv_slice = qkv_slice.reshape(-1, 3 * part_cols)
         mod_sum = (jnp.sum(mod_parts, axis=0) + mod_bias.astype(full)).reshape(
@@ -1053,17 +1120,30 @@
             (hop, 0, to_z, 0, lambda me, peer: (me.chip, me.z), None) for hop in Z_HOPS + [SELF]
         ]
         plan += [(hop, 0, by_chip, 0, by_chip, (0, 1, 2, 3)) for hop in PLANE_HOPS]
-        (group_mod,) = exchange(
-            3, [mod_sum], [((PLANE, z_size, slots, mod_cols), full)], plan
+        plan += [(hop, 1, up_rest, 1, by_z, None) for hop in Z_HOPS + [SELF]]
+        group_mod, up_z_rest = exchange(
+            3,
+            [mod_sum, up_weight],
+            [
+                ((PLANE, z_size, slots, mod_cols), full),
+                ((z_size, shard - up_cut, up_cols), low),
+            ],
+            plan,
         )
         group_mod = group_mod.transpose(0, 2, 1, 3).reshape(PLANE, slots, z_size * mod_cols)
         modulation = lax.dynamic_index_in_dim(group_mod, chip, 0, keepdims=False)
 
         units = up_weight.shape[1] // 2
-        up_pieces = whole_call(functools.partial(split_kernel, 2), up_z)
+        up_pieces = whole_call(functools.partial(split_kernel, 2), up_z_part, up_z_rest)
         segments = meta_all[:, 0].reshape(-1)
-        meta_rows = meta_all.transpose(0, 2, 1)
-        seg_col = meta_all[:, 0][:, None, :]
+
+        def in_steps(values):
+            values = xor_order(values, chip, PLANE)
+            return jnp.stack([values[k] for k in (3, 1, 2, 0)])
+
+        meta_steps = in_steps(meta_all)
+        meta_rows = meta_steps.transpose(0, 2, 1)
+        seg_col = meta_steps[:, 0][:, None, :]
         cos_rows, sin_rows = rotary_rows(head_size)
 
         gain_cols = qk_gains.shape[1]
@@ -1081,12 +1161,11 @@
             parts = flat.reshape(groups, PLANE, -1)
             return lax.dynamic_slice_in_dim(parts, chip, 1, axis=1).reshape(-1)
 
-        seg_spans = segments.reshape(PLANE, spans, SPAN)[:, :, 0]
-        hot = (seg_spans[:, :, None] == jnp.arange(slots, dtype=jnp.int32)).astype(full)
-        group_spans = jnp.sum(hot[:, :, :, None] * group_mod[:, None], axis=2)
-        own_spans_ids = segment_ids.reshape(spans, SPAN)[:, 0]
-        own_hot = (own_spans_ids[:, None] == jnp.arange(slots, dtype=jnp.int32)).astype(full)
-        own_spans = jnp.sum(own_hot[:, :, None] * modulation[None], axis=1)
+        assert spans == slots
+        many = (meta_all[:, 0, row_count - 1] != 0)[:, None, None]
+        group_spans = jnp.where(many, group_mod, group_mod[:, :1])
+        own_many = segment_ids[row_count - 1] != 0
+        own_spans = jnp.where(own_many, modulation, modulation[:1])
 
         def spread(values):
             count = values.shape[0]
@@ -1119,7 +1198,7 @@
             return ((parts.shape[0],) + parts.shape[2:], low)
 
         def sum_cores(parts, other):
-            mine = jnp.where(upper, parts[:, 1], parts[:, 0])
+            mine = lax.dynamic_index_in_dim(parts, core, 1, keepdims=False)
             return (mine.astype(full) + other.astype(full)).astype(low)
 
         def own_of(values, index):
@@ -1150,14 +1229,36 @@
             return block_sum(blocks, lax.dynamic_index_in_dim(sent, chip, 0, keepdims=False))
 
         def group_span(k):
-            return group_spans[:, :, None, k * width : (k + 1) * width]
+            return in_steps(group_spans[:, :, None, k * width : (k + 1) * width])
 
         gain_pad = jnp.zeros((2, LANES), full)
         gains = lax.dynamic_update_slice(gain_pad, jnp.stack([gain_q, gain_k]), (0, 0))
-        hidden_one, qkv_rows, attended_low, attn_terms, proj_slice, up_same = block_call(
+        steps = PLANE_HOPS[2:] + PLANE_HOPS[:2]
+        others = (PLANE - 1, row_count, width)
+
+        def in_step(source, out):
+            return [
+                (hop, source, lambda me, peer, k=k: (k,), out, lambda me, peer, k=k: (k,), None)
+                for k, hop in enumerate(steps)
+            ]
+
+        plan = [(hop, 0, to_chip, 0, by_chip, None) for hop in PLANE_HOPS + [SELF]]
+        plan += gather_moves(Z_HOPS + [SELF], 1, 1, by_z)
+        plan += in_step(2, 2)
+        (
+            hidden_one,
+            qkv_rows,
+            attended_low,
+            attn_terms,
+            proj_slice,
+            up_same,
+            down_z,
+            branch_blocks,
+        ) = block_call(
             functools.partial(attention_forward_kernel, head_size, heads),
             [
-                patch_all,
+                patches,
+                patch_blocks.reshape(others),
                 group_span(0),
                 group_span(1),
                 qkv_slice,
@@ -1170,36 +1271,26 @@
                 proj_z,
                 proj_other,
             ],
-            [1, 1, 1, 0, 0, 0, 0, 0, 1, 1, 0, 0],
+            [0, 2, 1, 1, 0, 0, 0, 0, 0, 1, 1, 0, 0],
             [
                 ((PLANE, row_count, width), low),
                 ((PLANE, row_count, 3 * part_cols), full),
                 ((PLANE, row_count, part_cols), low),
-                ((PLANE, row_count, width), low),
-            ],
-            [((part_cols, width), low)],
-            [],
+            ],
+            [((row_count, width), low), ((part_cols, width), low)],
+            [(others, low)],
             PLANE,
             rows_all * width * 8 * part_cols,
             11,
-            [up_pieces],
-            [(up_pieces.shape, low)],
-            [(hop, 0, to_chip, 0, by_chip, None) for hop in PLANE_HOPS + [SELF]],
-        )
-        plan = scatter_plan + gather_moves(Z_HOPS, 1, 1, by_z)
-        plan.append((CORE_HOP, 2, None, 2, None, None))
-        branch_blocks, down_z, up_other = exchange(
-            4,
-            [attn_terms, down_weight, up_same],
-            [
+            [up_pieces, down_weight],
+            [
+                (up_pieces.shape, low),
+                ((z_size,) + down_weight.shape, low),
                 (others, low),
-                ((z_size,) + down_weight.shape, low),
-                (up_same.shape, low),
             ],
             plan,
         )
-        down_z = put(down_z, down_weight, z_index)
-        branch_attn = plane_sum_of(branch_blocks, attn_terms) + proj_vector
+        branch_attn = block_sum(branch_blocks, attn_terms) + proj_vector
 
         patch_full = patches.astype(full)
         scale_one = rms_scale(patch_full)
@@ -1209,15 +1300,13 @@
         normed_two = middle * scale_two
         hidden_two = (normed_two * (1.0 + per_row(4)) + per_row(3)).astype(low)
 
-        hidden_blocks, down_other = exchange(
+        hidden_blocks, down_other, up_other = exchange(
             5,
-            [halves(hidden_two), down_z],
-            [((PLANE - 1, 2, row_count // 2, width), low), (down_z.shape, low)],
-            relayed(0, 0, hop_place, 0) + [(CORE_HOP, 1, None, 1, None, None)],
-        )
-        steps = PLANE_HOPS[2:] + PLANE_HOPS[:2]
-        gate_spans = xor_order(group_spans[:, :, 5 * width :], chip, PLANE)
-        gate_spans = jnp.stack([gate_spans[k] for k in (3, 1, 2, 0)])
+            [halves(hidden_two), down_z, up_same],
+            [((PLANE - 1, 2, row_count // 2, width), low), (down_z.shape, low), (up_same.shape, low)],
+            [(CORE_HOP, k, None, k, None, None) for k in (1, 2)] + relayed(0, 0, hop_place, 2),
+        )
+        gate_spans = in_steps(group_spans[:, :, 5 * width :])
         ffn_terms, own_terms, up_bias_cols, up_parts, down_parts, hidden_two_blocks = block_call(
             ffn_kernel,
             [
@@ -1252,10 +1341,7 @@
             6,
             [],
             [(others, low)],
-            [
-                (hop, 0, lambda me, peer, k=k: (k,), 0, lambda me, peer, k=k: (k,), None)
-                for k, hop in enumerate(steps)
-            ],
+            in_step(0, 0),
         )
         grad_hidden_two = block_sum(hidden_two_blocks, own_terms)
 
@@ -1265,30 +1351,23 @@
         grad_middle = grad_out + norm_backward(
             grad_hidden_two * (1.0 + per_row(4)), normed_two, scale_two
         )
-        grad_gate_attn = grad_middle * branch_attn
         grad_branch_attn = (grad_middle * per_row(2)).astype(low)
         proj_bias_grad = jnp.sum(grad_branch_attn.astype(full), axis=0)
-        grad_branch_all, down_swapped, up_swapped = exchange(
+        grad_branch_blocks, down_swapped, up_swapped = exchange(
             7,
             [halves(grad_branch_attn), down_parts, up_parts],
             [
-                ((PLANE, 2, row_count // 2, width), low),
+                ((PLANE - 1, 2, row_count // 2, width), low),
                 half_of(down_parts),
                 half_of(up_parts),
             ],
-            relayed(0, 0, chip_place, 0)
+            relayed(0, 0, hop_place, 0)
             + core_swap(1, 1, z_size)
             + core_swap(2, 2, PLANE),
         )
         down_mine = sum_cores(down_parts, down_swapped)
         up_mine = sum_cores(up_parts, up_swapped)
-        grad_branch_all = put(
-            grad_branch_all.reshape(PLANE, row_count, width), grad_branch_attn, chip
-        )
-        plan = [
-            (hop, 0, lambda me, peer, k=k: (k,), 0, lambda me, peer, k=k: (k,), None)
-            for k, hop in enumerate(steps)
-        ]
+        plan = in_step(0, 0)
         plan += [(hop, 1, to_chip, 1, by_chip, None) for hop in PLANE_HOPS + [SELF]]
         plan += slotted(Z_HOPS, 2, to_z, 2)
         (
@@ -1303,7 +1382,8 @@
         ) = block_call(
             functools.partial(attention_backward_kernel, head_size, heads),
             [
-                grad_branch_all,
+                grad_branch_attn,
+                grad_branch_blocks.reshape(others),
                 qkv_rows,
                 qkv_slice,
                 gains,
@@ -1315,7 +1395,7 @@
                 hidden_one,
                 attended_low,
             ],
-            [1, 1, 0, 0, 0, 0, 1, 1, 0, 1, 1],
+            [0, 2, 1, 0, 0, 0, 0, 1, 1, 0, 1, 1],
             [((PLANE, row_count, width), low)],
             [
                 ((1, 3 * part_cols), full),
@@ -1337,40 +1417,37 @@
         )
         gain_q_grad, gain_k_grad = gain_grads[0, :head_size], gain_grads[1, :head_size]
         up_wide = whole_call(functools.partial(merge_kernel, 2), up_moved)
-        hidden_one_terms, up_wide = tie(hidden_one_terms, up_wide)
-        up_grad = lax.psum_scatter(up_wide, "fsdp", scatter_dimension=0, tiled=False).astype(full)
-        hidden_one_blocks, qkv_other, proj_other = exchange(
+        to_z_part = lambda me, peer: (peer.z, pl.ds(0, up_cut))
+        to_z_rest = lambda me, peer: (peer.z, pl.ds(up_cut, shard - up_cut))
+        hidden_one_blocks, qkv_other, proj_other, up_blocks = exchange(
             8,
-            [hidden_one_terms, qkv_parts, proj_parts],
-            [(others, low), half_of(qkv_parts), half_of(proj_parts)],
-            scatter_plan + core_swap(1, 1, PLANE) + core_swap(2, 2, z_size),
-        )
-        grad_hidden_one = plane_sum_of(hidden_one_blocks, hidden_one_terms)
-        branch_ffn = block_sum(ffn_blocks, ffn_terms[PLANE - 1]) + down_vector
+            [hidden_one_terms, qkv_parts, proj_parts, up_wide],
+            [
+                (others, low),
+                half_of(qkv_parts),
+                half_of(proj_parts),
+                ((z_size - 1, up_cut, up_cols), low),
+            ],
+            in_step(0, 0)
+            + core_swap(1, 1, PLANE)
+            + core_swap(2, 2, z_size)
+            + slotted(Z_HOPS, 3, to_z_part, 3),
+        )
         down_grad = z_sum_of(down_blocks, down_mine)
-        block_out = (middle + per_row(5) * branch_ffn).astype(low)
-        grad_gate_ffn = grad_out * branch_ffn
         qkv_mine = sum_cores(qkv_parts, qkv_other)
         proj_mine = sum_cores(proj_parts, proj_other)
-        patch_grad = (
-            grad_middle + norm_backward(grad_hidden_one * (1.0 + per_row(1)), normed_one, scale_one)
-        ).astype(low)
-
-        def span_sum(values):
-            return jnp.sum(values.reshape(spans, SPAN, width), axis=1)
-
-        grad_spans = jnp.concatenate(
-            [
-                span_sum(grad_hidden_one),
-                span_sum(grad_hidden_one * normed_one),
-                span_sum(grad_gate_attn),
-                span_sum(grad_hidden_two),
-                span_sum(grad_hidden_two * normed_two),
-                span_sum(grad_gate_ffn),
-            ],
-            axis=1,
-        )
-        grad_modulation = jnp.sum(own_hot[:, :, None] * grad_spans[:, None, :], axis=0).astype(low)
+        patch_grad, block_out, grad_spans = tail_call(
+            [patches, out_cotangent, middle, branch_attn, grad_middle, grad_hidden_two],
+            [hidden_one_blocks, hidden_one_terms, ffn_blocks, ffn_terms],
+            own_spans.reshape(spans, -1, width),
+            down_vector[None],
+        )
+        grad_spans = grad_spans.reshape(spans, -1)
+
+        one_image = jnp.concatenate(
+            [jnp.sum(grad_spans, axis=0, keepdims=True), jnp.zeros_like(grad_spans[1:])], axis=0
+        )
+        grad_modulation = jnp.where(own_many, grad_spans, one_image).astype(low)
         grad_mod = grad_modulation.reshape(slots, z_size, mod_cols).transpose(1, 0, 2)
 
         def place(flat, groups):
@@ -1390,24 +1467,31 @@
             (hop, 1, to_z, 1, lambda me, peer: (me.dp, me.z), None) for hop in Z_HOPS + [SELF]
         ]
         plan += [(hop, 2, to_z, 2, by_z, None) for hop in Z_HOPS + [SELF]]
-        plan += [(hop, 0, to_chip, 0, by_chip, None) for hop in PLANE_HOPS]
+        plan += [(hop, 0, to_chip, 0, by_chip, None) for hop in PLANE_HOPS + [SELF]]
         plan += [(hop, 1, by_dp, 1, by_dp, (0, 1, 2, 3)) for hop in DP_HOPS if hop != SELF]
-        plan += slotted(Z_HOPS, 3, to_z, 3)
-        qkv_moved, grad_mod, vector_parts, proj_blocks = exchange(
+        plan += slotted(Z_HOPS, 3, to_z, 3) + slotted(Z_HOPS, 4, to_z_rest, 4)
+        qkv_moved, grad_mod, vector_parts, proj_blocks, up_rest_blocks = exchange(
             9,
-            [qkv_mine, grad_mod, vector_grad, proj_mine],
+            [qkv_mine, grad_mod, vector_grad, proj_mine, up_wide],
             [
                 (qkv_mine.shape, low),
                 ((2 * PLANE, z_size, slots, mod_cols), low),
                 (vector_grad.shape, full),
                 ((z_size - 1,) + proj_mine.shape[1:], low),
+                ((z_size - 1, shard - up_cut, up_cols), low),
             ],
             plan,
         )
         proj_grad = z_sum_of(proj_blocks, proj_mine)
-        qkv_wide = whole_call(
-            functools.partial(merge_kernel, 3), put(qkv_moved, own_of(qkv_mine, chip), chip)
-        )
+        up_own = own_of(up_wide, z_index)
+        up_grad = jnp.concatenate(
+            [
+                block_sum(up_blocks, up_own[:up_cut]),
+                block_sum(up_rest_blocks, up_own[up_cut:]),
+            ],
+            axis=0,
+        )
+        qkv_wide = whole_call(functools.partial(merge_kernel, 3), qkv_moved)
         grad_mod = grad_mod.reshape(-1, mod_cols)
         vector_sum = jnp.sum(vector_parts, axis=0)
         cond_part = dot_t(grad_mod, mod_weight).reshape(2 * PLANE, z_size, slots, mod_rows)

time: 517 us -> 459 us (0.89); the launches traced: 507 us -> 458 us
  local copies, waits for them, and re-layouts: 40.3 us -> 18.8 us
  other arithmetic: 57.9 us -> 37 us
  between operations: 15.1 us -> 2.06 us
  Pallas kernels: 389 us -> 396 us
    pallas_call x3, Pallas kernels: 124 us -> 148 us  [block_call(): pl.pallas_call(body, grid=(steps,), out_shape=[jax.ShapeDtypeStruct(*o) f...]
    pallas_call x9 -> x8, Pallas kernels: 255 us -> 231 us  [exchange(): pl.pallas_call(kernel, out_shape=[jax.ShapeDtypeStruct(shape, dtype) for...]
    dynamic_update_slice x8 -> x0, local copies, waits for them, and re-layouts: 8.84 us -> none  [put(): lax.dynamic_update_slice(values, own.reshape((1,) * len(at) + own.shape),...]
    unnamed x87 -> x68, local copies, waits for them, and re-layouts: 11.1 us -> 2.75 us
    reduce_sum x6 -> x1, other arithmetic: 7.61 us -> 0.02 us  [per_device(): jnp.sum(grad_spans, axis=0, keepdims=True)]
    convert_element_type x5 -> x1, other arithmetic: 6.69 us -> 0.04 us  [per_device(): grad_modulation = jnp.where(own_many, grad_spans, one_image).astype(low)]
    pallas_call x4 -> x5, Pallas kernels: 10.7 us -> 17.1 us  [the longest x4 10.6 us: whole_call(): pl.pallas_call(kernel, out_shape=jax.ShapeDtypeStruct((count, rows, cols)...]
  transfers between devices with their start and end apart: 2 -> 0, of which waited for: 0 -> 0; matrix products, arithmetic and copies ran while one was open for 11% -> 0% of each run, Pallas kernels for 21% -> 0%
where the time goes in v5:
time: 459 us; the launch traced here: 458 us
  Pallas kernels  396 us (86%)
  other arithmetic  37 us (8%)
  local copies, waits for them, and re-layouts  18.8 us (4%)
    pallas_call x8, Pallas kernels, exchange(): pl.pallas_call(kernel, out_shape=[jax.ShapeDtypeStruct(shape, dtype) for...  231 us
    pallas_call x3, Pallas kernels, block_call(): pl.pallas_call(body, grid=(steps,), out_shape=[jax.ShapeDtypeStruct(*o) f...  148 us
    pallas_call x4, Pallas kernels, whole_call(): pl.pallas_call(kernel, out_shape=jax.ShapeDtypeStruct((count, rows, cols)...  10.6 us

profile of v5, /device:TPU:0, one launch (start us, length us, event | category | flops | bytes accessed | tf_op | source)
XLA Modules:
  0.0 457.8 jit_solution(13640499700782930306)
XLA Ops:
  0.7 1.4 fusion.21.refs_0_
  2.0 0.7 slice_bitcast_fusion
  2.8 2.8 concatenate.15
  5.6 0.6 broadcast_in_dim.50.refs_4_
  6.2 1.3 pad_add_fusion.1.refs_5_
  7.5 52.6 %shard_map.281 = (bf16[8,4,4,1152]{3,2,1,0:T(4,128)(2,1)}, bf16[4,144,864]{2,1,0:T(8,128)(2,1)}, bf16[3,2,128,1152]{3,2,1,0:T(8,128)(2,1)}, bf16[4,144,288]{2,1,...) custom-call(bf16[4,1152]{1,0:T(4,128)(2,1)} %fusion.21.refs_0_, ...), custom_call_target="tpu_custom_call" | custom-call | tf_op jit(solution)/shard_map/pallas_call | solution.py:527
  60.1 2.5 shard_map.282.refs_0_
  62.7 1.3 fusion.16
  64.0 24.7 %shard_map.283 = (bf16[8,144,864]{2,1,0:T(8,128)(2,1)}, f32[8,16,1728]{2,1,0:T(8,128)}, bf16[4,144,288]{2,1,0:T(8,128)(2,1)}, bf16[4,96,1536]{2,1,0:T(8,128)(2,1)}) custom-call(bf16[4,144,864]{2,1,0:T(8,128)(2,1)} %shard_map.282.refs_0_, f32[8,16,1728]{2,1,0:T(8,128)} %bitcast.125, bf16[4,144,288]{2,1,0:T(8,128)(2,1)} %get-tuple-element.72.refs_2_.refs_11_, ...), custom_call_target="tpu_custom_call" | custom-call | tf_op jit(solution)/shard_map/pallas_call | solution.py:527
  88.7 1.2 reduce_sum.159
  90.0 0.7 broadcast_add_fusion.refs_0_
  90.7 21.6 %shard_map.284 = (f32[4,4,4,1728]{3,2,1,0:T(4,128)}, bf16[4,48,1536]{2,1,0:T(8,128)(2,1)}) custom-call(f32[4,4,1728]{2,1,0:T(4,128)} %broadcast_add_fusion.refs_0_, bf16[144,1536]{1,0:T(8,128)(2,1)} %refs_1_.4), custom_call_target="tpu_custom_call" | custom-call | tf_op jit(solution)/shard_map/pallas_call | solution.py:527
  112.3 1.2 copy.73
  114.0 0.6 slice.153
  116.5 0.7 pad_maximum_fusion.1.refs_2_
  117.2 0.7 pad_maximum_fusion.2.refs_3_
  118.1 0.7 broadcast_in_dim_reshape.10.refs_5_
  119.6 1.0 copy.79.refs_9_.refs_7_
  120.6 0.6 slice.215.refs_10_.refs_8_
  121.2 2.8 shard_map.285.refs_13_
  124.0 0.9 copy.80.refs_14_
  124.9 51.0 %shard_map.286 = (bf16[4,256,1152]{2,1,0:T(8,128)(2,1)}, f32[4,256,864]{2,1,0:T(8,128)}, bf16[4,256,288]{2,1,0:T(8,128)(2,1)}, bf16[256,1152]{1,0:T(8,128)(2,1)}...) custom-call(bf16[256,1152]{1,0:T(8,128)(2,1)} %refs_0_.3, ...), custom_call_target="tpu_custom_call" | custom-call | flops 2717908992 | bytes 5214592 | tf_op jit(solution)/shard_map/pallas_call | solution.py:979
  176.0 1.9 convert_reduce_fusion.1
  177.9 1.4 multiply_reduce_fusion.1
  179.3 1.2 fusion.7.refs_0_
  180.5 22.2 %shard_map.287 = (bf16[3,2,128,1152]{3,2,1,0:T(8,128)(2,1)}, bf16[4,384,288]{2,1,0:T(8,128)(2,1)}, bf16[4,144,1536]{2,1,0:T(8,128)(2,1)}) custom-call(bf16[2,128,1152]{2,1,0:T(8,128)(2,1)} %bitcast.127, bf16[4,384,288]{2,1,0:T(8,128)(2,1)} %get-tuple-element.84.refs_1_.refs_7_, bf16[4,144,1536]{2,1,0:T(8,128)(2,1)} %get-tuple-element.85.refs_2_.refs_5_), custom_call_target="tpu_custom_call" | custom-call | tf_op jit(solution)/shard_map/pallas_call | solution.py:527
  202.8 0.7 broadcast_in_dim.97.refs_4_
  203.5 0.6 constant_dynamic-slice_fusion
  204.1 43.9 %shard_map.288 = (bf16[4,256,1152]{2,1,0:T(8,128)(2,1)}, bf16[256,1152]{1,0:T(8,128)(2,1)}, f32[1,1536]{1,0:T(1,128)}, bf16[4,2,144,1536]{3,2,1,0:T(8,128)(2,1)}...) custom-call(bf16[256,1152]{1,0:T(8,128)(2,1)} %fusion.7.refs_0_, bf16[3,256,1152]{2,1,0:T(8,128)(2,1)} %bitcast.165, ...), custom_call_target="tpu_custom_call" | custom-call | flops 16307453952 | bytes 10106880 | tf_op jit(solution)/shard_map/pallas_call | solution.py:979
  248.0 1.9 convert_reduce_fusion
  250.4 0.7 copy-done.5
  251.0 1.8 convert_reduce_fusion.6
  252.8 22.0 %shard_map.289 = (bf16[3,2,128,1152]{3,2,1,0:T(8,128)(2,1)}, bf16[4,384,288]{2,1,0:T(8,128)(2,1)}, bf16[4,144,1536]{2,1,0:T(8,128)(2,1)}) custom-call(bf16[2,128,1152]{2,1,0:T(8,128)(2,1)} %bitcast.126, bf16[4,2,384,288]{3,2,1,0:T(8,128)(2,1)} %get-tuple-element.92.refs_1_, bf16[4,2,144,1536]{3,2,1,0:T(8,128)(2,1)} %get-tuple-element.93.refs_2_), custom_call_target="tpu_custom_call" | custom-call | tf_op jit(solution)/shard_map/pallas_call | solution.py:527
  274.9 3.8 fusion.refs_13_
  278.7 1.3 fusion.1.refs_14_
  280.0 52.7 %shard_map.290 = (bf16[4,256,1152]{2,1,0:T(8,128)(2,1)}, f32[1,864]{1,0:T(1,128)}, f32[2,128]{1,0:T(2,128)}, bf16[4,2,144,864]{3,2,1,0:T(8,128)(2,1)}, bf16[4,2,...) custom-call(bf16[256,1152]{1,0:T(8,128)(2,1)} %get-tuple-element.173, ...), custom_call_target="tpu_custom_call" | custom-call | flops 6115295232 | bytes 11551744 | tf_op jit(solution)/shard_map/pallas_call | solution.py:979
  332.7 2.8 shard_map.291.refs_3_.refs_4_
  335.5 28.1 %shard_map.292 = (bf16[3,256,1152]{2,1,0:T(8,128)(2,1)}, bf16[4,144,864]{2,1,0:T(8,128)(2,1)}, bf16[4,144,288]{2,1,0:T(8,128)(2,1)}, bf16[3,96,1536]{2,1,0:T(8,128)(2,1)}) custom-call(bf16[4,256,1152]{2,1,0:T(8,128)(2,1)} %get-tuple-element.102.refs_0_.refs_7_, bf16[4,2,144,864]{3,2,1,0:T(8,128)(2,1)} %get-tuple-element.103.refs_1_, ...), custom_call_target="tpu_custom_call" | custom-call | tf_op jit(solution)/shard_map/pallas_call | solution.py:527
  363.6 0.7 broadcast_select_fusion.5.refs_10_
  364.3 0.7 broadcast_in_dim_reshape.12.refs_11_
  365.0 6.6 %shard_map.293 = (bf16[256,1152]{1,0:T(8,128)(2,1)}, bf16[256,1152]{1,0:T(8,128)(2,1)}, f32[4,6,1152]{2,1,0:T(8,128)}) custom-call(bf16[256,1152]{1,0:T(8,128)(2,1)} %refs_0_.3, bf16[256,1152]{1,0:T(8,128)(2,1)} %refs_1_.5, f32[256,1152]{1,0:T(8,128)} %copy-done.1, f32[256,1152]{1,0:T(8,128)} %get-tuple-element.179.refs_3_, ...), custom_call_target="tpu_custom_call" | custom-call | tf_op jit(solution)/shard_map/pallas_call | solution.py:915
  371.6 2.5 fusion.2.refs_0_
  374.4 0.6 copy.112
  375.9 0.8 concatenate.18.refs_2_
  376.6 0.9 fusion.8.refs_3_
  377.5 28.1 %shard_map.294 = (bf16[4,144,864]{2,1,0:T(8,128)(2,1)}, bf16[8,4,4,1728]{3,2,1,0:T(4,128)(2,1)}, f32[4,1,3012]{2,1,0:T(1,128)}, bf16[3,144,288]{2,1,0:T(8,128)(2,1)}, bf16[3,48,1536]{2,1,0:T(8,128)(2,1)}) custom-call(bf16[4,144,864]{2,1,0:T(8,128)(2,1)} %fusion.2.refs_0_, bf16[4,4,1728]{2,1,0:T(4,128)(2,1)} %bitcast.140, f32[4,1,3012]{2,1,0:T(1,128)} %concatenate.18.refs_2_, ...), custom_call_target="tpu_custom_call" | custom-call | tf_op jit(solution)/shard_map/pallas_call | solution.py:527
  405.6 2.5 shard_map.295.refs_0_
  408.1 1.1 fusion.9.refs_1_
  409.2 0.6 reduce_sum.168
  409.8 32.2 %shard_map.296 = (bf16[3,144,864]{2,1,0:T(8,128)(2,1)}, f32[8,4,4,144]{3,2,1,0:T(4,128)}, f32[8,1,3012]{2,1,0:T(1,128)}) custom-call(bf16[4,144,864]{2,1,0:T(8,128)(2,1)} %shard_map.295.refs_0_, f32[8,4,4,144]{3,2,1,0:T(4,128)} %fusion.9.refs_1_, f32[1,3012]{1,0:T(1,128)} %bitcast.155), custom_call_target="tpu_custom_call" | custom-call | tf_op jit(solution)/shard_map/pallas_call | solution.py:527
  442.0 0.9 reduce_sum.170
  443.1 0.6 fusion.25
  443.9 1.4 fusion.14
  445.3 0.8 convert_reduce_fusion.7
  446.3 1.9 convert_add_fusion.8
  448.2 0.6 slice_reduce_fusion.1
  449.5 1.7 convert_add_fusion.10
  451.2 0.7 slice_reduce_fusion.2
  451.9 1.0 convert_add_fusion.9
  453.0 1.0 convert_add_fusion.7
  454.1 1.0 pad_maximum_fusion
  455.0 0.6 slice_reduce_fusion
  455.8 1.0 convert_add_fusion.6
  456.8 1.0 copy.91
  (139 shorter events, 5.9 us)
Async XLA Ops:
  0.6 62.1 %copy-start = (bf16[144,1728]{1,0:T(8,128)(2,1)S(1)}, bf16[144,1728]{1,0:T(8,128)(2,1)}, u32[]{:S(2)}) copy-start(bf16[144,1728]{1,0:T(8,128)(2,1)} %param.22) | copy-start | bytes 1492996
  60.1 2.5 copy-start.19
  88.7 1.3 copy-start.27
  90.7 23.3 %copy-start.29 = (s32[256]{0:T(256)S(1)}, s32[256]{0:T(256)}, u32[]{:S(2)}) copy-start(s32[256]{0:T(256)} %param.20) | copy-start | bytes 3076
  112.3 3.0 copy-start.22
  113.5 2.2 copy-start.25
  121.2 2.8 copy-start.20
  175.9 2.0 copy-start.4
  175.9 2.0 copy-start.13
  179.3 71.1 %copy-start.1 = (f32[256,1152]{1,0:T(8,128)}, f32[256,1152]{1,0:T(8,128)S(1)}, u32[]{:S(2)}) copy-start(f32[256,1152]{1,0:T(8,128)S(1)} %get-tuple-element.178.refs_2_) | copy-start | bytes 3538948
  248.0 1.9 copy-start.14
  250.0 1.1 copy-start.5
  250.4 2.5 copy-start.2
  274.8 3.8 copy-start.3
  274.9 3.8 copy-start.9
  365.0 6.6 %copy-start.6 = (bf16[4,2,144,864]{3,2,1,0:T(8,128)(2,1)S(1)}, bf16[4,2,144,864]{3,2,1,0:T(8,128)(2,1)}, u32[]{:S(2)}) copy-start(bf16[4,2,144,864]{3,2,1,0:T(8,128)(2,1)} %get-tuple-element.103.refs_1_) | copy-start | bytes 5971972
  371.6 2.5 copy-start.15
  371.6 3.5 copy-start.28
  371.6 3.8 copy-start.26
  371.6 4.0 copy-start.30
  371.6 5.0 %copy-start.16 = (bf16[4,144,288]{2,1,0:T(8,128)(2,1)S(1)}, bf16[4,144,288]{2,1,0:T(8,128)(2,1)}, u32[]{:S(2)}) copy-start(bf16[4,144,288]{2,1,0:T(8,128)(2,1)} %get-tuple-element.115) | copy-start | bytes 995332
  374.1 2.5 copy-start.7
  405.6 2.5 copy-start.8
  408.1 1.1 copy-start.23
  408.1 35.0 %copy-start.24 = (bf16[4,1152]{1,0:T(4,128)(2,1)S(1)}, bf16[4,1152]{1,0:T(4,128)(2,1)}, u32[]{:S(2)}) copy-start(bf16[4,1152]{1,0:T(4,128)(2,1)} %param.19) | copy-start | bytes 27652
  443.9 2.2 copy-start.12
  446.1 2.0 copy-start.21
  446.1 3.3 copy-start.18
  446.2 5.6 %copy-start.17 = (bf16[3,48,1536]{2,1,0:T(8,128)(2,1)S(1)}, bf16[3,48,1536]{2,1,0:T(8,128)(2,1)}, u32[]{:S(2)}) copy-start(bf16[3,48,1536]{2,1,0:T(8,128)(2,1)} %get-tuple-element.124) | copy-start | bytes 1327108
  449.5 3.4 copy-start.11
  454.1 1.6 copy-start.10

commit v6 on v5

--- a/solution.py
+++ b/solution.py
@@ -509,19 +509,80 @@
                 self.copy(number).wait_send()
 
 
-def exchange(identity, inputs, out_shapes, plan):
+def exchange(identity, inputs, out_shapes, plan, chains=()):
+    near, across = (0, 0, 0, 1), (0, 0, 0, 3)
+    moves = list(plan)
+    for source, out in chains:
+        first = len(moves)
+        moves += [
+            (near, source, None, out, by_z, None),
+            (across, source, None, out, by_z, None),
+            (across, out, lambda me, peer: (me.hop(*near).z,), out, lambda me, peer: (me.hop(*near).z,), (first,)),
+            (near, out, lambda me, peer: (me.hop(*across).z,), out, lambda me, peer: (me.hop(*across).z,), (first + 1,)),
+            (near, out, lambda me, peer: (me.hop(0, 0, 0, 2).z,), out, lambda me, peer: (me.hop(0, 0, 0, 2).z,), (first + 2,)),
+        ]
+
     def kernel(*refs):
         ins, outs = refs[: len(inputs)], refs[len(inputs) : len(inputs) + len(out_shapes)]
-        copies = Copies(plan, ins, outs, *refs[-2:])
+        copies = Copies(moves, ins, outs, *refs[-2:])
         copies.greet()
+        z_index = lax.axis_index("fsdp")
+        middle = (z_index + 1) // 2 == 1
+        firsts = [len(plan) + 5 * k for k in range(len(chains))]
+        for first in firsts:
+            copies.start(first)
+        if chains:
+
+            @pl.when(middle)
+            def _():
+                for first in firsts:
+                    copies.start(first + 1)
+
         done = set()
+
+        def follow(wanted):
+            for number in wanted:
+                for earlier in plan[number][5]:
+                    if earlier not in done:
+                        copies.wait_arrival(earlier)
+                        done.add(earlier)
+                copies.start(number)
+
+        later = [number for number, move in enumerate(plan) if move[5] is not None]
         for number, move in enumerate(plan):
-            for earlier in move[5] or ():
-                if earlier not in done:
-                    copies.wait_arrival(earlier)
-                    done.add(earlier)
-            copies.start(number)
-        copies.finish(done)
+            if move[5] is None:
+                copies.start(number)
+        follow(later[: len(later) // 2])
+        if chains:
+
+            @pl.when(middle)
+            def _():
+                for step in range(3):
+                    for first in firsts:
+                        copies.wait_arrival(first + step)
+                        copies.start(first + step + 2)
+
+        follow(later[len(later) // 2 :])
+        for number, move in enumerate(plan):
+            if number not in done:
+                copies.wait_arrival(number)
+            if move[0] != SELF:
+                copies.copy(number).wait_send()
+        for first in firsts:
+            copies.copy(first).wait_send()
+        if chains:
+
+            @pl.when(middle)
+            def _():
+                for first in firsts:
+                    for step in range(1, 5):
+                        copies.copy(first + step).wait_send()
+
+            @pl.when(jnp.logical_not(middle))
+            def _():
+                for first in firsts:
+                    for step in (0, 3, 4):
+                        copies.wait_arrival(first + step)
 
     anywhere = pl.BlockSpec(memory_space=pl.ANY)
     return pl.pallas_call(
@@ -530,8 +591,8 @@
         in_specs=[anywhere] * len(inputs),
         out_specs=[anywhere] * len(out_shapes),
         scratch_shapes=[
-            pltpu.SemaphoreType.DMA((len(plan),)),
-            pltpu.SemaphoreType.DMA((len(plan),)),
+            pltpu.SemaphoreType.DMA((len(moves),)),
+            pltpu.SemaphoreType.DMA((len(moves),)),
         ],
         compiler_params=pltpu.CompilerParams(collective_id=identity, has_side_effects=True),
     )(*inputs)
@@ -808,17 +869,18 @@
 def ffn_kernel(copies, rest, *refs):
     (own_hidden, hiddens, own_cot, cots, gate, up_mine, up_other) = refs[:7]
     (down_mine, down_other, bias) = refs[7:10]
-    ffn_terms, hidden_terms, bias_out, up_parts, down_parts = refs[10:15]
-    down, up, up_total, down_total, terms = refs[15:]
+    hidden_terms, bias_out, ffn_terms, up_parts, down_parts = refs[10:15]
+    down, up, terms, all_hidden, all_branch, all_gated, all_grads = refs[15:]
     copies.ins = [terms]
     step = pl.program_id(0)
+    count, width = own_hidden.shape
+    units = down.shape[0]
+    last = PLANE - 1
 
     @pl.when(step == 0)
     def _():
+        copies.greet()
         bias_out[...] = jnp.zeros_like(bias_out)
-        up_total[...] = jnp.zeros_like(up_total)
-        down_total[...] = jnp.zeros_like(down_total)
-        copies.greet()
         fill_rows(down, down_mine, down_other)
         rows = up_mine.shape[1]
         core = lax.axis_index("dp") % 2
@@ -827,48 +889,58 @@
                 at = pl.multiple_of((2 * p + place) * rows, 16)
                 up[pl.ds(at, rows), :] = source[p]
 
-    count, width = own_hidden.shape
-    last = pl.num_programs(0) - 1
-    units = down.shape[0]
-    hidden = jnp.where(step == last, own_hidden[...], hiddens[0])
-    cot = jnp.where(step == last, own_cot[...], cots[0])
-    grad_branch = cot.astype(full).reshape(count // SPAN, SPAN, width) * gate[0]
-    grad_branch = grad_branch.reshape(count, width).astype(low)
-    grad_gated = dot_t(grad_branch, down[...])
-    gate_up = dot(hidden, up[...]) + bias[...]
-    gate_part, up_part = gate_up[:, :units], gate_up[:, units:]
-    sigmoid = jax.nn.sigmoid(gate_part)
-    silu = gate_part * sigmoid
-    gated = (silu * up_part).astype(low)
-    slope = sigmoid * (1.0 + gate_part * (1.0 - sigmoid))
-    grad_gate = (grad_gated * up_part * slope).astype(low)
-    grad_up = (grad_gated * silu).astype(low)
-    grads = jnp.concatenate([grad_gate, grad_up], axis=1)
-    bias_out[...] += jnp.sum(grads.astype(full), axis=0, keepdims=True)
-
-    for number in range(PLANE - 1):
-        @pl.when(step == number + 1)
-        def _(number=number):
-            copies.start(number)
-
-    hidden_term = dot_t(grads, up[...]).astype(low)
-
-    @pl.when(step < last)
+    @pl.when(step < PLANE)
     def _():
-        terms[step] = hidden_term
-
-    @pl.when(step == last)
+        here = pl.ds(pl.multiple_of(step * count, count), count)
+        hidden = jnp.where(step == last, own_hidden[...], hiddens[0])
+        cot = jnp.where(step == last, own_cot[...], cots[0])
+        grad_branch = cot.astype(full).reshape(count // SPAN, SPAN, width) * gate[0]
+        grad_branch = grad_branch.reshape(count, width).astype(low)
+        all_hidden[here, :] = hidden
+        all_branch[here, :] = grad_branch
+        grad_gated = dot_t(grad_branch, down[...])
+        gate_up = dot(hidden, up[...]) + bias[...]
+        gate_part, up_part = gate_up[:, :units], gate_up[:, units:]
+        sigmoid = jax.nn.sigmoid(gate_part)
+        silu = gate_part * sigmoid
+        all_gated[here, :] = (silu * up_part).astype(low)
+        slope = sigmoid * (1.0 + gate_part * (1.0 - sigmoid))
+        grad_gate = (grad_gated * up_part * slope).astype(low)
+        grad_up = (grad_gated * silu).astype(low)
+        grads = jnp.concatenate([grad_gate, grad_up], axis=1)
+        all_grads[here, :] = grads
+        bias_out[...] += jnp.sum(grads.astype(full), axis=0, keepdims=True)
+
+        for number in range(PLANE - 1):
+            @pl.when(step == number + 1)
+            def _(number=number):
+                copies.start(number)
+
+        hidden_term = dot_t(grads, up[...]).astype(low)
+
+        @pl.when(step < last)
+        def _():
+            terms[step] = hidden_term
+
+        @pl.when(step == last)
+        def _():
+            hidden_terms[...] = hidden_term
+
+    @pl.when(step == PLANE)
     def _():
-        hidden_terms[...] = hidden_term
-
-    ffn_terms[0] = dot(gated, down[...]).astype(low)
-    up_total[...] += outer_grad(hidden, grads)
-    down_total[...] += outer_grad(gated, grad_branch)
-
-    @pl.when(step == pl.num_programs(0) - 1)
-    def _():
-        up_parts[...] = up_total[...].astype(low).reshape(up_parts.shape)
-        cut_columns(down_parts, down_total[...])
+        @pl.loop(0, PLANE)
+        def _(k):
+            rows = pl.ds(pl.multiple_of(k * count, count), count)
+            ffn_terms[k] = dot(all_gated[rows, :], down[...]).astype(low)
+
+        cut = width // 3
+
+        @pl.loop(0, 3)
+        def _(k):
+            part = pl.ds(pl.multiple_of(k * cut, 128), cut)
+            up_parts[part, :] = outer_grad(all_hidden[:, part], all_grads[...]).astype(low)
+
+        cut_columns(down_parts, outer_grad(all_gated[...], all_branch[...]))
         copies.finish()
 
 
@@ -961,7 +1033,7 @@
         tail = (0,) * (len(shape) - 1)
         if mark == 2:
             return pl.BlockSpec((1,) + shape[1:], lambda p: ((p + 2) % 3,) + tail)
-        return pl.BlockSpec((1,) + shape[1:], lambda p: (p,) + tail)
+        return pl.BlockSpec((1,) + shape[1:], lambda p: (jnp.minimum(p, shape[0] - 1),) + tail)
 
     def whole_spec(shape):
         return pl.BlockSpec(shape, lambda p: (0,) * len(shape))
@@ -1048,14 +1120,12 @@
         cols_qkv = qkv_weight.shape[1]
         cols_proj = proj_weight.shape[1]
         plan = gather_moves(Z_HOPS + [SELF], 0, 0, lambda me, peer: (me.dp, me.z))
-        plan += gather_moves(Z_HOPS + [SELF], 1, 1, by_z)
-        plan += gather_moves(Z_HOPS + [SELF], 3, 3, by_z)
+        plan += [(SELF, k, None, k, by_z, None) for k in (1, 3)]
         plan += gather_moves(Z_HOPS + [SELF], 4, 4, by_z)
         plan += gather_moves(PLANE_HOPS + [SELF], 5, 5, by_chip)
         plan += [(hop, 0, by_dp, 0, by_dp, (0, 1, 2, 3)) for hop in DP_HOPS if hop != SELF]
         plan += relayed(2, 2, hop_place, len(plan))
-        plan += relayed(6, 6, hop_place, len(plan))
-        silu_all, qkv_z, patch_blocks, proj_z, vectors, meta_all, cot_blocks = exchange(
+        silu_all, qkv_z, patch_blocks, proj_z, vectors, meta_all = exchange(
             1,
             [
                 silu_low,
@@ -1064,7 +1134,6 @@
                 proj_weight,
                 vector,
                 meta,
-                halves(out_cotangent),
             ],
             [
                 ((2 * PLANE, z_size, slots, width), low),
@@ -1073,9 +1142,9 @@
                 ((z_size, shard, cols_proj), low),
                 ((z_size,) + vector.shape, low),
                 ((PLANE,) + meta.shape, jnp.int32),
-                ((PLANE - 1, 2, row_count // 2, width), low),
             ],
             plan,
+            [(1, 1), (3, 3)],
         )
 
         up_cut = shard // 48 * 32
@@ -1121,12 +1190,14 @@
         ]
         plan += [(hop, 0, by_chip, 0, by_chip, (0, 1, 2, 3)) for hop in PLANE_HOPS]
         plan += [(hop, 1, up_rest, 1, by_z, None) for hop in Z_HOPS + [SELF]]
-        group_mod, up_z_rest = exchange(
+        plan += relayed(2, 2, hop_place, len(plan))
+        group_mod, up_z_rest, cot_blocks = exchange(
             3,
-            [mod_sum, up_weight],
+            [mod_sum, up_weight, halves(out_cotangent)],
             [
                 ((PLANE, z_size, slots, mod_cols), full),
                 ((z_size, shard - up_cut, up_cols), low),
+                ((PLANE - 1, 2, row_count // 2, width), low),
             ],
             plan,
         )
@@ -1307,7 +1378,7 @@
             [(CORE_HOP, k, None, k, None, None) for k in (1, 2)] + relayed(0, 0, hop_place, 2),
         )
         gate_spans = in_steps(group_spans[:, :, 5 * width :])
-        ffn_terms, own_terms, up_bias_cols, up_parts, down_parts, hidden_two_blocks = block_call(
+        own_terms, up_bias_cols, ffn_terms, up_parts, down_parts, hidden_two_blocks = block_call(
             ffn_kernel,
             [
                 hidden_two,
@@ -1322,27 +1393,31 @@
                 own_columns(up_vector, 2)[None],
             ],
             [0, 2, 0, 2, 1, 0, 0, 0, 0, 0],
-            [((PLANE, row_count, width), low)],
+            [],
             [
                 ((row_count, width), low),
                 ((1, 2 * units), full),
-                ((PLANE, 2, shard, 2 * units), low),
+                ((PLANE, row_count, width), low),
+                ((width, 2 * units), low),
                 ((z_size, 2) + down_weight.shape, low),
             ],
             [
                 ((units, width), low),
                 ((width, 2 * units), low),
-                ((width, 2 * units), full),
-                ((units, width), full),
                 (others, low),
-            ],
-            PLANE,
+                ((rows_all, width), low),
+                ((rows_all, width), low),
+                ((rows_all, units), low),
+                ((rows_all, 2 * units), low),
+            ],
+            PLANE + 1,
             rows_all * width * 18 * units,
             6,
             [],
             [(others, low)],
             in_step(0, 0),
         )
+        up_parts = up_parts.reshape(PLANE, 2, shard, 2 * units)
         grad_hidden_two = block_sum(hidden_two_blocks, own_terms)
 
         grad_out = out_cotangent.astype(full)

time: 459 us -> 450 us (0.980)
  Pallas kernels: 396 us -> 387 us
    pallas_call x8, Pallas kernels: 231 us -> 224 us  [exchange(): pl.pallas_call(kernel, out_shape=[jax.ShapeDtypeStruct(shape, dtype) for...]
where the time goes in v6:
time: 450 us; the launch traced here: 449 us
  Pallas kernels  387 us (86%)
  other arithmetic  37 us (8%)
  local copies, waits for them, and re-layouts  18.8 us (4%)
    pallas_call x8, Pallas kernels, exchange(): pl.pallas_call(kernel, out_shape=[jax.ShapeDtypeStruct(shape, dtype) for...  224 us
    pallas_call x3, Pallas kernels, block_call(): pl.pallas_call(body, grid=(steps,), out_shape=[jax.ShapeDtypeStruct(*o) f...  146 us
    pallas_call x4, Pallas kernels, whole_call(): pl.pallas_call(kernel, out_shape=jax.ShapeDtypeStruct((count, rows, cols)...  10.6 us

profile of v6, /device:TPU:0, one launch (start us, length us, event | category | flops | bytes accessed | tf_op | source)
XLA Modules:
  0.0 448.8 jit_solution(11362658565853085418)
XLA Ops:
  0.7 1.4 fusion.21.refs_0_
  2.0 0.7 slice_bitcast_fusion
  2.8 2.8 concatenate.15
  5.6 0.6 broadcast_in_dim.50.refs_4_
  6.2 1.3 pad_add_fusion.1.refs_5_
  7.5 34.5 %shard_map.281 = (bf16[8,4,4,1152]{3,2,1,0:T(4,128)(2,1)}, bf16[4,144,864]{2,1,0:T(8,128)(2,1)}, bf16[3,2,128,1152]{3,2,1,0:T(8,128)(2,1)}, bf16[4,144,288]{2,1,...) custom-call(bf16[4,1152]{1,0:T(4,128)(2,1)} %fusion.21.refs_0_, bf16[144,864]{1,0:T(8,128)(2,1)} %refs_1_.3, ...), custom_call_target="tpu_custom_call" | custom-call | tf_op jit(solution)/shard_map/pallas_call | solution.py:588
  42.1 2.5 shard_map.282.refs_0_
  44.6 1.3 fusion.16
  45.9 24.9 %shard_map.283 = (bf16[8,144,864]{2,1,0:T(8,128)(2,1)}, f32[8,16,1728]{2,1,0:T(8,128)}, bf16[4,144,288]{2,1,0:T(8,128)(2,1)}, bf16[4,96,1536]{2,1,0:T(8,128)(2,1)}) custom-call(bf16[4,144,864]{2,1,0:T(8,128)(2,1)} %shard_map.282.refs_0_, f32[8,16,1728]{2,1,0:T(8,128)} %bitcast.130, bf16[4,144,288]{2,1,0:T(8,128)(2,1)} %get-tuple-element.72.refs_2_.refs_11_, ...), custom_call_target="tpu_custom_call" | custom-call | tf_op jit(solution)/shard_map/pallas_call | solution.py:588
  70.9 1.2 reduce_sum.159
  72.2 0.7 broadcast_add_fusion.refs_0_
  72.8 32.4 %shard_map.284 = (f32[4,4,4,1728]{3,2,1,0:T(4,128)}, bf16[4,48,1536]{2,1,0:T(8,128)(2,1)}, bf16[3,2,128,1152]{3,2,1,0:T(8,128)(2,1)}) custom-call(f32[4,4,1728]{2,1,0:T(4,128)} %broadcast_add_fusion.refs_0_, bf16[144,1536]{1,0:T(8,128)(2,1)} %refs_1_.4, bf16[2,128,1152]{2,1,0:T(8,128)(2,1)} %bitcast.129), custom_call_target="tpu_custom_call" | custom-call | tf_op jit(solution)/shard_map/pallas_call | solution.py:588
  105.2 1.2 copy.73
  107.0 0.6 slice.153
  109.4 0.7 pad_maximum_fusion.1.refs_2_
  110.2 0.7 pad_maximum_fusion.2.refs_3_
  111.0 0.7 broadcast_in_dim_reshape.10.refs_5_
  112.6 1.0 copy.79.refs_9_.refs_7_
  113.6 0.6 slice.215.refs_10_.refs_8_
  114.2 2.8 shard_map.285.refs_13_
  117.0 0.9 copy.80.refs_14_
  117.9 51.8 %shard_map.286 = (bf16[4,256,1152]{2,1,0:T(8,128)(2,1)}, f32[4,256,864]{2,1,0:T(8,128)}, bf16[4,256,288]{2,1,0:T(8,128)(2,1)}, bf16[256,1152]{1,0:T(8,128)(2,1)}...) custom-call(bf16[256,1152]{1,0:T(8,128)(2,1)} %refs_0_.3, ...), custom_call_target="tpu_custom_call" | custom-call | flops 2717908992 | bytes 5214592 | tf_op jit(solution)/shard_map/pallas_call | solution.py:1051
  169.7 1.9 convert_reduce_fusion.1
  171.7 1.4 multiply_reduce_fusion.1
  173.1 1.2 fusion.7.refs_0_
  174.3 22.0 %shard_map.287 = (bf16[3,2,128,1152]{3,2,1,0:T(8,128)(2,1)}, bf16[4,384,288]{2,1,0:T(8,128)(2,1)}, bf16[4,144,1536]{2,1,0:T(8,128)(2,1)}) custom-call(bf16[2,128,1152]{2,1,0:T(8,128)(2,1)} %bitcast.132, bf16[4,384,288]{2,1,0:T(8,128)(2,1)} %get-tuple-element.84.refs_1_.refs_7_, bf16[4,144,1536]{2,1,0:T(8,128)(2,1)} %get-tuple-element.85.refs_2_.refs_5_), custom_call_target="tpu_custom_call" | custom-call | tf_op jit(solution)/shard_map/pallas_call | solution.py:588
  196.4 0.7 broadcast_in_dim.97.refs_4_
  197.1 0.6 constant_dynamic-slice_fusion
  197.7 41.4 %shard_map.288 = (bf16[256,1152]{1,0:T(8,128)(2,1)}, f32[1,1536]{1,0:T(1,128)}, bf16[4,256,1152]{2,1,0:T(8,128)(2,1)}, bf16[1152,1536]{1,0:T(8,128)(2,1)}, bf16[...) custom-call(bf16[256,1152]{1,0:T(8,128)(2,1)} %fusion.7.refs_0_, bf16[3,256,1152]{2,1,0:T(8,128)(2,1)} %bitcast.170, ...), custom_call_target="tpu_custom_call" | custom-call | flops 16307453952 | bytes 10106880 | tf_op jit(solution)/shard_map/pallas_call | solution.py:1051
  239.1 1.9 convert_reduce_fusion
  241.5 0.7 copy-done.5
  242.1 1.8 convert_reduce_fusion.6
  243.9 22.2 %shard_map.289 = (bf16[3,2,128,1152]{3,2,1,0:T(8,128)(2,1)}, bf16[4,384,288]{2,1,0:T(8,128)(2,1)}, bf16[4,144,1536]{2,1,0:T(8,128)(2,1)}) custom-call(bf16[2,128,1152]{2,1,0:T(8,128)(2,1)} %bitcast.131, bf16[4,2,384,288]{3,2,1,0:T(8,128)(2,1)} %get-tuple-element.92.refs_1_, bf16[4,2,144,1536]{3,2,1,0:T(8,128)(2,1)} %bitcast.126), custom_call_target="tpu_custom_call" | custom-call | tf_op jit(solution)/shard_map/pallas_call | solution.py:588
  266.1 3.8 fusion.refs_13_
  269.9 1.3 fusion.1.refs_14_
  271.3 52.8 %shard_map.290 = (bf16[4,256,1152]{2,1,0:T(8,128)(2,1)}, f32[1,864]{1,0:T(1,128)}, f32[2,128]{1,0:T(2,128)}, bf16[4,2,144,864]{3,2,1,0:T(8,128)(2,1)}, bf16[4,2,...) custom-call(bf16[256,1152]{1,0:T(8,128)(2,1)} %get-tuple-element.173, ...), custom_call_target="tpu_custom_call" | custom-call | flops 6115295232 | bytes 11551744 | tf_op jit(solution)/shard_map/pallas_call | solution.py:1051
  324.1 2.8 shard_map.291.refs_3_.refs_4_
  326.9 28.2 %shard_map.292 = (bf16[3,256,1152]{2,1,0:T(8,128)(2,1)}, bf16[4,144,864]{2,1,0:T(8,128)(2,1)}, bf16[4,144,288]{2,1,0:T(8,128)(2,1)}, bf16[3,96,1536]{2,1,0:T(8,128)(2,1)}) custom-call(bf16[4,256,1152]{2,1,0:T(8,128)(2,1)} %get-tuple-element.102.refs_0_.refs_7_, bf16[4,2,144,864]{3,2,1,0:T(8,128)(2,1)} %get-tuple-element.103.refs_1_, ...), custom_call_target="tpu_custom_call" | custom-call | tf_op jit(solution)/shard_map/pallas_call | solution.py:588
  355.2 0.7 broadcast_select_fusion.5.refs_10_
  355.9 0.7 broadcast_in_dim_reshape.12.refs_11_
  356.6 6.6 %shard_map.293 = (bf16[256,1152]{1,0:T(8,128)(2,1)}, bf16[256,1152]{1,0:T(8,128)(2,1)}, f32[4,6,1152]{2,1,0:T(8,128)}) custom-call(bf16[256,1152]{1,0:T(8,128)(2,1)} %refs_0_.3, bf16[256,1152]{1,0:T(8,128)(2,1)} %refs_1_.5, f32[256,1152]{1,0:T(8,128)} %copy-done.1, f32[256,1152]{1,0:T(8,128)} %get-tuple-element.179.refs_3_, ...), custom_call_target="tpu_custom_call" | custom-call | tf_op jit(solution)/shard_map/pallas_call | solution.py:987
  363.2 2.5 fusion.2.refs_0_
  366.0 0.6 copy.111
  367.5 0.8 concatenate.18.refs_2_
  368.2 0.9 fusion.8.refs_3_
  369.1 26.5 %shard_map.294 = (bf16[4,144,864]{2,1,0:T(8,128)(2,1)}, bf16[8,4,4,1728]{3,2,1,0:T(4,128)(2,1)}, f32[4,1,3012]{2,1,0:T(1,128)}, bf16[3,144,288]{2,1,0:T(8,128)(2,1)}, bf16[3,48,1536]{2,1,0:T(8,128)(2,1)}) custom-call(bf16[4,144,864]{2,1,0:T(8,128)(2,1)} %fusion.2.refs_0_, bf16[4,4,1728]{2,1,0:T(4,128)(2,1)} %bitcast.145, f32[4,1,3012]{2,1,0:T(1,128)} %concatenate.18.refs_2_, ...), custom_call_target="tpu_custom_call" | custom-call | tf_op jit(solution)/shard_map/pallas_call | solution.py:588
  395.6 2.5 shard_map.295.refs_0_
  398.1 1.1 fusion.9.refs_1_
  399.2 0.6 reduce_sum.168
  399.9 33.2 %shard_map.296 = (bf16[3,144,864]{2,1,0:T(8,128)(2,1)}, f32[8,4,4,144]{3,2,1,0:T(4,128)}, f32[8,1,3012]{2,1,0:T(1,128)}) custom-call(bf16[4,144,864]{2,1,0:T(8,128)(2,1)} %shard_map.295.refs_0_, f32[8,4,4,144]{3,2,1,0:T(4,128)} %fusion.9.refs_1_, f32[1,3012]{1,0:T(1,128)} %bitcast.160), custom_call_target="tpu_custom_call" | custom-call | tf_op jit(solution)/shard_map/pallas_call | solution.py:588
  433.1 0.9 reduce_sum.170
  434.1 0.6 fusion.25
  435.0 1.4 fusion.14
  436.4 0.8 convert_reduce_fusion.7
  437.3 1.9 convert_add_fusion.8
  439.2 0.6 slice_reduce_fusion.1
  440.5 1.7 convert_add_fusion.10
  442.2 0.7 slice_reduce_fusion.2
  443.0 1.0 convert_add_fusion.9
  444.1 1.0 convert_add_fusion.7
  445.1 1.0 pad_maximum_fusion
  446.1 0.6 slice_reduce_fusion
  446.8 1.0 convert_add_fusion.6
  447.9 1.0 copy.91
  (139 shorter events, 5.9 us)
Async XLA Ops:
  0.6 44.0 %copy-start = (bf16[144,1728]{1,0:T(8,128)(2,1)S(1)}, bf16[144,1728]{1,0:T(8,128)(2,1)}, u32[]{:S(2)}) copy-start(bf16[144,1728]{1,0:T(8,128)(2,1)} %param.22) | copy-start | bytes 1492996
  42.1 2.5 copy-start.19
  70.9 1.3 copy-start.27
  105.2 1.7 copy-start.29
  105.2 3.0 copy-start.22
  106.4 2.2 copy-start.25
  114.2 2.8 copy-start.20
  169.7 2.0 copy-start.4
  169.7 2.0 copy-start.13
  173.1 68.4 %copy-start.1 = (f32[256,1152]{1,0:T(8,128)}, f32[256,1152]{1,0:T(8,128)S(1)}, u32[]{:S(2)}) copy-start(f32[256,1152]{1,0:T(8,128)S(1)} %get-tuple-element.178.refs_2_) | copy-start | bytes 3538948
  239.1 1.9 copy-start.14
  241.1 1.1 copy-start.5
  241.5 2.5 copy-start.2
  266.1 3.8 copy-start.3
  266.1 3.8 copy-start.9
  356.6 6.6 %copy-start.6 = (bf16[4,2,144,864]{3,2,1,0:T(8,128)(2,1)S(1)}, bf16[4,2,144,864]{3,2,1,0:T(8,128)(2,1)}, u32[]{:S(2)}) copy-start(bf16[4,2,144,864]{3,2,1,0:T(8,128)(2,1)} %get-tuple-element.103.refs_1_) | copy-start | bytes 5971972
  363.2 2.5 copy-start.15
  363.2 3.5 copy-start.28
  363.2 3.8 copy-start.26
  363.2 4.0 copy-start.30
  363.2 5.0 %copy-start.16 = (bf16[4,144,288]{2,1,0:T(8,128)(2,1)S(1)}, bf16[4,144,288]{2,1,0:T(8,128)(2,1)}, u32[]{:S(2)}) copy-start(bf16[4,144,288]{2,1,0:T(8,128)(2,1)} %get-tuple-element.115) | copy-start | bytes 995332
  365.7 2.5 copy-start.7
  395.6 2.5 copy-start.8
  398.1 1.1 copy-start.23
  398.1 36.0 %copy-start.24 = (bf16[4,1152]{1,0:T(4,128)(2,1)S(1)}, bf16[4,1152]{1,0:T(4,128)(2,1)}, u32[]{:S(2)}) copy-start(bf16[4,1152]{1,0:T(4,128)(2,1)} %param.19) | copy-start | bytes 27652
  435.0 2.2 copy-start.12
  437.2 2.0 copy-start.21
  437.2 3.3 copy-start.18
  437.3 5.6 %copy-start.17 = (bf16[3,48,1536]{2,1,0:T(8,128)(2,1)S(1)}, bf16[3,48,1536]{2,1,0:T(8,128)(2,1)}, u32[]{:S(2)}) copy-start(bf16[3,48,1536]{2,1,0:T(8,128)(2,1)} %get-tuple-element.124) | copy-start | bytes 1327108
  440.5 3.4 copy-start.11
  445.1 1.6 copy-start.10

commit v7 on v6

--- a/solution.py
+++ b/solution.py
@@ -1154,7 +1154,8 @@
 
         silu_all = silu_all.reshape(-1, width)
         silu_cols = lax.dynamic_slice_in_dim(silu_all, dp_index * mod_rows, mod_rows, axis=1)
-        mod_part = dot(silu_cols, mod_weight).reshape(2 * PLANE, z_size * slots, mod_cols)
+        mod_part = dot(silu_cols, mod_weight).astype(low)
+        mod_part = mod_part.reshape(2 * PLANE, z_size * slots, mod_cols)
         qkv_pieces = whole_call(functools.partial(split_kernel, 3), qkv_z)
         plan = [
             (hop, 0, to_chip, 0, by_dp, None) for hop in PLANE_HOPS
@@ -1175,14 +1176,14 @@
             [qkv_pieces, mod_part, proj_z, up_weight],
             [
                 ((2 * PLANE, shard, 3 * part_cols), low),
-                (mod_part.shape, full),
+                (mod_part.shape, low),
                 (proj_z.shape, low),
                 ((z_size, up_cut, up_cols), low),
             ],
             plan,
         )
         qkv_slice = qkv_slice.reshape(-1, 3 * part_cols)
-        mod_sum = (jnp.sum(mod_parts, axis=0) + mod_bias.astype(full)).reshape(
+        mod_sum = (jnp.sum(mod_parts.astype(full), axis=0) + mod_bias.astype(full)).reshape(
             z_size, slots, mod_cols
         )
         plan = [

time: 450 us -> 450 us (level)
  no operation moved by 1% of the time
where the time goes in v7:
time: 450 us; the launch traced here: 449 us
  Pallas kernels  387 us (86%)
  other arithmetic  36.9 us (8%)
  local copies, waits for them, and re-layouts  19.8 us (4%)
    pallas_call x8, Pallas kernels, exchange(): pl.pallas_call(kernel, out_shape=[jax.ShapeDtypeStruct(shape, dtype) for...  224 us
    pallas_call x3, Pallas kernels, block_call(): pl.pallas_call(body, grid=(steps,), out_shape=[jax.ShapeDtypeStruct(*o) f...  146 us
    pallas_call x4, Pallas kernels, whole_call(): pl.pallas_call(kernel, out_shape=jax.ShapeDtypeStruct((count, rows, cols)...  10.6 us

profile of v7, /device:TPU:0, one launch (start us, length us, event | category | flops | bytes accessed | tf_op | source)
XLA Modules:
  0.0 449.0 jit_solution(16496894307637434241)
XLA Ops:
  0.7 1.4 fusion.20.refs_0_
  2.0 0.7 slice_bitcast_fusion
  2.8 2.8 concatenate.15
  5.6 0.6 broadcast_in_dim.50.refs_4_
  6.2 1.3 pad_add_fusion.1.refs_5_
  7.5 34.5 %shard_map.281 = (bf16[8,4,4,1152]{3,2,1,0:T(4,128)(2,1)}, bf16[4,144,864]{2,1,0:T(8,128)(2,1)}, bf16[3,2,128,1152]{3,2,1,0:T(8,128)(2,1)}, bf16[4,144,288]{2,1,...) custom-call(bf16[4,1152]{1,0:T(4,128)(2,1)} %fusion.20.refs_0_, bf16[144,864]{1,0:T(8,128)(2,1)} %refs_1_.3, ...), custom_call_target="tpu_custom_call" | custom-call | tf_op jit(solution)/shard_map/pallas_call | solution.py:588
  42.1 2.5 shard_map.282.refs_0_
  45.2 1.0 copy.72
  46.2 24.9 %shard_map.283 = (bf16[8,144,864]{2,1,0:T(8,128)(2,1)}, bf16[8,16,1728]{2,1,0:T(8,128)(2,1)}, bf16[4,144,288]{2,1,0:T(8,128)(2,1)}, bf16[4,96,1536]{2,1,0:T(8,128)(2,1)}) custom-call(bf16[4,144,864]{2,1,0:T(8,128)(2,1)} %shard_map.282.refs_0_, bf16[8,16,1728]{2,1,0:T(8,128)(2,1)} %bitcast.132, bf16[4,144,288]{2,1,0:T(8,128)(2,1)} %get-tuple-element.72.refs_2_.refs_11_, ...), custom_call_target="tpu_custom_call" | custom-call | tf_op jit(solution)/shard_map/pallas_call | solution.py:588
  71.1 1.1 convert_reduce_fusion.8
  72.3 0.7 broadcast_add_fusion.refs_0_
  73.0 32.4 %shard_map.284 = (f32[4,4,4,1728]{3,2,1,0:T(4,128)}, bf16[4,48,1536]{2,1,0:T(8,128)(2,1)}, bf16[3,2,128,1152]{3,2,1,0:T(8,128)(2,1)}) custom-call(f32[4,4,1728]{2,1,0:T(4,128)} %broadcast_add_fusion.refs_0_, bf16[144,1536]{1,0:T(8,128)(2,1)} %refs_1_.4, bf16[2,128,1152]{2,1,0:T(8,128)(2,1)} %bitcast.129), custom_call_target="tpu_custom_call" | custom-call | tf_op jit(solution)/shard_map/pallas_call | solution.py:588
  105.4 1.2 copy.73
  107.1 0.6 slice.153
  109.5 0.7 pad_maximum_fusion.1.refs_2_
  110.3 0.7 pad_maximum_fusion.2.refs_3_
  111.1 0.7 broadcast_in_dim_reshape.10.refs_5_
  112.7 1.0 copy.79.refs_9_.refs_7_
  113.7 0.6 slice.215.refs_10_.refs_8_
  114.3 2.8 shard_map.285.refs_13_
  117.1 0.9 copy.80.refs_14_
  118.0 51.8 %shard_map.286 = (bf16[4,256,1152]{2,1,0:T(8,128)(2,1)}, f32[4,256,864]{2,1,0:T(8,128)}, bf16[4,256,288]{2,1,0:T(8,128)(2,1)}, bf16[256,1152]{1,0:T(8,128)(2,1)}...) custom-call(bf16[256,1152]{1,0:T(8,128)(2,1)} %refs_0_.3, ...), custom_call_target="tpu_custom_call" | custom-call | flops 2717908992 | bytes 5214592 | tf_op jit(solution)/shard_map/pallas_call | solution.py:1051
  169.9 1.9 convert_reduce_fusion.1
  171.8 1.4 multiply_reduce_fusion.1
  173.2 1.2 fusion.7.refs_0_
  174.4 22.0 %shard_map.287 = (bf16[3,2,128,1152]{3,2,1,0:T(8,128)(2,1)}, bf16[4,384,288]{2,1,0:T(8,128)(2,1)}, bf16[4,144,1536]{2,1,0:T(8,128)(2,1)}) custom-call(bf16[2,128,1152]{2,1,0:T(8,128)(2,1)} %bitcast.131, bf16[4,384,288]{2,1,0:T(8,128)(2,1)} %get-tuple-element.84.refs_1_.refs_7_, bf16[4,144,1536]{2,1,0:T(8,128)(2,1)} %get-tuple-element.85.refs_2_.refs_5_), custom_call_target="tpu_custom_call" | custom-call | tf_op jit(solution)/shard_map/pallas_call | solution.py:588
  196.5 0.7 broadcast_in_dim.97.refs_4_
  197.2 0.6 constant_dynamic-slice_fusion
  197.8 41.4 %shard_map.288 = (bf16[256,1152]{1,0:T(8,128)(2,1)}, f32[1,1536]{1,0:T(1,128)}, bf16[4,256,1152]{2,1,0:T(8,128)(2,1)}, bf16[1152,1536]{1,0:T(8,128)(2,1)}, bf16[...) custom-call(bf16[256,1152]{1,0:T(8,128)(2,1)} %fusion.7.refs_0_, bf16[3,256,1152]{2,1,0:T(8,128)(2,1)} %bitcast.170, ...), custom_call_target="tpu_custom_call" | custom-call | flops 16307453952 | bytes 10106880 | tf_op jit(solution)/shard_map/pallas_call | solution.py:1051
  239.2 1.9 convert_reduce_fusion
  241.6 0.7 copy-done.5
  242.3 1.8 convert_reduce_fusion.6
  244.0 22.2 %shard_map.289 = (bf16[3,2,128,1152]{3,2,1,0:T(8,128)(2,1)}, bf16[4,384,288]{2,1,0:T(8,128)(2,1)}, bf16[4,144,1536]{2,1,0:T(8,128)(2,1)}) custom-call(bf16[2,128,1152]{2,1,0:T(8,128)(2,1)} %bitcast.130, bf16[4,2,384,288]{3,2,1,0:T(8,128)(2,1)} %get-tuple-element.92.refs_1_, bf16[4,2,144,1536]{3,2,1,0:T(8,128)(2,1)} %bitcast.126), custom_call_target="tpu_custom_call" | custom-call | tf_op jit(solution)/shard_map/pallas_call | solution.py:588
  266.2 3.8 fusion.refs_13_
  270.1 1.3 fusion.1.refs_14_
  271.4 52.8 %shard_map.290 = (bf16[4,256,1152]{2,1,0:T(8,128)(2,1)}, f32[1,864]{1,0:T(1,128)}, f32[2,128]{1,0:T(2,128)}, bf16[4,2,144,864]{3,2,1,0:T(8,128)(2,1)}, bf16[4,2,...) custom-call(bf16[256,1152]{1,0:T(8,128)(2,1)} %get-tuple-element.173, ...), custom_call_target="tpu_custom_call" | custom-call | flops 6115295232 | bytes 11551744 | tf_op jit(solution)/shard_map/pallas_call | solution.py:1051
  324.2 2.8 shard_map.291.refs_3_.refs_4_
  327.1 28.2 %shard_map.292 = (bf16[3,256,1152]{2,1,0:T(8,128)(2,1)}, bf16[4,144,864]{2,1,0:T(8,128)(2,1)}, bf16[4,144,288]{2,1,0:T(8,128)(2,1)}, bf16[3,96,1536]{2,1,0:T(8,128)(2,1)}) custom-call(bf16[4,256,1152]{2,1,0:T(8,128)(2,1)} %get-tuple-element.102.refs_0_.refs_7_, bf16[4,2,144,864]{3,2,1,0:T(8,128)(2,1)} %get-tuple-element.103.refs_1_, ...), custom_call_target="tpu_custom_call" | custom-call | tf_op jit(solution)/shard_map/pallas_call | solution.py:588
  355.4 0.7 broadcast_select_fusion.5.refs_10_
  356.0 0.7 broadcast_in_dim_reshape.12.refs_11_
  356.7 6.6 %shard_map.293 = (bf16[256,1152]{1,0:T(8,128)(2,1)}, bf16[256,1152]{1,0:T(8,128)(2,1)}, f32[4,6,1152]{2,1,0:T(8,128)}) custom-call(bf16[256,1152]{1,0:T(8,128)(2,1)} %refs_0_.3, bf16[256,1152]{1,0:T(8,128)(2,1)} %refs_1_.5, f32[256,1152]{1,0:T(8,128)} %copy-done.1, f32[256,1152]{1,0:T(8,128)} %get-tuple-element.179.refs_3_, ...), custom_call_target="tpu_custom_call" | custom-call | tf_op jit(solution)/shard_map/pallas_call | solution.py:987
  363.4 2.5 fusion.2.refs_0_
  366.1 0.6 copy.110
  367.6 0.8 concatenate.18.refs_2_
  368.3 0.9 fusion.8.refs_3_
  369.2 26.5 %shard_map.294 = (bf16[4,144,864]{2,1,0:T(8,128)(2,1)}, bf16[8,4,4,1728]{3,2,1,0:T(4,128)(2,1)}, f32[4,1,3012]{2,1,0:T(1,128)}, bf16[3,144,288]{2,1,0:T(8,128)(2,1)}, bf16[3,48,1536]{2,1,0:T(8,128)(2,1)}) custom-call(bf16[4,144,864]{2,1,0:T(8,128)(2,1)} %fusion.2.refs_0_, bf16[4,4,1728]{2,1,0:T(4,128)(2,1)} %bitcast.145, f32[4,1,3012]{2,1,0:T(1,128)} %concatenate.18.refs_2_, ...), custom_call_target="tpu_custom_call" | custom-call | tf_op jit(solution)/shard_map/pallas_call | solution.py:588
  395.7 2.5 shard_map.295.refs_0_
  398.2 1.1 fusion.9.refs_1_
  399.3 0.6 reduce_sum.168
  400.0 33.2 %shard_map.296 = (bf16[3,144,864]{2,1,0:T(8,128)(2,1)}, f32[8,4,4,144]{3,2,1,0:T(4,128)}, f32[8,1,3012]{2,1,0:T(1,128)}) custom-call(bf16[4,144,864]{2,1,0:T(8,128)(2,1)} %shard_map.295.refs_0_, f32[8,4,4,144]{3,2,1,0:T(4,128)} %fusion.9.refs_1_, f32[1,3012]{1,0:T(1,128)} %bitcast.160), custom_call_target="tpu_custom_call" | custom-call | tf_op jit(solution)/shard_map/pallas_call | solution.py:588
  433.2 0.9 reduce_sum.170
  434.2 0.6 fusion.24
  435.1 1.4 fusion.14
  436.5 0.8 convert_reduce_fusion.7
  437.4 1.9 convert_add_fusion.8
  439.3 0.6 slice_reduce_fusion.1
  440.6 1.7 convert_add_fusion.10
  442.3 0.7 slice_reduce_fusion.2
  443.1 1.0 convert_add_fusion.9
  444.2 1.0 convert_add_fusion.7
  445.2 1.0 pad_maximum_fusion
  446.2 0.6 slice_reduce_fusion
  446.9 1.0 convert_add_fusion.6
  448.0 1.0 copy.91
  (140 shorter events, 6.5 us)
Async XLA Ops:
  0.6 44.0 %copy-start = (bf16[144,1728]{1,0:T(8,128)(2,1)S(1)}, bf16[144,1728]{1,0:T(8,128)(2,1)}, u32[]{:S(2)}) copy-start(bf16[144,1728]{1,0:T(8,128)(2,1)} %param.22) | copy-start | bytes 1492996
  42.1 2.5 copy-start.19
  46.2 26.1 %copy-start.27 = (bf16[1728]{0:T(1024)(128)(2,1)S(1)}, bf16[1728]{0:T(1024)(128)(2,1)}, u32[]{:S(2)}) copy-start(bf16[1728]{0:T(1024)(128)(2,1)} %param.23) | copy-start | bytes 10372
  105.3 1.7 copy-start.29
  105.4 3.0 copy-start.22
  106.5 2.2 copy-start.25
  114.3 2.8 copy-start.20
  169.8 2.0 copy-start.4
  169.8 2.0 copy-start.13
  173.2 68.4 %copy-start.1 = (f32[256,1152]{1,0:T(8,128)}, f32[256,1152]{1,0:T(8,128)S(1)}, u32[]{:S(2)}) copy-start(f32[256,1152]{1,0:T(8,128)S(1)} %get-tuple-element.178.refs_2_) | copy-start | bytes 3538948
  239.2 1.9 copy-start.14
  241.2 1.1 copy-start.5
  241.6 2.5 copy-start.2
  266.2 3.8 copy-start.3
  266.2 3.8 copy-start.9
  356.7 6.6 %copy-start.6 = (bf16[4,2,144,864]{3,2,1,0:T(8,128)(2,1)S(1)}, bf16[4,2,144,864]{3,2,1,0:T(8,128)(2,1)}, u32[]{:S(2)}) copy-start(bf16[4,2,144,864]{3,2,1,0:T(8,128)(2,1)} %get-tuple-element.103.refs_1_) | copy-start | bytes 5971972
  363.3 2.5 copy-start.15
  363.3 3.5 copy-start.28
  363.3 3.8 copy-start.26
  363.3 4.0 copy-start.30
  363.3 5.0 %copy-start.16 = (bf16[4,144,288]{2,1,0:T(8,128)(2,1)S(1)}, bf16[4,144,288]{2,1,0:T(8,128)(2,1)}, u32[]{:S(2)}) copy-start(bf16[4,144,288]{2,1,0:T(8,128)(2,1)} %get-tuple-element.115) | copy-start | bytes 995332
  365.8 2.5 copy-start.7
  395.7 2.5 copy-start.8
  398.2 1.1 copy-start.23
  398.2 36.0 %copy-start.24 = (bf16[4,1152]{1,0:T(4,128)(2,1)S(1)}, bf16[4,1152]{1,0:T(4,128)(2,1)}, u32[]{:S(2)}) copy-start(bf16[4,1152]{1,0:T(4,128)(2,1)} %param.19) | copy-start | bytes 27652
  435.1 2.2 copy-start.12
  437.3 2.0 copy-start.21
  437.3 3.3 copy-start.18
  437.4 5.6 %copy-start.17 = (bf16[3,48,1536]{2,1,0:T(8,128)(2,1)S(1)}, bf16[3,48,1536]{2,1,0:T(8,128)(2,1)}, u32[]{:S(2)}) copy-start(bf16[3,48,1536]{2,1,0:T(8,128)(2,1)} %get-tuple-element.124) | copy-start | bytes 1327108
  440.6 3.4 copy-start.11
  445.2 1.6 copy-start.10
